TPU v7x, 32 devices: a whole 2x2x4 slice. The times are simulated.
32 devices in a mesh: tile: 8 (over z, x), chan: 4 (over y, core).
Axes of the slice: x: 2, y: 2, z: 4, core: 2. Of those that a mesh axis runs over, the one named last changes fastest.
Arguments:
- features: bfloat16 [192, 16384], P('chan', 'tile'), may hold values from -6 to 6
- pre_act: bfloat16 [192, 16384], P('chan', 'tile'), may hold values from -6 to 6
- cotangent: bfloat16 [192, 16384], P('chan', 'tile'), may hold values from -6 to 6
- weight_one: bfloat16 [27, 192, 192], P(None, 'chan'), may hold values from -0.109375 to 0.109375
- weight_two: bfloat16 [27, 192, 192], P(None, 'chan'), may hold values from -0.109375 to 0.109375
- send_list: int32 [8, 8, 4], P('tile'), may hold values from 0 to 16, as said below
- pair_in: int32 [8, 27, 16], P('tile'), may hold values from 0 to 48, as said below
- pair_out: int32 [8, 27, 16], P('tile'), may hold values from 0 to 16, as said below
Outputs:
- grad_features: bfloat16 [192, 16384], P('chan', 'tile')
- grad_weight_one: float32 [27, 192, 192], P(None, 'chan')
- grad_weight_two: float32 [27, 192, 192], P(None, 'chan')
Inputs may be any that keep to these rules, and one draw needn't show every extreme that they name: send_list[t, n, :] names distinct blocks of tile t, live entries first and then 16; a direction that leaves the tile grid has only 16; the list of tile 0 for direction 6 is full. pair_out[t, k, p] is p for a live pair and 16 for an empty one; at offset 27 // 2 every pair is live. pair_in[t, k, p] is 48 exactly for empty pairs; for live pairs it is a block of tile t or an entry 16 + n * 4 + s whose list entry send_list[u, 7 - n, s] of the neighbour u in direction n is live; at offset 27 // 2 it is p.
All inputs are finite; a program needn't handle non-finite values.
Results may differ from a plain program's by a relative error of at most 0.0037.
Values may be sent and summed in bfloat16 or wider, within the bound.
No kernel may reach another device: no remote copies, remote signals or barrier semaphores. Data moves between devices by JAX's collectives and lax.ppermute only.
A program may use at most 64 MiB of HBM per device.

v0:
```python
import math

import jax
import jax.numpy as jnp
from jax import lax
from jax.sharding import PartitionSpec as P

TILE_Y = 4


STEP_ROW = (-1, -1, -1, 0, 0, 1, 1, 1)
STEP_COL = (-1, 0, 1, -1, 1, -1, 0, 1)
group_size = 3


def shifted(value, axis, by):
    devices = lax.axis_size(axis)
    pairs = [(i, i + by) for i in range(devices) if 0 <= i + by < devices]
    return lax.ppermute(value, axis, pairs)


def blocked(values, block_count):
    part_width, voxel_count = values.shape
    return values.reshape(part_width, block_count, voxel_count // block_count)


def pack_sends(own_blocks, send_flat, slot_count):
    part_width, block_count, block_rows = own_blocks.shape
    padded = jnp.concatenate(
        [own_blocks, jnp.zeros((part_width, 1, block_rows), own_blocks.dtype)], axis=1
    )
    return jnp.take(padded, send_flat, axis=1).reshape(part_width, 8, slot_count, block_rows)


def trade_blocks(stacked):
    arrived = []
    for direction in range(8):
        reach_step = STEP_ROW[direction] * TILE_Y + STEP_COL[direction]
        arrived.append(shifted(stacked[:, :, 7 - direction], "tile", -reach_step))
    return jnp.stack(arrived, axis=2)


def offset_sweep(own_blocks, ghost_blocks, full_grad, weight, in_table, out_table):
    part_width, block_count, block_rows = own_blocks.shape
    full_width = full_grad.shape[0]
    offset_count = weight.shape[0]
    turns = offset_count // group_size
    extended = jnp.concatenate(
        [
            own_blocks,
            ghost_blocks.reshape(part_width, -1, block_rows),
            jnp.zeros((part_width, 1, block_rows), own_blocks.dtype),
        ],
        axis=1,
    )
    extent = extended.shape[1]
    grad_blocks = jnp.concatenate(
        [
            full_grad.reshape(full_width, block_count, block_rows),
            jnp.zeros((full_width, 1, block_rows), full_grad.dtype),
        ],
        axis=1,
    )
    grouped_weight = weight.reshape(turns, group_size, part_width, full_width)
    grouped_in = in_table.reshape(turns, group_size * block_count)
    grouped_out = out_table.reshape(turns, group_size * block_count)
    entry_ids = jnp.arange(extent, dtype=jnp.int32)

    def offset_step(running, inputs):
        kernels, sources, targets = inputs
        in_blocks = jnp.take(extended, sources, axis=1).reshape(
            part_width, group_size, block_count, block_rows
        )
        out_blocks = jnp.take(grad_blocks, targets, axis=1).reshape(
            full_width, group_size, block_count, block_rows
        )
        weight_grad = jnp.einsum(
            "ckpr,dkpr->kcd", in_blocks, out_blocks, preferred_element_type=jnp.float32
        )
        partial_term = jnp.einsum(
            "kcd,dkpr->ckpr", kernels, out_blocks, preferred_element_type=jnp.float32
        )
        partial_term = partial_term.reshape(part_width, group_size * block_count, block_rows)
        selector = (entry_ids[:, None] == sources[None, :]).astype(jnp.float32)
        landed = jnp.einsum(
            "ep,cpr->cer",
            selector,
            partial_term,
            precision=lax.Precision.HIGHEST,
            preferred_element_type=jnp.float32,
        )
        return (running + landed, weight_grad)

    initial = jnp.zeros((part_width, extent, block_rows), jnp.float32)
    running, weight_grads = lax.scan(
        offset_step, initial, (grouped_weight, grouped_in, grouped_out)
    )
    weight_grads = weight_grads.reshape(offset_count, part_width, full_width)
    local_part = running[:, :block_count]
    ghost_part = (
        running[:, block_count:-1].astype(jnp.bfloat16).reshape(part_width, 8, -1, block_rows)
    )
    return (local_part, ghost_part, weight_grads)


def settle(local_part, returned, send_flat):
    part_width, block_count, block_rows = local_part.shape
    flat_back = returned.reshape(part_width, -1, block_rows).astype(jnp.float32)
    return local_part.at[:, send_flat].add(flat_back, mode="drop")


def shards(features, pre_act, cotangent, weight_one, weight_two, send_list, pair_in, pair_out):
    part_width = features.shape[0]
    block_count = pair_out.shape[2]
    block_rows = features.shape[1] // block_count
    slot_count = send_list.shape[2]
    send_flat = send_list[0].reshape(-1)
    in_table = pair_in[0]
    out_table = pair_out[0]
    hidden = jnp.maximum(pre_act, 0)
    hidden_blocks = blocked(hidden, block_count)
    input_blocks = blocked(features, block_count)
    hidden_sends = pack_sends(hidden_blocks, send_flat, slot_count)
    input_sends = pack_sends(input_blocks, send_flat, slot_count)
    arrived = trade_blocks(jnp.stack((hidden_sends, input_sends)))
    hidden_ghost = arrived[0]
    input_ghost = arrived[1]
    full_cotangent = lax.all_gather(cotangent, "chan", axis=0, tiled=True)
    local_two, ghost_two, weight_sum_two = offset_sweep(
        hidden_blocks, hidden_ghost, full_cotangent, weight_two, in_table, out_table
    )
    back_two = trade_blocks(ghost_two[None])[0]
    grad_hidden = settle(local_two, back_two, send_flat).reshape(part_width, -1)
    grad_pre = jnp.where(pre_act > 0, grad_hidden, 0.0).astype(jnp.bfloat16)
    full_pre = lax.all_gather(grad_pre, "chan", axis=0, tiled=True)
    local_one, ghost_one, weight_sum_one = offset_sweep(
        input_blocks, input_ghost, full_pre, weight_one, in_table, out_table
    )
    back_one = trade_blocks(ghost_one[None])[0]
    grad_inner = settle(local_one, back_one, send_flat).reshape(part_width, -1)
    grad_features = (cotangent.astype(jnp.float32) + grad_inner).astype(jnp.bfloat16)
    summed_one, summed_two = lax.psum((weight_sum_one, weight_sum_two), "tile")
    factor = 1.0 / math.sqrt(lax.axis_size("tile") * block_count * block_rows)
    return (grad_features, summed_one * factor, summed_two * factor)


def solution(mesh):
    return jax.shard_map(
        shards,
        mesh=mesh,
        in_specs=(
            P("chan", "tile"),
            P("chan", "tile"),
            P("chan", "tile"),
            P(None, "chan", None),
            P(None, "chan", None),
            P("tile", None, None),
            P("tile", None, None),
            P("tile", None, None),
        ),
        out_specs=(P("chan", "tile"), P(None, "chan", None), P(None, "chan", None)),
        check_vma=False,
    )
```

profile of v0, /device:TPU:2, one launch (start us, length us, event | category | flops | bytes accessed | tf_op | source)
XLA Modules:
  0.0 509.8 jit_solution(1256147624878276680)
XLA Ops:
  10.7 5.5 %collective-permute-start = (bf16[2,48,4,128]{3,1,2,0:T(8,128)(2,1)S(1)}, bf16[2,48,4,128]{3,1,2,0:T(8,128)(2,1)S(1)}, u32[]{:S(2)}, u32[]{:S(2)}) collective-permute-start(bf16[2,48,4,128]{3,1,2,0:T(8,128)(2,1)S(1)} %get-tuple-element.245), channel_id=1, source_target_pairs={{0,20},{4,24},{8,28},{1,21},{5,25},{9,29},{2,22},{6,26},{10,30},{3... | collective-permute-start | bytes 294920 | tf_op jit(solution)/shard_map/ppermute | solution.py:19
  24.7 8.6 %all_gather.6 = bf16[192,2048]{1,0:T(8,128)(2,1)S(1)} all-gather(bf16[48,2048]{1,0:T(8,128)(2,1)S(1)} %copy-done.6), channel_id=1, replica_groups=mesh['tile'=8,'chan'=4] {'chan'}, dimensions={0}, use_global_device_ids=true | all-gather | bytes 983040 | tf_op jit(solution)/shard_map/all_gather | solution.py:128
  38.1 11.6 %collective-permute-done.5 = bf16[2,48,4,128]{3,1,2,0:T(8,128)(2,1)S(1)} collective-permute-done((bf16[2,48,4,128]{3,1,2,0:T(8,128)(2,1)S(1)}, bf16[2,48,4,128]{3,1,2,0:T(8,128)(2,1)S(1)}, u32[]{:S(2)}, u32[]{:S(2)}) %collective-permute-start.5) | collective-permute-done | bytes 98336 | tf_op jit(solution)/shard_map/ppermute | solution.py:19
  52.2 144.2 %while.26 = (s32[]{:T(128)}, f32[48,49,128]{2,1,0:T(8,128)}, f32[9,3,48,192]{3,2,1,0:T(8,128)}, s32[9,48]{1,0:T(8,128)S(1)}, bf16[192,17,128]{2,0,1:T(8,128)(2,1...) while((s32[]{:T(128)}, f32[48,49,128]{2,1,0:T(8,128)}, ...), condition=%wide.region_1.5_spmd.clone, body=%wide.region_0.4_spmd.clone.sunk | while | flops 401982464 | bytes 22105460 | solution.py:95
  74.7 4.0 fusion.85
  90.8 4.0 fusion.85
  106.8 4.0 fusion.85
  122.9 4.0 fusion.85
  139.0 4.0 fusion.85
  155.0 4.0 fusion.85
  171.1 4.0 fusion.85
  187.2 4.0 fusion.85
  224.8 7.6 %all_gather.7 = bf16[192,2048]{1,0:T(8,128)(2,1)S(1)} all-gather(bf16[48,2048]{1,0:T(8,128)(2,1)S(1)} %fusion.29), channel_id=1, replica_groups=mesh['tile'=8,'chan'=4] {'chan'}, dimensions={0}, use_global_device_ids=true | all-gather | bytes 983040 | tf_op jit(solution)/shard_map/all_gather | solution.py:135
  233.9 144.1 %while.27 = (s32[]{:T(128)}, f32[48,49,128]{2,1,0:T(8,128)}, f32[9,3,48,192]{3,2,1,0:T(8,128)}, s32[9,48]{1,0:T(8,128)S(1)}, bf16[192,17,128]{2,0,1:T(8,128)(2,1...) while((s32[]{:T(128)}, f32[48,49,128]{2,1,0:T(8,128)}, ...), condition=%wide.region_4.8_spmd.clone, body=%wide.region_3.7_spmd.clone.sunk | while | flops 401982464 | bytes 22105460 | solution.py:95
  256.4 4.0 fusion.94
  272.4 4.0 fusion.94
  288.5 4.0 fusion.94
  304.5 4.0 fusion.94
  320.6 4.0 fusion.94
  336.7 4.0 fusion.94
  352.7 4.0 fusion.94
  368.8 4.0 fusion.94
  396.8 9.2 %collective-permute-done.21 = bf16[1,48,4,128]{3,1,2,0:T(8,128)(2,1)S(1)} collective-permute-done((bf16[1,48,4,128]{3,1,2,0:T(8,128)(2,1)S(1)}, bf16[1,48,4,128]{3,1,2,0:T(8,128)(2,1)S(1)}, u32[]{:S(2)}, u32[]{:S(2)}) %collective-permute-start.21) | collective-permute-done | bytes 49184 | tf_op jit(solution)/shard_map/ppermute | solution.py:19
  411.6 87.6 %all-reduce.7.cloned.1.call-done = (f32[27,48,192]{2,1,0:T(8,128)}, f32[27,48,192]{2,1,0:T(8,128)}) async-done(((f32[27,48,192]{2,1,0:T(8,128)}, f32[27,48,192]{2,1,0:T(8,128)}), (f32[27,48,192]{2,1,0:T(8,128)}, f32[27,48,192]{2,1,0:T(8,128)})) %all-reduce.7.cloned.1.call-update) | async-done | bytes 1990672 | tf_op jit(solution)/shard_map/psum | solution.py:142
  (322 shorter events, 300.3 us)
Async XLA Ops:
  7.2 492.0 %all-reduce.7.cloned.1.call-start = ((), (), s32[]{:S(2)}) async-start(), calls=%async_computation | async-start | bytes 5308416 | tf_op jit(solution)/shard_map/psum | solution.py:142
  10.7 23.3 %collective-permute-start = (bf16[2,48,4,128]{3,1,2,0:T(8,128)(2,1)S(1)}, bf16[2,48,4,128]{3,1,2,0:T(8,128)(2,1)S(1)}, u32[]{:S(2)}, u32[]{:S(2)}) collective-permute-start(bf16[2,48,4,128]{3,1,2,0:T(8,128)(2,1)S(1)} %get-tuple-element.245), channel_id=1, source_target_pairs={{0,20},{4,24},{8,28},{1,21},{5,25},{9,29},{2,22},{6,26},{10,30},{3... | collective-permute-start | bytes 294920 | tf_op jit(solution)/shard_map/ppermute | solution.py:19
  16.2 19.1 %collective-permute-start.1 = (bf16[2,48,4,128]{3,1,2,0:T(8,128)(2,1)S(1)}, bf16[2,48,4,128]{3,1,2,0:T(8,128)(2,1)S(1)}, u32[]{:S(2)}, u32[]{:S(2)}) collective-permute-start(bf16[2,48,4,128]{3,1,2,0:T(8,128)(2,1)S(1)} %get-tuple-element.246), channel_id=1, source_target_pairs={{0,16},{4,20},{8,24},{12,28},{1,17},{5,21},{9,25},{13,29},{2,18},{... | collective-permute-start | bytes 294920 | tf_op jit(solution)/shard_map/ppermute | solution.py:19
  17.5 19.2 %collective-permute-start.2 = (bf16[2,48,4,128]{3,1,2,0:T(8,128)(2,1)S(1)}, bf16[2,48,4,128]{3,1,2,0:T(8,128)(2,1)S(1)}, u32[]{:S(2)}, u32[]{:S(2)}) collective-permute-start(bf16[2,48,4,128]{3,1,2,0:T(8,128)(2,1)S(1)} %get-tuple-element.247), channel_id=1, source_target_pairs={{0,12},{4,16},{8,20},{12,24},{16,28},{1,13},{5,17},{9,21},{13,25},... | collective-permute-start | bytes 294920 | tf_op jit(solution)/shard_map/ppermute | solution.py:19
  18.8 19.2 %collective-permute-start.3 = (bf16[2,48,4,128]{3,1,2,0:T(8,128)(2,1)S(1)}, bf16[2,48,4,128]{3,1,2,0:T(8,128)(2,1)S(1)}, u32[]{:S(2)}, u32[]{:S(2)}) collective-permute-start(bf16[2,48,4,128]{3,1,2,0:T(8,128)(2,1)S(1)} %get-tuple-element.248), channel_id=1, source_target_pairs={{0,4},{4,8},{8,12},{12,16},{16,20},{20,24},{24,28},{1,5},{5,9},{9,... | collective-permute-start | bytes 294920 | tf_op jit(solution)/shard_map/ppermute | solution.py:19
  22.2 15.8 %collective-permute-start.4 = (bf16[2,48,4,128]{3,1,2,0:T(8,128)(2,1)S(1)}, bf16[2,48,4,128]{3,1,2,0:T(8,128)(2,1)S(1)}, u32[]{:S(2)}, u32[]{:S(2)}) collective-permute-start(bf16[2,48,4,128]{3,1,2,0:T(8,128)(2,1)S(1)} %get-tuple-element.249), channel_id=1, source_target_pairs={{4,0},{8,4},{12,8},{16,12},{20,16},{24,20},{28,24},{5,1},{9,5},{13... | collective-permute-start | bytes 294920 | tf_op jit(solution)/shard_map/ppermute | solution.py:19
  34.0 15.6 %collective-permute-start.5 = (bf16[2,48,4,128]{3,1,2,0:T(8,128)(2,1)S(1)}, bf16[2,48,4,128]{3,1,2,0:T(8,128)(2,1)S(1)}, u32[]{:S(2)}, u32[]{:S(2)}) collective-permute-start(bf16[2,48,4,128]{3,1,2,0:T(8,128)(2,1)S(1)} %get-tuple-element.250), channel_id=1, source_target_pairs={{12,0},{16,4},{20,8},{24,12},{28,16},{13,1},{17,5},{21,9},{25,13},... | collective-permute-start | bytes 294920 | tf_op jit(solution)/shard_map/ppermute | solution.py:19
  35.4 14.3 %collective-permute-start.6 = (bf16[2,48,4,128]{3,1,2,0:T(8,128)(2,1)S(1)}, bf16[2,48,4,128]{3,1,2,0:T(8,128)(2,1)S(1)}, u32[]{:S(2)}, u32[]{:S(2)}) collective-permute-start(bf16[2,48,4,128]{3,1,2,0:T(8,128)(2,1)S(1)} %get-tuple-element.251), channel_id=1, source_target_pairs={{16,0},{20,4},{24,8},{28,12},{17,1},{21,5},{25,9},{29,13},{18,2},{... | collective-permute-start | bytes 294920 | tf_op jit(solution)/shard_map/ppermute | solution.py:19
  36.7 13.0 %collective-permute-start.7 = (bf16[2,48,4,128]{3,1,2,0:T(8,128)(2,1)S(1)}, bf16[2,48,4,128]{3,1,2,0:T(8,128)(2,1)S(1)}, u32[]{:S(2)}, u32[]{:S(2)}) collective-permute-start(bf16[2,48,4,128]{3,1,2,0:T(8,128)(2,1)S(1)} %get-tuple-element.244), channel_id=1, source_target_pairs={{20,0},{24,4},{28,8},{21,1},{25,5},{29,9},{22,2},{26,6},{30,10},{2... | collective-permute-start | bytes 294920 | tf_op jit(solution)/shard_map/ppermute | solution.py:19
  198.1 11.5 %collective-permute-start.8 = (bf16[1,48,4,128]{3,1,2,0:T(8,128)(2,1)S(1)}, bf16[1,48,4,128]{3,1,2,0:T(8,128)(2,1)S(1)}, u32[]{:S(2)}, u32[]{:S(2)}) collective-permute-start(bf16[1,48,4,128]{3,1,2,0:T(8,128)(2,1)S(1)} %get-tuple-element.267), channel_id=1, source_target_pairs={{0,20},{4,24},{8,28},{1,21},{5,25},{9,29},{2,22},{6,26},{10,30},{3... | collective-permute-start | bytes 147464 | tf_op jit(solution)/shard_map/ppermute | solution.py:19
  199.4 11.5 %collective-permute-start.9 = (bf16[1,48,4,128]{3,1,2,0:T(8,128)(2,1)S(1)}, bf16[1,48,4,128]{3,1,2,0:T(8,128)(2,1)S(1)}, u32[]{:S(2)}, u32[]{:S(2)}) collective-permute-start(bf16[1,48,4,128]{3,1,2,0:T(8,128)(2,1)S(1)} %get-tuple-element.266), channel_id=1, source_target_pairs={{0,16},{4,20},{8,24},{12,28},{1,17},{5,21},{9,25},{13,29},{2,18},{... | collective-permute-start | bytes 147464 | tf_op jit(solution)/shard_map/ppermute | solution.py:19
  202.3 9.9 %collective-permute-start.10 = (bf16[1,48,4,128]{3,1,2,0:T(8,128)(2,1)S(1)}, bf16[1,48,4,128]{3,1,2,0:T(8,128)(2,1)S(1)}, u32[]{:S(2)}, u32[]{:S(2)}) collective-permute-start(bf16[1,48,4,128]{3,1,2,0:T(8,128)(2,1)S(1)} %get-tuple-element.265), channel_id=1, source_target_pairs={{0,12},{4,16},{8,20},{12,24},{16,28},{1,13},{5,17},{9,21},{13,25},... | collective-permute-start | bytes 147464 | tf_op jit(solution)/shard_map/ppermute | solution.py:19
  203.7 10.1 %collective-permute-start.11 = (bf16[1,48,4,128]{3,1,2,0:T(8,128)(2,1)S(1)}, bf16[1,48,4,128]{3,1,2,0:T(8,128)(2,1)S(1)}, u32[]{:S(2)}, u32[]{:S(2)}) collective-permute-start(bf16[1,48,4,128]{3,1,2,0:T(8,128)(2,1)S(1)} %get-tuple-element.264), channel_id=1, source_target_pairs={{0,4},{4,8},{8,12},{12,16},{16,20},{20,24},{24,28},{1,5},{5,9},{9,... | collective-permute-start | bytes 147464 | tf_op jit(solution)/shard_map/ppermute | solution.py:19
  209.6 8.4 %collective-permute-start.13 = (bf16[1,48,4,128]{3,1,2,0:T(8,128)(2,1)S(1)}, bf16[1,48,4,128]{3,1,2,0:T(8,128)(2,1)S(1)}, u32[]{:S(2)}, u32[]{:S(2)}) collective-permute-start(bf16[1,48,4,128]{3,1,2,0:T(8,128)(2,1)S(1)} %get-tuple-element.262), channel_id=1, source_target_pairs={{12,0},{16,4},{20,8},{24,12},{28,16},{13,1},{17,5},{21,9},{25,13},... | collective-permute-start | bytes 147464 | tf_op jit(solution)/shard_map/ppermute | solution.py:19
  210.9 8.8 %collective-permute-start.14 = (bf16[1,48,4,128]{3,1,2,0:T(8,128)(2,1)S(1)}, bf16[1,48,4,128]{3,1,2,0:T(8,128)(2,1)S(1)}, u32[]{:S(2)}, u32[]{:S(2)}) collective-permute-start(bf16[1,48,4,128]{3,1,2,0:T(8,128)(2,1)S(1)} %get-tuple-element.261), channel_id=1, source_target_pairs={{16,0},{20,4},{24,8},{28,12},{17,1},{21,5},{25,9},{29,13},{18,2},{... | collective-permute-start | bytes 147464 | tf_op jit(solution)/shard_map/ppermute | solution.py:19
  212.2 8.7 %collective-permute-start.15 = (bf16[1,48,4,128]{3,1,2,0:T(8,128)(2,1)S(1)}, bf16[1,48,4,128]{3,1,2,0:T(8,128)(2,1)S(1)}, u32[]{:S(2)}, u32[]{:S(2)}) collective-permute-start(bf16[1,48,4,128]{3,1,2,0:T(8,128)(2,1)S(1)} %get-tuple-element.260), channel_id=1, source_target_pairs={{20,0},{24,4},{28,8},{21,1},{25,5},{29,9},{22,2},{26,6},{30,10},{2... | collective-permute-start | bytes 147464 | tf_op jit(solution)/shard_map/ppermute | solution.py:19
  379.7 10.3 %collective-permute-start.16 = (bf16[1,48,4,128]{3,1,2,0:T(8,128)(2,1)S(1)}, bf16[1,48,4,128]{3,1,2,0:T(8,128)(2,1)S(1)}, u32[]{:S(2)}, u32[]{:S(2)}) collective-permute-start(bf16[1,48,4,128]{3,1,2,0:T(8,128)(2,1)S(1)} %get-tuple-element.259), channel_id=1, source_target_pairs={{0,20},{4,24},{8,28},{1,21},{5,25},{9,29},{2,22},{6,26},{10,30},{3... | collective-permute-start | bytes 147464 | tf_op jit(solution)/shard_map/ppermute | solution.py:19
  381.4 10.0 %collective-permute-start.17 = (bf16[1,48,4,128]{3,1,2,0:T(8,128)(2,1)S(1)}, bf16[1,48,4,128]{3,1,2,0:T(8,128)(2,1)S(1)}, u32[]{:S(2)}, u32[]{:S(2)}) collective-permute-start(bf16[1,48,4,128]{3,1,2,0:T(8,128)(2,1)S(1)} %get-tuple-element.258), channel_id=1, source_target_pairs={{0,16},{4,20},{8,24},{12,28},{1,17},{5,21},{9,25},{13,29},{2,18},{... | collective-permute-start | bytes 147464 | tf_op jit(solution)/shard_map/ppermute | solution.py:19
  382.7 10.0 %collective-permute-start.18 = (bf16[1,48,4,128]{3,1,2,0:T(8,128)(2,1)S(1)}, bf16[1,48,4,128]{3,1,2,0:T(8,128)(2,1)S(1)}, u32[]{:S(2)}, u32[]{:S(2)}) collective-permute-start(bf16[1,48,4,128]{3,1,2,0:T(8,128)(2,1)S(1)} %get-tuple-element.257), channel_id=1, source_target_pairs={{0,12},{4,16},{8,20},{12,24},{16,28},{1,13},{5,17},{9,21},{13,25},... | collective-permute-start | bytes 147464 | tf_op jit(solution)/shard_map/ppermute | solution.py:19
  384.0 10.3 %collective-permute-start.19 = (bf16[1,48,4,128]{3,1,2,0:T(8,128)(2,1)S(1)}, bf16[1,48,4,128]{3,1,2,0:T(8,128)(2,1)S(1)}, u32[]{:S(2)}, u32[]{:S(2)}) collective-permute-start(bf16[1,48,4,128]{3,1,2,0:T(8,128)(2,1)S(1)} %get-tuple-element.256), channel_id=1, source_target_pairs={{0,4},{4,8},{8,12},{12,16},{16,20},{20,24},{24,28},{1,5},{5,9},{9,... | collective-permute-start | bytes 147464 | tf_op jit(solution)/shard_map/ppermute | solution.py:19
  387.5 9.2 %collective-permute-start.20 = (bf16[1,48,4,128]{3,1,2,0:T(8,128)(2,1)S(1)}, bf16[1,48,4,128]{3,1,2,0:T(8,128)(2,1)S(1)}, u32[]{:S(2)}, u32[]{:S(2)}) collective-permute-start(bf16[1,48,4,128]{3,1,2,0:T(8,128)(2,1)S(1)} %get-tuple-element.255), channel_id=1, source_target_pairs={{4,0},{8,4},{12,8},{16,12},{20,16},{24,20},{28,24},{5,1},{9,5},{13... | collective-permute-start | bytes 147464 | tf_op jit(solution)/shard_map/ppermute | solution.py:19
  390.0 15.9 %collective-permute-start.21 = (bf16[1,48,4,128]{3,1,2,0:T(8,128)(2,1)S(1)}, bf16[1,48,4,128]{3,1,2,0:T(8,128)(2,1)S(1)}, u32[]{:S(2)}, u32[]{:S(2)}) collective-permute-start(bf16[1,48,4,128]{3,1,2,0:T(8,128)(2,1)S(1)} %get-tuple-element.254), channel_id=1, source_target_pairs={{12,0},{16,4},{20,8},{24,12},{28,16},{13,1},{17,5},{21,9},{25,13},... | collective-permute-start | bytes 147464 | tf_op jit(solution)/shard_map/ppermute | solution.py:19
  391.3 15.6 %collective-permute-start.22 = (bf16[1,48,4,128]{3,1,2,0:T(8,128)(2,1)S(1)}, bf16[1,48,4,128]{3,1,2,0:T(8,128)(2,1)S(1)}, u32[]{:S(2)}, u32[]{:S(2)}) collective-permute-start(bf16[1,48,4,128]{3,1,2,0:T(8,128)(2,1)S(1)} %get-tuple-element.253), channel_id=1, source_target_pairs={{16,0},{20,4},{24,8},{28,12},{17,1},{21,5},{25,9},{29,13},{18,2},{... | collective-permute-start | bytes 147464 | tf_op jit(solution)/shard_map/ppermute | solution.py:19
  392.6 14.4 %collective-permute-start.23 = (bf16[1,48,4,128]{3,1,2,0:T(8,128)(2,1)S(1)}, bf16[1,48,4,128]{3,1,2,0:T(8,128)(2,1)S(1)}, u32[]{:S(2)}, u32[]{:S(2)}) collective-permute-start(bf16[1,48,4,128]{3,1,2,0:T(8,128)(2,1)S(1)} %get-tuple-element.252), channel_id=1, source_target_pairs={{20,0},{24,4},{28,8},{21,1},{25,5},{29,9},{22,2},{26,6},{30,10},{2... | collective-permute-start | bytes 147464 | tf_op jit(solution)/shard_map/ppermute | solution.py:19
  (13 other events, 114.0 us)
Sparse Core Ops, SparseCore 0:
  378.2 120.9 all-reduce.6
where the time goes:
time: 516 us; the launch traced here: 510 us
  matrix products  143 us (28%)
  waiting for transfers between devices  118 us (23%)
  local copies, waits for them, and re-layouts  102 us (20%)
  other arithmetic  68.4 us (13%)
  starting transfers between devices  47.2 us (9%)
  blocking collectives  16.2 us (3%)
  between operations  14.9 us (3%)
    psum x1, waiting for transfers between devices, shards(): summed_one, summed_two = lax.psum((weight_sum_one, weight_sum_two), 'tile')  87.6 us
    dot_general x18, matrix products, offset_step(): jnp.einsum('ep,cpr->cer', selector, partial_term, precision=lax.Precision...  71.2 us
    ppermute x24, starting transfers between devices, shifted(): return lax.ppermute(value, axis, pairs)  47.1 us
    gather x18, local copies, waits for them, and re-layouts, offset_step(): jnp.take(extended, sources, axis=1)  45.5 us
    dot_general x18, matrix products, offset_step(): jnp.einsum('kcd,dkpr->ckpr', kernels, out_blocks, preferred_element_type=...  44 us
    gather x18, local copies, waits for them, and re-layouts, offset_step(): jnp.take(grad_blocks, targets, axis=1)  42.9 us
    select_n x18, other arithmetic, offset_step(): jnp.take(grad_blocks, targets, axis=1)  34.9 us
    ppermute x24, waiting for transfers between devices, shifted(): return lax.ppermute(value, axis, pairs)  30.9 us
  transfers between devices with their start and end apart: 25, of which 9 were waited for; matrix products, arithmetic and copies ran while one was open for 1% of the time, Pallas kernels for 0%

commit v1 on v0

v1 whole, which is shorter than its diff:
```python
import functools
import math

import jax
import jax.numpy as jnp
import numpy as np
from jax import lax
from jax.experimental import pallas as pl
from jax.experimental.pallas import tpu as pltpu
from jax.sharding import PartitionSpec as P

TILE_Y = 4
STEP_ROW = (-1, -1, -1, 0, 0, 1, 1, 1)
STEP_COL = (-1, 0, 1, -1, 1, -1, 0, 1)

VMEM = pltpu.VMEM
SMEM = pltpu.SMEM
BF16 = jnp.bfloat16
F32 = jnp.float32


def vmem_spec():
    return pl.BlockSpec(memory_space=VMEM)


def smem_spec():
    return pl.BlockSpec(memory_space=SMEM)


def cost(flops, moved):
    return pl.CostEstimate(flops=flops, bytes_accessed=moved, transcendentals=0)


def ghost_plan(tile_count, block_count, slot_count):
    rows = tile_count // TILE_Y
    groups = []
    for direction in (1, 6, 3, 4, 0, 7, 2, 5):
        pairs = []
        for tile in range(tile_count):
            row = tile // TILE_Y + STEP_ROW[direction]
            col = tile % TILE_Y + STEP_COL[direction]
            if 0 <= row < rows and 0 <= col < TILE_Y:
                pairs.append((tile, row * TILE_Y + col, direction))
        for group in groups:
            sources = {p[0] for p in group}
            targets = {p[1] for p in group}
            if all(p[0] not in sources and p[1] not in targets for p in pairs):
                group.extend(pairs)
                break
        else:
            groups.append(list(pairs))
    groups = [g for g in groups if g]
    trash = block_count + 8 * slot_count + 1
    send_dir = np.zeros((len(groups), tile_count), np.int32)
    recv_base = np.full((len(groups), tile_count), trash, np.int32)
    for index, group in enumerate(groups):
        for source, target, direction in group:
            send_dir[index, source] = direction
            recv_base[index, target] = block_count + (7 - direction) * slot_count
    pair_lists = [[(s, t) for s, t, _ in g] for g in groups]
    return pair_lists, np.stack([send_dir, recv_base], axis=1)


def pack_kernel(lists_ref, plan_ref, pre_ref, feat_ref, *out_refs):
    me = lax.axis_index("tile")
    for index, out_ref in enumerate(out_refs):
        direction = plan_ref[index, 0, me]
        for slot in range(out_ref.shape[1]):
            block = jnp.minimum(lists_ref[0, direction, slot], pre_ref.shape[1] // 128 - 1)
            lanes = pl.ds(pl.multiple_of(block * 128, 128), 128)
            out_ref[0, slot] = jnp.maximum(pre_ref[:, lanes], 0)
            out_ref[1, slot] = feat_ref[:, lanes]


def pack(lists, plan, pre_act, features, slot_count):
    width = features.shape[0]
    group_count = plan.shape[0]
    shape = jax.ShapeDtypeStruct((2, slot_count, width, 128), BF16)
    return pl.pallas_call(
        pack_kernel,
        out_shape=[shape] * group_count,
        in_specs=[smem_spec(), smem_spec(), vmem_spec(), vmem_spec()],
        out_specs=[vmem_spec()] * group_count,
        name="pack_sends",
        cost_estimate=cost(0, 4 * features.size + 4 * group_count * slot_count * width * 128),
    )(lists, plan, pre_act, features)


def gather_full(parts, full):
    me = lax.axis_index("chan")
    width = parts[0].shape[0]
    for step, part in enumerate(parts):
        place = pl.multiple_of((me ^ step) * width, 16)
        full[pl.ds(place, width), :] = part[...]


def partial_kernel(group_count, pin_ref, plan_ref, *refs):
    parts, refs = refs[:4], refs[4:]
    weight_ref, local_ref = refs[:2]
    back_refs = refs[2 : 2 + group_count]
    full, product, total = refs[2 + group_count :]
    me = lax.axis_index("tile")
    offset_count, block_count = pin_ref.shape[1:]
    width = local_ref.shape[1]
    gather_full(parts, full)
    total[...] = jnp.zeros_like(total)

    def two_blocks(turn, _):
        lanes = pl.ds(pl.multiple_of(turn * 256, 256), 256)
        product[...] = jnp.dot(weight_ref[...], full[:, lanes], preferred_element_type=F32)
        for offset in range(offset_count):
            for half in range(2):
                entry = pin_ref[0, offset, turn * 2 + half]
                total[entry] += product[
                    offset * width : (offset + 1) * width, half * 128 : (half + 1) * 128
                ]
        return 0

    lax.fori_loop(0, block_count // 2, two_blocks, 0)
    local_ref[...] = total[:block_count]
    for index, back_ref in enumerate(back_refs):
        base = plan_ref[index, 1, me]
        for slot in range(back_ref.shape[0]):
            back_ref[slot] = total[base + slot].astype(BF16)


def partial_sums(pin, plan, parts, weight, slot_count):
    width, voxels = parts[0].shape
    offset_count, block_count = pin.shape[1:]
    group_count = plan.shape[0]
    entries = block_count + 9 * slot_count + 1
    outs = [jax.ShapeDtypeStruct((block_count, width, 128), F32)]
    outs += [jax.ShapeDtypeStruct((slot_count, width, 128), BF16)] * group_count
    result = pl.pallas_call(
        functools.partial(partial_kernel, group_count),
        out_shape=outs,
        in_specs=[smem_spec(), smem_spec()] + [vmem_spec()] * 5,
        out_specs=[vmem_spec()] * (1 + group_count),
        scratch_shapes=[
            VMEM((4 * width, voxels), BF16),
            VMEM((offset_count * width, 256), F32),
            VMEM((entries, width, 128), F32),
        ],
        name="partial_sums",
        cost_estimate=cost(2 * weight.size * voxels, 2 * weight.size + 12 * width * voxels),
        compiler_params=pltpu.CompilerParams(vmem_limit_bytes=24 << 20),
    )(pin, plan, *parts, weight.reshape(offset_count * width, 4 * width))
    return result[0], result[1:]


def weight_kernel(group_count, which, factor, finish, pin_ref, plan_ref, *refs):
    parts, refs = refs[:4], refs[4:]
    own_ref = refs[0]
    ghost_refs = refs[1 : 1 + group_count]
    out_count = finish.out_count
    out_refs = refs[1 + group_count : 1 + group_count + out_count]
    full, extended, gathered, *extra = refs[1 + group_count + out_count :]
    me = lax.axis_index("tile")
    offset_count, block_count = pin_ref.shape[1:]
    width = own_ref.shape[0]
    gather_full(parts, full)
    for block in range(block_count):
        value = own_ref[:, block * 128 : (block + 1) * 128]
        extended[block] = jnp.maximum(value, 0) if which == 0 else value
    for index, ghost_ref in enumerate(ghost_refs):
        base = plan_ref[index, 1, me]
        for slot in range(ghost_ref.shape[1]):
            extended[base + slot] = ghost_ref[which, slot]
    empty = block_count + 8 * ghost_refs[0].shape[1]
    extended[empty] = jnp.zeros_like(extended[empty])
    chunk = gathered.shape[0] // width

    def some_offsets(turn, _):
        for step in range(chunk):
            for block in range(block_count):
                entry = pin_ref[0, turn * chunk + step, block]
                gathered[step * width : (step + 1) * width, block * 128 : (block + 1) * 128] = (
                    extended[entry]
                )
        grads = lax.dot_general(
            gathered[...], full[...], (((1,), (1,)), ((), ())), preferred_element_type=F32
        )
        finish.store(turn, grads * factor, out_refs, extra)
        return 0

    lax.fori_loop(0, offset_count // chunk, some_offsets, 0)
    finish.end(out_refs, extra)


class PlainFinish:
    out_count = 1

    def __init__(self, rows, columns):
        self.shapes = [jax.ShapeDtypeStruct((rows, columns), F32)]
        self.scratch = []

    def store(self, turn, grads, out_refs, extra):
        rows = grads.shape[0]
        out_refs[0][pl.ds(pl.multiple_of(turn * rows, 16), rows), :] = grads

    def end(self, out_refs, extra):
        pass


def packed_rows(rows, tile_count):
    used = rows + rows // 2
    step = 16 * tile_count
    return -(-used // step) * step


class SplitFinish:
    out_count = 2

    def __init__(self, rows, columns, tile_count):
        self.rows = rows
        self.tall = packed_rows(rows, tile_count)
        half = (self.tall // 2, 128)
        self.shapes = [jax.ShapeDtypeStruct(half, F32), jax.ShapeDtypeStruct(half, BF16)]
        self.scratch = [VMEM((rows, 256), F32), VMEM((self.tall, 128), F32)]

    def store(self, turn, grads, out_refs, extra):
        rows = grads.shape[0]
        here = pl.ds(pl.multiple_of(turn * rows, 16), rows)
        extra[0][here, :192] = grads

    def end(self, out_refs, extra):
        wide, tall = extra
        rows, half = self.rows, self.rows // 2
        tall[:rows] = wide[:, :128]
        tall[rows : rows + half, :64] = wide[:half, 128:192]
        tall[rows : rows + half, 64:] = wide[half:, 128:192]
        if self.tall > rows + half:
            tall[rows + half :] = jnp.zeros((self.tall - rows - half, 128), F32)
        bit = exchange_bit(0)
        split = self.tall // 2
        out_refs[0][...] = tall[pl.ds(pl.multiple_of(bit * split, 16), split), :]
        out_refs[1][...] = tall[pl.ds(pl.multiple_of((1 - bit) * split, 16), split), :].astype(BF16)


def weight_sums(pin, plan, parts, own, ghosts, which, factor, finish):
    width, voxels = own.shape
    offset_count, block_count = pin.shape[1:]
    group_count = plan.shape[0]
    slot_count = ghosts[0].shape[1]
    entries = block_count + 9 * slot_count + 1
    chunk = 9 if offset_count % 9 == 0 else 1
    flops = 2 * offset_count * width * 4 * width * voxels
    return pl.pallas_call(
        functools.partial(weight_kernel, group_count, which, factor, finish),
        out_shape=finish.shapes,
        in_specs=[smem_spec(), smem_spec()] + [vmem_spec()] * (5 + group_count),
        out_specs=[vmem_spec()] * finish.out_count,
        scratch_shapes=[
            VMEM((4 * width, voxels), BF16),
            VMEM((entries, width, 128), BF16),
            VMEM((chunk * width, voxels), BF16),
        ]
        + finish.scratch,
        name="weight_sums",
        cost_estimate=cost(flops, 16 * width * voxels + 4 * offset_count * width * 4 * width),
        compiler_params=pltpu.CompilerParams(vmem_limit_bytes=24 << 20),
    )(pin, plan, *parts, own, *ghosts)


def settle_kernel(first, group_count, lists_ref, plan_ref, local_ref, other_ref, *refs):
    back_refs = refs[:group_count]
    out_ref, total = refs[group_count:]
    me = lax.axis_index("tile")
    block_count = local_ref.shape[0]
    total[:block_count] = local_ref[...]
    for index, back_ref in enumerate(back_refs):
        direction = plan_ref[index, 0, me]
        for slot in range(back_ref.shape[0]):
            block = lists_ref[0, direction, slot]
            total[block] += back_ref[slot].astype(F32)
    for block in range(block_count):
        lanes = slice(block * 128, (block + 1) * 128)
        other = other_ref[:, lanes].astype(F32)
        if first:
            value = jnp.where(other > 0, total[block], 0.0)
        else:
            value = other + total[block]
        out_ref[:, lanes] = value.astype(BF16)


def settle(first, lists, plan, local, other, backs):
    block_count, width, _ = local.shape
    group_count = len(backs)
    return pl.pallas_call(
        functools.partial(settle_kernel, first, group_count),
        out_shape=jax.ShapeDtypeStruct(other.shape, BF16),
        in_specs=[smem_spec(), smem_spec()] + [vmem_spec()] * (2 + group_count),
        out_specs=vmem_spec(),
        scratch_shapes=[VMEM((block_count + 1, width, 128), F32)],
        name="settle",
        cost_estimate=cost(local.size, 8 * local.size),
    )(lists, plan, local, other, *backs)


def exchange_dim(step):
    parity = lax.axis_index("chan") % 2
    if step < 2:
        return jnp.where(parity == 0, step, 1 - step)
    return step


def exchange_bit(step):
    return lax.shift_right_logical(lax.axis_index("tile"), exchange_dim(step)) & 1


def exchange_pairs(step, tile_count, chan_count):
    pairs = []
    for tile in range(tile_count):
        for chan in range(chan_count):
            dim = (1 - step if chan % 2 else step) if step < 2 else step
            pairs.append((tile * chan_count + chan, (tile ^ (1 << dim)) * chan_count + chan))
    return pairs


def halve_kernel(step, keep_ref, got_ref, next_ref, send_ref):
    bit = exchange_bit(step)
    split = next_ref.shape[0]
    mine = pl.ds(pl.multiple_of(bit * split, 16), split)
    theirs = pl.ds(pl.multiple_of((1 - bit) * split, 16), split)
    next_ref[...] = keep_ref[mine, :] + got_ref[mine, :].astype(F32)
    send_ref[...] = (keep_ref[theirs, :] + got_ref[theirs, :].astype(F32)).astype(BF16)


def halve(step, keep, got):
    rows = keep.shape[0] // 2
    return pl.pallas_call(
        functools.partial(halve_kernel, step),
        out_shape=[jax.ShapeDtypeStruct((rows, 128), F32), jax.ShapeDtypeStruct((rows, 128), BF16)],
        in_specs=[vmem_spec()] * 2,
        out_specs=[vmem_spec()] * 2,
        name="halve",
        cost_estimate=cost(keep.size, 10 * keep.size),
    )(keep, got)


def unpack_kernel(tile_count, own_ref, got_ref, out_ref, tall):
    steps = tile_count.bit_length() - 1
    chunk = tall.shape[0] // tile_count
    mine = 0
    for step in range(steps):
        mine = mine * 2 + exchange_bit(step)
    for index in range(tile_count):
        source, place = (own_ref, index) if index < tile_count // 2 else (got_ref, index - tile_count // 2)
        rows = pl.ds(pl.multiple_of((mine ^ index) * chunk, 16), chunk)
        tall[rows, :] = source[place * chunk : (place + 1) * chunk, :].astype(F32)
    rows = out_ref.shape[0]
    half = rows // 2
    out_ref[:, :128] = tall[:rows]
    out_ref[:half, 128:192] = tall[rows : rows + half, :64]
    out_ref[half:, 128:192] = tall[rows : rows + half, 64:]


def unpack(own, got, rows, columns, tile_count):
    tall = own.shape[0] * 2
    return pl.pallas_call(
        functools.partial(unpack_kernel, tile_count),
        out_shape=jax.ShapeDtypeStruct((rows, columns), F32),
        in_specs=[vmem_spec()] * 2,
        out_specs=vmem_spec(),
        scratch_shapes=[VMEM((tall, 128), F32)],
        name="unpack_sum",
        cost_estimate=cost(0, 6 * rows * columns),
    )(own, got)


def sum_over_tiles(keep, send, rows, columns):
    tile_count = lax.axis_size("tile")
    chan_count = lax.axis_size("chan")
    steps = tile_count.bit_length() - 1
    trade = lambda value, step: lax.ppermute(
        value, ("tile", "chan"), exchange_pairs(step, tile_count, chan_count)
    )
    for step in range(steps):
        got = trade(send, step)
        if step < steps - 1:
            keep, send = halve(step + 1, keep, got)
        else:
            chunk = (keep + got.astype(F32)).astype(BF16)
    for step in reversed(range(steps)):
        got = trade(chunk, step)
        if step:
            chunk = jnp.concatenate([chunk, got], axis=0)
    return unpack(chunk, got, rows, columns, tile_count)


def all_parts(part):
    trade = lambda value, bits: lax.ppermute(value, "chan", [(i, i ^ bits) for i in range(4)])
    far = trade(part, 2)
    near = trade(part, 1)
    return (part, near, far, trade(far, 1))


def shards(features, pre_act, cotangent, weight_one, weight_two, send_list, pair_in, pair_out):
    tile_count = lax.axis_size("tile")
    width, voxels = features.shape
    offset_count, _, columns = weight_one.shape
    block_count = pair_out.shape[2]
    slot_count = send_list.shape[2]
    rows = offset_count * width
    pair_lists, plan = ghost_plan(tile_count, block_count, slot_count)
    plan = jnp.asarray(plan)
    factor = 1.0 / math.sqrt(tile_count * voxels)

    sends = pack(send_list, plan, pre_act, features, slot_count)
    cot_parts = all_parts(cotangent)
    ghosts = [lax.ppermute(s, "tile", p) for s, p in zip(sends, pair_lists)]
    back_lists = [[(t, s) for s, t in p] for p in pair_lists]
    give_back = lambda backs: [lax.ppermute(b, "tile", p) for b, p in zip(backs, back_lists)]

    local_two, back_two = partial_sums(pair_in, plan, cot_parts, weight_two, slot_count)
    back_two = give_back(back_two)
    sum_two = weight_sums(
        pair_in, plan, cot_parts, pre_act, ghosts, 0, factor, PlainFinish(rows, columns)
    )[0]
    grad_two = lax.psum(sum_two, "tile")
    grad_pre = settle(True, send_list, plan, local_two, pre_act, back_two)

    pre_parts = all_parts(grad_pre)
    keep, send = weight_sums(
        pair_in, plan, pre_parts, features, ghosts, 1, factor, SplitFinish(rows, columns, tile_count)
    )
    local_one, back_one = partial_sums(pair_in, plan, pre_parts, weight_one, slot_count)
    grad_one = sum_over_tiles(keep, send, rows, columns)
    grad_features = settle(False, send_list, plan, local_one, cotangent, give_back(back_one))
    shape = (offset_count, width, columns)
    return grad_features, grad_one.reshape(shape), grad_two.reshape(shape)


def solution(mesh):
    return jax.shard_map(
        shards,
        mesh=mesh,
        in_specs=(
            P("chan", "tile"),
            P("chan", "tile"),
            P("chan", "tile"),
            P(None, "chan", None),
            P(None, "chan", None),
            P("tile", None, None),
            P("tile", None, None),
            P("tile", None, None),
        ),
        out_specs=(P("chan", "tile"), P(None, "chan", None), P(None, "chan", None)),
        check_vma=False,
    )
```

time: 516 us -> 191 us (0.37)
  matrix products: 143 us -> 0 us
  local copies, waits for them, and re-layouts: 102 us -> 13.1 us
  other arithmetic: 68.4 us -> 0.95 us
  waiting for transfers between devices: 118 us -> 84.3 us
  Pallas kernels: 0 us -> 29 us
  blocking collectives: 16.2 us -> 0 us
    dot_general x54 -> x0, matrix products: 143 us -> none  [the longest x18 71.2 us: offset_step(): jnp.einsum('ep,cpr->cer', selector, partial_term, precision=lax.Precision...]
    gather x38 -> x0, local copies, waits for them, and re-layouts: 89.7 us -> none  [the longest x18 45.5 us: offset_step(): jnp.take(extended, sources, axis=1)]
    psum x1, waiting for transfers between devices: 87.6 us -> 28.4 us  [shards(): grad_two = lax.psum(sum_two, 'tile')]
    select_n x57 -> x0, other arithmetic: 56.4 us -> none  [the longest x18 34.9 us: offset_step(): jnp.take(grad_blocks, targets, axis=1)]
    pallas_call x0 -> x10, Pallas kernels: none -> 29 us  [the longest x2 9.69 us: partial_sums(): pl.pallas_call(functools.partial(partial_kernel, group_count), out_shape=...]
    ppermute x24 -> x27, waiting for transfers between devices: 30.9 us -> 55.9 us  [the longest x6 31.5 us: sum_over_tiles(): lax.ppermute(value, ('tile', 'chan'), exchange_pairs(step, tile_count, ch...]
    all_gather x2 -> x0, blocking collectives: 16.2 us -> none  [the longest x1 8.63 us: shards(): full_cotangent = lax.all_gather(cotangent, 'chan', axis=0, tiled=True)]
    unnamed x31 -> x59, local copies, waits for them, and re-layouts: 2.63 us -> 13.1 us
  transfers between devices with their start and end apart: 25 -> 28, of which waited for: 9 -> 14; matrix products, arithmetic and copies ran while one was open for 1% -> 1% of each run, Pallas kernels for 0% -> 9%
where the time goes in v1:
time: 191 us; the launch traced here: 188 us
  waiting for transfers between devices  84.3 us (44%)
  starting transfers between devices  46.6 us (24%)
  Pallas kernels  29 us (15%)
  between operations  14.4 us (8%)
  local copies, waits for them, and re-layouts  13.1 us (7%)
    ppermute x6, waiting for transfers between devices, sum_over_tiles(): lax.ppermute(value, ('tile', 'chan'), exchange_pairs(step, tile_count, ch...  31.5 us
    ppermute x10, starting transfers between devices, shards(): lax.ppermute(b, 'tile', p)  28.5 us
    psum x1, waiting for transfers between devices, shards(): grad_two = lax.psum(sum_two, 'tile')  28.4 us
    unnamed x59, local copies, waits for them, and re-layouts  13.1 us
    ppermute x5, starting transfers between devices, shards(): ghosts = [lax.ppermute(s, 'tile', p) for s, p in zip(sends, pair_lists)]  13 us
    ppermute x10, waiting for transfers between devices, shards(): lax.ppermute(b, 'tile', p)  11.1 us
    pallas_call x2, Pallas kernels, partial_sums(): pl.pallas_call(functools.partial(partial_kernel, group_count), out_shape=...  9.69 us
    pallas_call x2, Pallas kernels, weight_sums(): pl.pallas_call(functools.partial(weight_kernel, group_count, which, facto...  7.38 us
  transfers between devices with their start and end apart: 28, of which 14 were waited for; matrix products, arithmetic and copies ran while one was open for 1% of the time, Pallas kernels for 9%

profile of v1, /device:TPU:2, one launch (start us, length us, event | category | flops | bytes accessed | tf_op | source)
XLA Modules:
  0.0 188.3 jit_solution(5587725750794253906)
XLA Ops:
  8.8 5.3 %collective-permute-done.1.refs_2_ = bf16[48,2048]{1,0:T(8,128)(2,1)S(1)} collective-permute-done((bf16[48,2048]{1,0:T(8,128)(2,1)}, bf16[48,2048]{1,0:T(8,128)(2,1)S(1)}, u32[]{:S(2)}, u32[]{:S(2)}) %collective-permute-start.1) | collective-permute-done | bytes 196640 | tf_op jit(solution)/shard_map/ppermute | solution.py:392
  18.3 4.8 %partial_sums.2 = (f32[16,48,128]{2,1,0:T(8,128)S(1)}, bf16[4,48,128]{2,1,0:T(8,128)(2,1)S(1)}, bf16[4,48,128]{2,1,0:T(8,128)(2,1)S(1)}, bf16[4,48,128]{2,1,0:T(...) custom-call(s32[1,27,16]{2,1,0:T(8,128)S(1)} %copy.13.pin_ref, ...), custom_call_target="tpu_custom_call" | custom-call | flops 1019215872 | bytes 1677312 | tf_op jit(solution)/shard_map/partial_sums/pallas_call | solution.py:134
  23.9 2.6 %collective-permute-start.3 = (bf16[4,48,128]{2,1,0:T(8,128)(2,1)S(1)}, bf16[4,48,128]{2,1,0:T(8,128)(2,1)S(1)}, u32[]{:S(2)}, u32[]{:S(2)}) collective-permute-start(bf16[4,48,128]{2,1,0:T(8,128)(2,1)S(1)} %get-tuple-element.27), channel_id=1, source_target_pairs={{0,16},{4,20},{8,24},{12,28},{16,0},{20,4},{24,8},{28,12},{1,17},{... | collective-permute-start | bytes 147464 | tf_op jit(solution)/shard_map/ppermute | solution.py:413
  26.5 3.4 %collective-permute-start.4 = (bf16[4,48,128]{2,1,0:T(8,128)(2,1)S(1)}, bf16[4,48,128]{2,1,0:T(8,128)(2,1)S(1)}, u32[]{:S(2)}, u32[]{:S(2)}) collective-permute-start(bf16[4,48,128]{2,1,0:T(8,128)(2,1)S(1)} %get-tuple-element.28), channel_id=1, source_target_pairs={{0,4},{4,8},{8,12},{16,20},{20,24},{24,28},{1,5},{5,9},{9,13},{17,... | collective-permute-start | bytes 147464 | tf_op jit(solution)/shard_map/ppermute | solution.py:413
  29.9 2.4 %collective-permute-start.5 = (bf16[4,48,128]{2,1,0:T(8,128)(2,1)S(1)}, bf16[4,48,128]{2,1,0:T(8,128)(2,1)S(1)}, u32[]{:S(2)}, u32[]{:S(2)}) collective-permute-start(bf16[4,48,128]{2,1,0:T(8,128)(2,1)S(1)} %get-tuple-element.29), channel_id=1, source_target_pairs={{4,0},{8,4},{12,8},{20,16},{24,20},{28,24},{5,1},{9,5},{13,9},{21,... | collective-permute-start | bytes 147464 | tf_op jit(solution)/shard_map/ppermute | solution.py:413
  32.3 4.2 %collective-permute-start.6 = (bf16[4,48,128]{2,1,0:T(8,128)(2,1)S(1)}, bf16[4,48,128]{2,1,0:T(8,128)(2,1)S(1)}, u32[]{:S(2)}, u32[]{:S(2)}) collective-permute-start(bf16[4,48,128]{2,1,0:T(8,128)(2,1)S(1)} %get-tuple-element.30), channel_id=1, source_target_pairs={{0,20},{4,24},{8,28},{20,0},{24,4},{28,8},{1,21},{5,25},{9,29},{21... | collective-permute-start | bytes 147464 | tf_op jit(solution)/shard_map/ppermute | solution.py:413
  41.3 3.0 %collective-permute-done.7.refs_4_ = bf16[4,48,128]{2,1,0:T(8,128)(2,1)S(1)} collective-permute-done((bf16[4,48,128]{2,1,0:T(8,128)(2,1)S(1)}, bf16[4,48,128]{2,1,0:T(8,128)(2,1)S(1)}, u32[]{:S(2)}, u32[]{:S(2)}) %collective-permute-start.7) | collective-permute-done | bytes 49184 | tf_op jit(solution)/shard_map/ppermute | solution.py:413
  50.4 2.6 %collective-permute-start.17 = (bf16[2,4,48,128]{3,2,1,0:T(8,128)(2,1)}, bf16[2,4,48,128]{3,2,1,0:T(8,128)(2,1)S(1)}, u32[]{:S(2)}, u32[]{:S(2)}) collective-permute-start(bf16[2,4,48,128]{3,2,1,0:T(8,128)(2,1)} %get-tuple-element.39), channel_id=1, source_target_pairs={{4,0},{8,4},{12,8},{20,16},{24,20},{28,24},{5,1},{9,5},{13,9},{21,... | collective-permute-start | bytes 294920 | tf_op jit(solution)/shard_map/ppermute | solution.py:411
  53.6 4.2 %collective-permute-start.18 = (bf16[2,4,48,128]{3,2,1,0:T(8,128)(2,1)}, bf16[2,4,48,128]{3,2,1,0:T(8,128)(2,1)S(1)}, u32[]{:S(2)}, u32[]{:S(2)}) collective-permute-start(bf16[2,4,48,128]{3,2,1,0:T(8,128)(2,1)} %get-tuple-element.40), channel_id=1, source_target_pairs={{0,4},{4,8},{8,12},{16,20},{20,24},{24,28},{1,5},{5,9},{9,13},{17,... | collective-permute-start | bytes 294920 | tf_op jit(solution)/shard_map/ppermute | solution.py:411
  57.8 4.2 %collective-permute-start.19 = (bf16[2,4,48,128]{3,2,1,0:T(8,128)(2,1)}, bf16[2,4,48,128]{3,2,1,0:T(8,128)(2,1)S(1)}, u32[]{:S(2)}, u32[]{:S(2)}) collective-permute-start(bf16[2,4,48,128]{3,2,1,0:T(8,128)(2,1)} %get-tuple-element.41), channel_id=1, source_target_pairs={{20,0},{24,4},{28,8},{0,20},{4,24},{8,28},{21,1},{25,5},{29,9},{1,... | collective-permute-start | bytes 294920 | tf_op jit(solution)/shard_map/ppermute | solution.py:411
  64.1 3.2 %collective-permute-done.19.refs_8_ = bf16[2,4,48,128]{3,2,1,0:T(8,128)(2,1)S(1)} collective-permute-done((bf16[2,4,48,128]{3,2,1,0:T(8,128)(2,1)}, bf16[2,4,48,128]{3,2,1,0:T(8,128)(2,1)S(1)}, u32[]{:S(2)}, u32[]{:S(2)}) %collective-permute-start.19) | collective-permute-done | bytes 98336 | tf_op jit(solution)/shard_map/ppermute | solution.py:411
  67.4 4.1 %collective-permute-done.20.refs_9_ = bf16[2,4,48,128]{3,2,1,0:T(8,128)(2,1)S(1)} collective-permute-done((bf16[2,4,48,128]{3,2,1,0:T(8,128)(2,1)}, bf16[2,4,48,128]{3,2,1,0:T(8,128)(2,1)S(1)}, u32[]{:S(2)}, u32[]{:S(2)}) %collective-permute-start.20) | collective-permute-done | bytes 98336 | tf_op jit(solution)/shard_map/ppermute | solution.py:411
  72.4 3.3 %weight_sums.2 = (f32[1024,128]{1,0:T(8,128)S(1)}, bf16[1024,128]{1,0:T(8,128)(2,1)S(1)}) custom-call(s32[1,27,16]{2,1,0:T(8,128)S(1)} %copy.13.pin_ref, s32[5,2,8]{2,1,0:T(2,128)S(1)} %copy-done.10, bf16[48,2048]{1,0:T(8,128)(2,1)S(1)} %copy-done.6, bf16[48,2048]{1,0:T(8,128)(2,1)S(1)} %collective-permute-done.8.refs_1_, ...), custom_call_target="tpu_custom_call" | custom-call | flops 1019215872 | bytes 2568192 | tf_op jit(solution)/shard_map/weight_sums/pallas_call | solution.py:248
  76.5 6.4 %collective-permute-done.21.got_ref = bf16[1024,128]{1,0:T(8,128)(2,1)S(1)} collective-permute-done((bf16[1024,128]{1,0:T(8,128)(2,1)S(1)}, bf16[1024,128]{1,0:T(8,128)(2,1)S(1)}, u32[]{:S(2)}, u32[]{:S(2)}) %collective-permute-start.21) | collective-permute-done | bytes 262176 | tf_op jit(solution)/shard_map/ppermute | solution.py:375
  85.5 4.1 %weight_sums.3 = f32[1296,192]{1,0:T(8,128)} custom-call(s32[1,27,16]{2,1,0:T(8,128)S(1)} %copy.13.pin_ref, s32[5,2,8]{2,1,0:T(2,128)S(1)} %copy-done.10, bf16[48,2048]{1,0:T(8,128)(2,1)S(1)} %copy-done.5, bf16[48,2048]{1,0:T(8,128)(2,1)S(1)} %collective-permute-done.refs_1_, bf16[48,2048]{1,0:T(8,128)(2,1)S(1)} %collective-permute-done.1.refs_2_, ...), custom_call_target="tpu_custom_call" | custom-call | flops 1019215872 | bytes 2568192 | tf_op jit(solution)/shard_map/weight_sums/pallas_call | solution.py:248
  93.5 9.4 %collective-permute-done.23 = bf16[256,128]{1,0:T(8,128)(2,1)S(1)} collective-permute-done((bf16[256,128]{1,0:T(8,128)(2,1)}, bf16[256,128]{1,0:T(8,128)(2,1)S(1)}, u32[]{:S(2)}, u32[]{:S(2)}) %collective-permute-start.23) | collective-permute-done | bytes 65568 | tf_op jit(solution)/shard_map/ppermute | solution.py:375
  103.9 8.9 %collective-permute-done.24 = bf16[256,128]{1,0:T(8,128)(2,1)S(1)} collective-permute-done((bf16[256,128]{1,0:T(8,128)(2,1)S(1)}, bf16[256,128]{1,0:T(8,128)(2,1)S(1)}, u32[]{:S(2)}, u32[]{:S(2)}) %collective-permute-start.24) | collective-permute-done | bytes 65568 | tf_op jit(solution)/shard_map/ppermute | solution.py:375
  112.9 5.8 %collective-permute-done.25 = bf16[512,128]{1,0:T(8,128)(2,1)S(1)} collective-permute-done((bf16[512,128]{1,0:T(8,128)(2,1)S(1)}, bf16[512,128]{1,0:T(8,128)(2,1)S(1)}, u32[]{:S(2)}, u32[]{:S(2)}) %collective-permute-start.25) | collective-permute-done | bytes 131104 | tf_op jit(solution)/shard_map/ppermute | solution.py:375
  119.3 4.8 %partial_sums.3 = (f32[16,48,128]{2,1,0:T(8,128)S(1)}, bf16[4,48,128]{2,1,0:T(8,128)(2,1)S(1)}, bf16[4,48,128]{2,1,0:T(8,128)(2,1)S(1)}, bf16[4,48,128]{2,1,0:T(...) custom-call(s32[1,27,16]{2,1,0:T(8,128)S(1)} %copy.13.pin_ref, ...), custom_call_target="tpu_custom_call" | custom-call | flops 1019215872 | bytes 1677312 | tf_op jit(solution)/shard_map/partial_sums/pallas_call | solution.py:134
  125.5 4.5 %collective-permute-start.12 = (bf16[4,48,128]{2,1,0:T(8,128)(2,1)S(1)}, bf16[4,48,128]{2,1,0:T(8,128)(2,1)S(1)}, u32[]{:S(2)}, u32[]{:S(2)}) collective-permute-start(bf16[4,48,128]{2,1,0:T(8,128)(2,1)S(1)} %get-tuple-element.34), channel_id=1, source_target_pairs={{0,4},{4,8},{8,12},{16,20},{20,24},{24,28},{1,5},{5,9},{9,13},{17,... | collective-permute-start | bytes 147464 | tf_op jit(solution)/shard_map/ppermute | solution.py:413
  131.8 5.2 %collective-permute-start.14 = (bf16[4,48,128]{2,1,0:T(8,128)(2,1)S(1)}, bf16[4,48,128]{2,1,0:T(8,128)(2,1)S(1)}, u32[]{:S(2)}, u32[]{:S(2)}) collective-permute-start(bf16[4,48,128]{2,1,0:T(8,128)(2,1)S(1)} %get-tuple-element.36), channel_id=1, source_target_pairs={{0,20},{4,24},{8,28},{20,0},{24,4},{28,8},{1,21},{5,25},{9,29},{21... | collective-permute-start | bytes 147464 | tf_op jit(solution)/shard_map/ppermute | solution.py:413
  140.5 4.5 %collective-permute-done.15.refs_4_ = bf16[4,48,128]{2,1,0:T(8,128)(2,1)S(1)} collective-permute-done((bf16[4,48,128]{2,1,0:T(8,128)(2,1)S(1)}, bf16[4,48,128]{2,1,0:T(8,128)(2,1)S(1)}, u32[]{:S(2)}, u32[]{:S(2)}) %collective-permute-start.15) | collective-permute-done | bytes 49184 | tf_op jit(solution)/shard_map/ppermute | solution.py:413
  150.7 28.4 %all-reduce.2.cloned.1.call-done = f32[27,48,192]{2,1,0:T(8,128)} async-done(((f32[27,48,192]{2,1,0:T(8,128)}), f32[27,48,192]{2,1,0:T(8,128)}) %all-reduce.2.cloned.1.call-update) | async-done | bytes 995344 | tf_op jit(solution)/shard_map/psum | solution.py:420
  179.0 2.5 %copy.19 = f32[27,48,192]{2,1,0:T(8,128)} copy(f32[27,48,192]{2,1,0:T(8,128)} %all-reduce.2.cloned.1.call-done) | data formatting | bytes 1990656
  (105 shorter events, 42.2 us)
Async XLA Ops:
  7.2 171.9 %all-reduce.2.cloned.1.call-start = ((), (), s32[]{:S(2)}) async-start(), calls=%async_computation | async-start | bytes 2654208 | tf_op jit(solution)/shard_map/psum | solution.py:420
  7.2 6.9 %collective-permute-start.1 = (bf16[48,2048]{1,0:T(8,128)(2,1)}, bf16[48,2048]{1,0:T(8,128)(2,1)S(1)}, u32[]{:S(2)}, u32[]{:S(2)}) collective-permute-start(bf16[48,2048]{1,0:T(8,128)(2,1)} %refs_0_.3), channel_id=1, source_target_pairs={{0,2},{1,3},{2,0},{3,1},{4,6},{5,7},{6,4},{7,5},{8,10},{9,11},{10,... | collective-permute-start | bytes 589832 | tf_op jit(solution)/shard_map/ppermute | solution.py:392
  23.9 15.2 %collective-permute-start.3 = (bf16[4,48,128]{2,1,0:T(8,128)(2,1)S(1)}, bf16[4,48,128]{2,1,0:T(8,128)(2,1)S(1)}, u32[]{:S(2)}, u32[]{:S(2)}) collective-permute-start(bf16[4,48,128]{2,1,0:T(8,128)(2,1)S(1)} %get-tuple-element.27), channel_id=1, source_target_pairs={{0,16},{4,20},{8,24},{12,28},{16,0},{20,4},{24,8},{28,12},{1,17},{... | collective-permute-start | bytes 147464 | tf_op jit(solution)/shard_map/ppermute | solution.py:413
  26.5 12.6 %collective-permute-start.4 = (bf16[4,48,128]{2,1,0:T(8,128)(2,1)S(1)}, bf16[4,48,128]{2,1,0:T(8,128)(2,1)S(1)}, u32[]{:S(2)}, u32[]{:S(2)}) collective-permute-start(bf16[4,48,128]{2,1,0:T(8,128)(2,1)S(1)} %get-tuple-element.28), channel_id=1, source_target_pairs={{0,4},{4,8},{8,12},{16,20},{20,24},{24,28},{1,5},{5,9},{9,13},{17,... | collective-permute-start | bytes 147464 | tf_op jit(solution)/shard_map/ppermute | solution.py:413
  29.9 9.2 %collective-permute-start.5 = (bf16[4,48,128]{2,1,0:T(8,128)(2,1)S(1)}, bf16[4,48,128]{2,1,0:T(8,128)(2,1)S(1)}, u32[]{:S(2)}, u32[]{:S(2)}) collective-permute-start(bf16[4,48,128]{2,1,0:T(8,128)(2,1)S(1)} %get-tuple-element.29), channel_id=1, source_target_pairs={{4,0},{8,4},{12,8},{20,16},{24,20},{28,24},{5,1},{9,5},{13,9},{21,... | collective-permute-start | bytes 147464 | tf_op jit(solution)/shard_map/ppermute | solution.py:413
  32.3 9.0 %collective-permute-start.6 = (bf16[4,48,128]{2,1,0:T(8,128)(2,1)S(1)}, bf16[4,48,128]{2,1,0:T(8,128)(2,1)S(1)}, u32[]{:S(2)}, u32[]{:S(2)}) collective-permute-start(bf16[4,48,128]{2,1,0:T(8,128)(2,1)S(1)} %get-tuple-element.30), channel_id=1, source_target_pairs={{0,20},{4,24},{8,28},{20,0},{24,4},{28,8},{1,21},{5,25},{9,29},{21... | collective-permute-start | bytes 147464 | tf_op jit(solution)/shard_map/ppermute | solution.py:413
  36.5 7.8 %collective-permute-start.7 = (bf16[4,48,128]{2,1,0:T(8,128)(2,1)S(1)}, bf16[4,48,128]{2,1,0:T(8,128)(2,1)S(1)}, u32[]{:S(2)}, u32[]{:S(2)}) collective-permute-start(bf16[4,48,128]{2,1,0:T(8,128)(2,1)S(1)} %get-tuple-element.31), channel_id=1, source_target_pairs={{4,16},{8,20},{12,24},{16,4},{20,8},{24,12},{5,17},{9,21},{13,25},... | collective-permute-start | bytes 147464 | tf_op jit(solution)/shard_map/ppermute | solution.py:413
  46.9 6.1 %collective-permute-start.9 = (bf16[48,2048]{1,0:T(8,128)(2,1)}, bf16[48,2048]{1,0:T(8,128)(2,1)S(1)}, u32[]{:S(2)}, u32[]{:S(2)}) collective-permute-start(bf16[48,2048]{1,0:T(8,128)(2,1)} %settle.2.refs_0_), channel_id=1, source_target_pairs={{0,2},{1,3},{2,0},{3,1},{4,6},{5,7},{6,4},{7,5},{8,10},{9,11},{10,... | collective-permute-start | bytes 589832 | tf_op jit(solution)/shard_map/ppermute | solution.py:392
  50.4 7.4 %collective-permute-start.16 = (bf16[2,4,48,128]{3,2,1,0:T(8,128)(2,1)}, bf16[2,4,48,128]{3,2,1,0:T(8,128)(2,1)S(1)}, u32[]{:S(2)}, u32[]{:S(2)}) collective-permute-start(bf16[2,4,48,128]{3,2,1,0:T(8,128)(2,1)} %get-tuple-element.38), channel_id=1, source_target_pairs={{16,0},{20,4},{24,8},{28,12},{0,16},{4,20},{8,24},{12,28},{17,1},{... | collective-permute-start | bytes 294920 | tf_op jit(solution)/shard_map/ppermute | solution.py:411
  50.4 11.6 %collective-permute-start.17 = (bf16[2,4,48,128]{3,2,1,0:T(8,128)(2,1)}, bf16[2,4,48,128]{3,2,1,0:T(8,128)(2,1)S(1)}, u32[]{:S(2)}, u32[]{:S(2)}) collective-permute-start(bf16[2,4,48,128]{3,2,1,0:T(8,128)(2,1)} %get-tuple-element.39), channel_id=1, source_target_pairs={{4,0},{8,4},{12,8},{20,16},{24,20},{28,24},{5,1},{9,5},{13,9},{21,... | collective-permute-start | bytes 294920 | tf_op jit(solution)/shard_map/ppermute | solution.py:411
  53.0 18.4 %collective-permute-start.8 = (bf16[48,2048]{1,0:T(8,128)(2,1)}, bf16[48,2048]{1,0:T(8,128)(2,1)S(1)}, u32[]{:S(2)}, u32[]{:S(2)}) collective-permute-start(bf16[48,2048]{1,0:T(8,128)(2,1)} %settle.2.refs_0_), channel_id=1, source_target_pairs={{0,1},{1,0},{2,3},{3,2},{4,5},{5,4},{6,7},{7,6},{8,9},{9,8},{10,11... | collective-permute-start | bytes 589832 | tf_op jit(solution)/shard_map/ppermute | solution.py:392
  53.1 18.4 %collective-permute-start.10 = (bf16[48,2048]{1,0:T(8,128)(2,1)S(1)}, bf16[48,2048]{1,0:T(8,128)(2,1)S(1)}, u32[]{:S(2)}, u32[]{:S(2)}) collective-permute-start(bf16[48,2048]{1,0:T(8,128)(2,1)S(1)} %collective-permute-done.9.refs_2_), channel_id=1, source_target_pairs={{0,1},{1,0},{2,3},{3,2},{4,5},{5,4},{6,7},{7,6},{8,9},{9,8},{10,11... | collective-permute-start | bytes 589832 | tf_op jit(solution)/shard_map/ppermute | solution.py:392
  53.6 10.5 %collective-permute-start.18 = (bf16[2,4,48,128]{3,2,1,0:T(8,128)(2,1)}, bf16[2,4,48,128]{3,2,1,0:T(8,128)(2,1)S(1)}, u32[]{:S(2)}, u32[]{:S(2)}) collective-permute-start(bf16[2,4,48,128]{3,2,1,0:T(8,128)(2,1)} %get-tuple-element.40), channel_id=1, source_target_pairs={{0,4},{4,8},{8,12},{16,20},{20,24},{24,28},{1,5},{5,9},{9,13},{17,... | collective-permute-start | bytes 294920 | tf_op jit(solution)/shard_map/ppermute | solution.py:411
  57.8 9.5 %collective-permute-start.19 = (bf16[2,4,48,128]{3,2,1,0:T(8,128)(2,1)}, bf16[2,4,48,128]{3,2,1,0:T(8,128)(2,1)S(1)}, u32[]{:S(2)}, u32[]{:S(2)}) collective-permute-start(bf16[2,4,48,128]{3,2,1,0:T(8,128)(2,1)} %get-tuple-element.41), channel_id=1, source_target_pairs={{20,0},{24,4},{28,8},{0,20},{4,24},{8,28},{21,1},{25,5},{29,9},{1,... | collective-permute-start | bytes 294920 | tf_op jit(solution)/shard_map/ppermute | solution.py:411
  62.1 9.4 %collective-permute-start.20 = (bf16[2,4,48,128]{3,2,1,0:T(8,128)(2,1)}, bf16[2,4,48,128]{3,2,1,0:T(8,128)(2,1)S(1)}, u32[]{:S(2)}, u32[]{:S(2)}) collective-permute-start(bf16[2,4,48,128]{3,2,1,0:T(8,128)(2,1)} %get-tuple-element.42), channel_id=1, source_target_pairs={{16,4},{20,8},{24,12},{4,16},{8,20},{12,24},{17,5},{21,9},{25,13},... | collective-permute-start | bytes 294920 | tf_op jit(solution)/shard_map/ppermute | solution.py:411
  76.5 6.4 %collective-permute-start.21 = (bf16[1024,128]{1,0:T(8,128)(2,1)S(1)}, bf16[1024,128]{1,0:T(8,128)(2,1)S(1)}, u32[]{:S(2)}, u32[]{:S(2)}) collective-permute-start(bf16[1024,128]{1,0:T(8,128)(2,1)S(1)} %get-tuple-element.44), channel_id=1, source_target_pairs={{0,4},{1,9},{2,6},{3,11},{4,0},{5,13},{6,2},{7,15},{8,12},{9,1},{1... | collective-permute-start | bytes 786440 | tf_op jit(solution)/shard_map/ppermute | solution.py:375
  93.0 9.9 %collective-permute-start.23 = (bf16[256,128]{1,0:T(8,128)(2,1)}, bf16[256,128]{1,0:T(8,128)(2,1)S(1)}, u32[]{:S(2)}, u32[]{:S(2)}) collective-permute-start(bf16[256,128]{1,0:T(8,128)(2,1)} %get-tuple-element.48), channel_id=1, source_target_pairs={{0,16},{1,17},{2,18},{3,19},{4,20},{5,21},{6,22},{7,23},{8,24},{9,... | collective-permute-start | bytes 196616 | tf_op jit(solution)/shard_map/ppermute | solution.py:375
  103.8 9.0 %collective-permute-start.24 = (bf16[256,128]{1,0:T(8,128)(2,1)S(1)}, bf16[256,128]{1,0:T(8,128)(2,1)S(1)}, u32[]{:S(2)}, u32[]{:S(2)}) collective-permute-start(bf16[256,128]{1,0:T(8,128)(2,1)S(1)} %add_convert_fusion), channel_id=1, source_target_pairs={{0,16},{1,17},{2,18},{3,19},{4,20},{5,21},{6,22},{7,23},{8,24},{9,... | collective-permute-start | bytes 196616 | tf_op jit(solution)/shard_map/ppermute | solution.py:375
  118.7 28.9 %collective-permute-start.26 = (bf16[1024,128]{1,0:T(8,128)(2,1)S(1)}, bf16[1024,128]{1,0:T(8,128)(2,1)S(1)}, u32[]{:S(2)}, u32[]{:S(2)}) collective-permute-start(bf16[1024,128]{1,0:T(8,128)(2,1)S(1)} %pad_maximum_fusion.own_ref), channel_id=1, source_target_pairs={{0,4},{1,9},{2,6},{3,11},{4,0},{5,13},{6,2},{7,15},{8,12},{9,1},{1... | collective-permute-start | bytes 786440 | tf_op jit(solution)/shard_map/ppermute | solution.py:375
  125.0 12.1 %collective-permute-start.11 = (bf16[4,48,128]{2,1,0:T(8,128)(2,1)S(1)}, bf16[4,48,128]{2,1,0:T(8,128)(2,1)S(1)}, u32[]{:S(2)}, u32[]{:S(2)}) collective-permute-start(bf16[4,48,128]{2,1,0:T(8,128)(2,1)S(1)} %get-tuple-element.33), channel_id=1, source_target_pairs={{0,16},{4,20},{8,24},{12,28},{16,0},{20,4},{24,8},{28,12},{1,17},{... | collective-permute-start | bytes 147464 | tf_op jit(solution)/shard_map/ppermute | solution.py:413
  125.5 13.6 %collective-permute-start.12 = (bf16[4,48,128]{2,1,0:T(8,128)(2,1)S(1)}, bf16[4,48,128]{2,1,0:T(8,128)(2,1)S(1)}, u32[]{:S(2)}, u32[]{:S(2)}) collective-permute-start(bf16[4,48,128]{2,1,0:T(8,128)(2,1)S(1)} %get-tuple-element.34), channel_id=1, source_target_pairs={{0,4},{4,8},{8,12},{16,20},{20,24},{24,28},{1,5},{5,9},{9,13},{17,... | collective-permute-start | bytes 147464 | tf_op jit(solution)/shard_map/ppermute | solution.py:413
  129.9 9.1 %collective-permute-start.13 = (bf16[4,48,128]{2,1,0:T(8,128)(2,1)S(1)}, bf16[4,48,128]{2,1,0:T(8,128)(2,1)S(1)}, u32[]{:S(2)}, u32[]{:S(2)}) collective-permute-start(bf16[4,48,128]{2,1,0:T(8,128)(2,1)S(1)} %get-tuple-element.35), channel_id=1, source_target_pairs={{4,0},{8,4},{12,8},{20,16},{24,20},{28,24},{5,1},{9,5},{13,9},{21,... | collective-permute-start | bytes 147464 | tf_op jit(solution)/shard_map/ppermute | solution.py:413
  131.8 8.7 %collective-permute-start.14 = (bf16[4,48,128]{2,1,0:T(8,128)(2,1)S(1)}, bf16[4,48,128]{2,1,0:T(8,128)(2,1)S(1)}, u32[]{:S(2)}, u32[]{:S(2)}) collective-permute-start(bf16[4,48,128]{2,1,0:T(8,128)(2,1)S(1)} %get-tuple-element.36), channel_id=1, source_target_pairs={{0,20},{4,24},{8,28},{20,0},{24,4},{28,8},{1,21},{5,25},{9,29},{21... | collective-permute-start | bytes 147464 | tf_op jit(solution)/shard_map/ppermute | solution.py:413
  137.1 7.9 %collective-permute-start.15 = (bf16[4,48,128]{2,1,0:T(8,128)(2,1)S(1)}, bf16[4,48,128]{2,1,0:T(8,128)(2,1)S(1)}, u32[]{:S(2)}, u32[]{:S(2)}) collective-permute-start(bf16[4,48,128]{2,1,0:T(8,128)(2,1)S(1)} %get-tuple-element.37), channel_id=1, source_target_pairs={{4,16},{8,20},{12,24},{16,4},{20,8},{24,12},{5,17},{9,21},{13,25},... | collective-permute-start | bytes 147464 | tf_op jit(solution)/shard_map/ppermute | solution.py:413
  (32 other events, 297.8 us)
Sparse Core Ops, SparseCore 0:
  89.7 89.2 all-reduce.1

commit v2 on v1

v2 whole, which is shorter than its diff:
```python
import functools
import math

import jax
import jax.numpy as jnp
import numpy as np
from jax import lax
from jax.experimental import pallas as pl
from jax.experimental.pallas import tpu as pltpu
from jax.sharding import PartitionSpec as P

TILE_Y = 4
STEP_ROW = (-1, -1, -1, 0, 0, 1, 1, 1)
STEP_COL = (-1, 0, 1, -1, 1, -1, 0, 1)

VMEM = pltpu.VMEM
SMEM = pltpu.SMEM
BF16 = jnp.bfloat16
F32 = jnp.float32


def call(kernel, name, outs, smem_count, args, scratch=(), flops=0, vmem_mib=4):
    moved = sum(a.size * a.dtype.itemsize for a in args)
    moved += sum(o.size * o.dtype.itemsize for o in outs)
    return pl.pallas_call(
        kernel,
        out_shape=list(outs),
        in_specs=[pl.BlockSpec(memory_space=SMEM)] * smem_count
        + [pl.BlockSpec(memory_space=VMEM)] * (len(args) - smem_count),
        out_specs=[pl.BlockSpec(memory_space=VMEM)] * len(outs),
        scratch_shapes=list(scratch),
        name=name,
        cost_estimate=pl.CostEstimate(flops=flops, bytes_accessed=moved, transcendentals=0),
        compiler_params=pltpu.CompilerParams(vmem_limit_bytes=vmem_mib << 20),
    )(*args)


def struct(shape, dtype):
    return jax.ShapeDtypeStruct(shape, dtype)


def ghost_plan(tile_count, block_count, slot_count):
    rows = tile_count // TILE_Y

    def pairs_of(direction, keep=lambda tile: True):
        found = []
        for tile in range(tile_count):
            row = tile // TILE_Y + STEP_ROW[direction]
            col = tile % TILE_Y + STEP_COL[direction]
            if 0 <= row < rows and 0 <= col < TILE_Y and keep(tile):
                found.append((tile, row * TILE_Y + col, direction))
        return found

    groups = [
        pairs_of(4, lambda t: t % 2 == 0) + pairs_of(3, lambda t: t % 2 == 1),
        pairs_of(4, lambda t: t % 2 == 1) + pairs_of(3, lambda t: t % 2 == 0),
    ]
    for direction in (1, 6, 0, 7, 2, 5):
        pairs = pairs_of(direction)
        for group in groups[2:]:
            sources = {p[0] for p in group}
            targets = {p[1] for p in group}
            if all(p[0] not in sources and p[1] not in targets for p in pairs):
                group.extend(pairs)
                break
        else:
            groups.append(pairs)
    groups = [g for g in groups if g]
    trash = block_count + 8 * slot_count + 1
    plan = np.zeros((len(groups), 2, tile_count), np.int32)
    plan[:, 1] = trash
    for index, group in enumerate(groups):
        for source, target, direction in group:
            plan[index, 0, source] = direction
            plan[index, 1, target] = block_count + (7 - direction) * slot_count
    return [[(s, t) for s, t, _ in g] for g in groups], plan


def pack_kernel(lists_ref, plan_ref, pre_ref, feat_ref, *out_refs):
    me = lax.axis_index("tile")
    last = pre_ref.shape[1] // 128 - 1
    for index, out_ref in enumerate(out_refs):
        direction = plan_ref[index, 0, me]
        for slot in range(out_ref.shape[1]):
            block = jnp.minimum(lists_ref[0, direction, slot], last)
            lanes = pl.ds(pl.multiple_of(block * 128, 128), 128)
            out_ref[0, slot] = jnp.maximum(pre_ref[:, lanes], 0)
            out_ref[1, slot] = feat_ref[:, lanes]


def pack(lists, plan, pre_act, features):
    shape = struct((2, lists.shape[2], features.shape[0], 128), BF16)
    return call(
        pack_kernel, "pack_sends", [shape] * plan.shape[0], 2, (lists, plan, pre_act, features)
    )


def gather_full(parts, full):
    me = lax.axis_index("chan")
    width = parts[0].shape[0]
    for step, part in enumerate(parts):
        place = pl.multiple_of((me ^ step) * width, 16)
        full[pl.ds(place, width), :] = part[...]


def partial_kernel(group_count, ride_count, pin_ref, plan_ref, *refs):
    parts, refs = refs[:4], refs[4:]
    weight_ref, refs = refs[0], refs[1:]
    ride_refs, refs = refs[:ride_count], refs[ride_count:]
    local_ref = refs[0]
    back_refs = refs[1 : 1 + group_count]
    full, product, total = refs[1 + group_count :]
    me = lax.axis_index("tile")
    offset_count, block_count = pin_ref.shape[1:]
    width = local_ref.shape[1]
    gather_full(parts, full)
    total[...] = jnp.zeros_like(total)

    def two_blocks(turn, _):
        lanes = pl.ds(pl.multiple_of(turn * 256, 256), 256)
        product[...] = jnp.dot(weight_ref[...], full[:, lanes], preferred_element_type=F32)
        for offset in range(offset_count):
            for half in range(2):
                entry = pin_ref[0, offset, turn * 2 + half]
                total[entry] += product[
                    offset * width : (offset + 1) * width, half * 128 : (half + 1) * 128
                ]
        return 0

    lax.fori_loop(0, block_count // 2, two_blocks, 0)
    local_ref[...] = total[:block_count]
    for index, back_ref in enumerate(back_refs):
        base = plan_ref[index, 1, me]
        for slot in range(back_ref.shape[1]):
            back_ref[0, slot] = total[base + slot].astype(BF16)
    for ride_ref, back_ref in zip(ride_refs, back_refs):
        back_ref[1:] = ride_ref[...]


def partial_sums(pin, plan, parts, weight, slot_count, rides=()):
    width, voxels = parts[0].shape
    offset_count, block_count = pin.shape[1:]
    group_count = plan.shape[0]
    entries = block_count + 9 * slot_count + 1
    back = (slot_count, width, 128)
    outs = [struct((block_count, width, 128), F32)]
    outs += [struct((3,) + back, BF16) for _ in rides]
    outs += [struct((1,) + back, BF16)] * (group_count - len(rides))
    flat = weight.reshape(offset_count * width, 4 * width)
    result = call(
        functools.partial(partial_kernel, group_count, len(rides)),
        "partial_sums",
        outs,
        2,
        (pin, plan, *parts, flat, *rides),
        [
            VMEM((4 * width, voxels), BF16),
            VMEM((offset_count * width, 256), F32),
            VMEM((entries, width, 128), F32),
        ],
        flops=2 * weight.size * voxels,
        vmem_mib=12,
    )
    return result[0], result[1:]


def packed_rows(rows, tile_count):
    step = 16 * tile_count
    return -(-(rows + rows // 2) // step) * step


def weight_kernel(group_count, which, factor, joined, pin_ref, plan_ref, *refs):
    parts, refs = refs[:4], refs[4:]
    own_ref, refs = refs[0], refs[1:]
    ghost_refs, refs = refs[:group_count], refs[group_count:]
    other_refs, refs = refs[: 2 * joined], refs[2 * joined :]
    keep_ref, send_ref, full, extended, gathered, wide, tall = refs
    me = lax.axis_index("tile")
    offset_count, block_count = pin_ref.shape[1:]
    width = own_ref.shape[0]
    gather_full(parts, full)
    for block in range(block_count):
        value = own_ref[:, block * 128 : (block + 1) * 128]
        extended[block] = jnp.maximum(value, 0) if which == 0 else value
    for index, ghost_ref in enumerate(ghost_refs):
        base = plan_ref[index, 1, me]
        lead = ghost_ref.shape[0] - 2 + which
        for slot in range(ghost_ref.shape[1]):
            extended[base + slot] = ghost_ref[lead, slot]
    empty = block_count + 8 * ghost_refs[0].shape[1]
    extended[empty] = jnp.zeros_like(extended[empty])
    chunk = gathered.shape[0] // width

    def some_offsets(turn, _):
        for step in range(chunk):
            for block in range(block_count):
                entry = pin_ref[0, turn * chunk + step, block]
                gathered[step * width : (step + 1) * width, block * 128 : (block + 1) * 128] = (
                    extended[entry]
                )
        grads = lax.dot_general(
            gathered[...], full[...], (((1,), (1,)), ((), ())), preferred_element_type=F32
        )
        rows = chunk * width
        here = pl.ds(pl.multiple_of(turn * rows, 16), rows)
        wide[here, : grads.shape[1]] = grads * factor
        return 0

    lax.fori_loop(0, offset_count // chunk, some_offsets, 0)
    rows, half = wide.shape[0], wide.shape[0] // 2
    tall[:rows] = wide[:, :128]
    tall[rows : rows + half, :64] = wide[:half, 128:192]
    tall[rows : rows + half, 64:] = wide[half:, 128:192]
    if tall.shape[0] > rows + half:
        tall[rows + half :] = jnp.zeros((tall.shape[0] - rows - half, 128), F32)
    bit = exchange_bit(0)
    split = tall.shape[0] // 2
    if joined:
        keep_ref[:1] = other_refs[0][...]
        send_ref[:1] = other_refs[1][...]
    keep_ref[joined] = tall[pl.ds(pl.multiple_of(bit * split, 16), split), :]
    send_ref[joined] = tall[pl.ds(pl.multiple_of((1 - bit) * split, 16), split), :].astype(BF16)


def weight_sums(pin, plan, parts, own, ghosts, which, factor, tile_count, others=()):
    width, voxels = own.shape
    offset_count, block_count = pin.shape[1:]
    slot_count = ghosts[0].shape[1]
    entries = block_count + 9 * slot_count + 1
    chunk = 9 if offset_count % 9 == 0 else 1
    rows = offset_count * width
    tall = packed_rows(rows, tile_count)
    joined = 1 if others else 0
    shape = (1 + joined, tall // 2, 128)
    return call(
        functools.partial(weight_kernel, len(ghosts), which, factor, joined),
        "weight_sums",
        [struct(shape, F32), struct(shape, BF16)],
        2,
        (pin, plan, *parts, own, *ghosts, *others),
        [
            VMEM((4 * width, voxels), BF16),
            VMEM((entries, width, 128), BF16),
            VMEM((chunk * width, voxels), BF16),
            VMEM((rows, 256), F32),
            VMEM((tall, 128), F32),
        ],
        flops=2 * rows * 4 * width * voxels,
        vmem_mib=16,
    )


def settle_kernel(first, lists_ref, plan_ref, local_ref, other_ref, *refs):
    *back_refs, out_ref, total = refs
    me = lax.axis_index("tile")
    block_count = local_ref.shape[0]
    total[:block_count] = local_ref[...]
    for index, back_ref in enumerate(back_refs):
        direction = plan_ref[index, 0, me]
        for slot in range(back_ref.shape[1]):
            block = lists_ref[0, direction, slot]
            total[block] += back_ref[0, slot].astype(F32)
    for block in range(block_count):
        lanes = slice(block * 128, (block + 1) * 128)
        other = other_ref[:, lanes].astype(F32)
        if first:
            value = jnp.where(other > 0, total[block], 0.0)
        else:
            value = other + total[block]
        out_ref[:, lanes] = value.astype(BF16)


def settle(first, lists, plan, local, other, backs):
    block_count, width, _ = local.shape
    return call(
        functools.partial(settle_kernel, first),
        "settle",
        [struct(other.shape, BF16)],
        2,
        (lists, plan, local, other, *backs),
        [VMEM((block_count + 1, width, 128), F32)],
        flops=local.size,
    )[0]


def exchange_dim(step):
    parity = lax.axis_index("chan") % 2
    if step < 2:
        return jnp.where(parity == 0, step, 1 - step)
    return step


def exchange_bit(step):
    return lax.shift_right_logical(lax.axis_index("tile"), exchange_dim(step)) & 1


def trade(value, step):
    tile_count = lax.axis_size("tile")
    chan_count = lax.axis_size("chan")
    pairs = []
    for tile in range(tile_count):
        for chan in range(chan_count):
            dim = (1 - step if chan % 2 else step) if step < 2 else step
            pairs.append((tile * chan_count + chan, (tile ^ (1 << dim)) * chan_count + chan))
    return lax.ppermute(value, ("tile", "chan"), pairs)


def halve_kernel(step, keep_ref, got_ref, next_ref, send_ref):
    bit = exchange_bit(step)
    split = next_ref.shape[1]
    mine = pl.ds(pl.multiple_of(bit * split, 16), split)
    theirs = pl.ds(pl.multiple_of((1 - bit) * split, 16), split)
    for index in range(keep_ref.shape[0]):
        next_ref[index] = keep_ref[index, mine, :] + got_ref[index, mine, :].astype(F32)
        send_ref[index] = (
            keep_ref[index, theirs, :] + got_ref[index, theirs, :].astype(F32)
        ).astype(BF16)


def halve(step, keep, got):
    shape = (keep.shape[0], keep.shape[1] // 2, 128)
    return call(
        functools.partial(halve_kernel, step),
        "halve",
        [struct(shape, F32), struct(shape, BF16)],
        0,
        (keep, got),
        flops=keep.size,
    )


def unpack_kernel(tile_count, own_ref, got_ref, *refs):
    *out_refs, tall = refs
    steps = tile_count.bit_length() - 1
    chunk = own_ref.shape[2]
    mine = 0
    for step in range(steps):
        mine = mine * 2 + exchange_bit(step)
    half_count = tile_count // 2
    for part, out_ref in enumerate(out_refs):
        for index in range(tile_count):
            source = own_ref if index < half_count else got_ref
            rows = pl.ds(pl.multiple_of((mine ^ index) * chunk, 16), chunk)
            tall[rows, :] = source[index % half_count, part].astype(F32)
        rows = out_ref.shape[0]
        half = rows // 2
        out_ref[:, :128] = tall[:rows]
        out_ref[:half, 128:192] = tall[rows : rows + half, :64]
        out_ref[half:, 128:192] = tall[rows : rows + half, 64:]


def unpack(own, got, rows, columns):
    tile_count = 2 * own.shape[0]
    return call(
        functools.partial(unpack_kernel, tile_count),
        "unpack_sums",
        [struct((rows, columns), F32)] * own.shape[1],
        0,
        (own, got),
        [VMEM((tile_count * own.shape[2], 128), F32)],
        vmem_mib=8,
    )


def swap_part(value, bits):
    return lax.ppermute(value, "chan", [(i, i ^ bits) for i in range(4)])


def shards(features, pre_act, cotangent, weight_one, weight_two, send_list, pair_in, pair_out):
    tile_count = lax.axis_size("tile")
    width, voxels = features.shape
    offset_count, _, columns = weight_one.shape
    block_count = pair_out.shape[2]
    slot_count = send_list.shape[2]
    rows = offset_count * width
    steps = tile_count.bit_length() - 1
    pair_lists, plan = ghost_plan(tile_count, block_count, slot_count)
    plan = jnp.asarray(plan)
    factor = 1.0 / math.sqrt(tile_count * voxels)
    tie = lambda *values: lax.optimization_barrier(values)

    def give(values, lists):
        return [lax.ppermute(v, "tile", p) for v, p in zip(values, lists)]

    back_lists = [[(t, s) for s, t in p] for p in pair_lists]

    sends = pack(send_list, plan, pre_act, features)
    far, near = swap_part(cotangent, 2), swap_part(cotangent, 1)
    far, near, sends = tie(far, near, sends)
    cot_parts = (cotangent, near, far, swap_part(far, 1))
    ghosts = give(sends[2:], pair_lists[2:])

    local_two, backs = partial_sums(pair_in, plan, cot_parts, weight_two, slot_count, sends[:2])
    backs = give(backs, back_lists)
    backs, ghosts = tie(backs, ghosts)
    ghosts = list(backs[:2]) + list(ghosts)
    grad_pre = settle(True, send_list, plan, local_two, pre_act, backs)

    far, near = swap_part(grad_pre, 2), swap_part(grad_pre, 1)
    split_two = weight_sums(
        pair_in, plan, cot_parts, pre_act, ghosts, 0, factor, tile_count
    )
    far, near, split_two = tie(far, near, split_two)
    pre_parts = (grad_pre, near, far, swap_part(far, 1))
    keep, send = weight_sums(
        pair_in, plan, pre_parts, features, ghosts, 1, factor, tile_count, split_two
    )
    got = trade(send, 0)
    pre_parts, keep = tie(pre_parts, keep)
    local_one, backs = partial_sums(pair_in, plan, pre_parts, weight_one, slot_count)
    got, backs = tie(got, backs)
    order = list(range(2, len(backs))) + [0, 1]
    waits = 2 * steps - 2
    returned = [None] * len(backs)

    def beside(value, wait):
        share = order[wait * len(order) // waits : (wait + 1) * len(order) // waits]
        if not share:
            return value
        value, mine = tie(value, give([backs[g] for g in share], [back_lists[g] for g in share]))
        for group, back in zip(share, mine):
            returned[group] = back
        return value

    for step in range(1, steps):
        keep, send = halve(step, keep, got)
        got = beside(trade(send, step), step - 1)
    chunk = (keep + got.astype(F32)).astype(BF16)[None]
    for step in reversed(range(1, steps)):
        got = beside(trade(chunk, step), 2 * steps - 2 - step)
        chunk = jnp.concatenate([chunk, got], axis=0)
    got = trade(chunk, 0)
    grad_features = settle(False, send_list, plan, local_one, cotangent, returned)
    sum_two, sum_one = unpack(chunk, got, rows, columns)
    shape = (offset_count, width, columns)
    return grad_features, sum_one.reshape(shape), sum_two.reshape(shape)


def solution(mesh):
    return jax.shard_map(
        shards,
        mesh=mesh,
        in_specs=(
            P("chan", "tile"),
            P("chan", "tile"),
            P("chan", "tile"),
            P(None, "chan", None),
            P(None, "chan", None),
            P("tile", None, None),
            P("tile", None, None),
            P("tile", None, None),
        ),
        out_specs=(P("chan", "tile"), P(None, "chan", None), P(None, "chan", None)),
        check_vma=False,
    )
```

time: 191 us -> 114 us (0.60)
  waiting for transfers between devices: 84.3 us -> 41.5 us
  between operations: 14.4 us -> 0.92 us
  Pallas kernels: 29 us -> 21.8 us
  local copies, waits for them, and re-layouts: 13.1 us -> 6.8 us
  starting transfers between devices: 46.6 us -> 41.4 us
    psum x1 -> x0, waiting for transfers between devices: 28.4 us -> none  [shards(): grad_two = lax.psum(sum_two, 'tile')]
    ppermute x27 -> x25, waiting for transfers between devices: 55.9 us -> 41.5 us  [the longest x13 22 us: give(): return [lax.ppermute(v, 'tile', p) for v, p in zip(values, lists)]]
    pallas_call x10, Pallas kernels: 29 us -> 21.8 us  [call(): pl.pallas_call(kernel, out_shape=list(outs), in_specs=[pl.BlockSpec(memor...]
    unnamed x59 -> x24, local copies, waits for them, and re-layouts: 13.1 us -> 6.8 us
    ppermute x27 -> x25, starting transfers between devices: 46.5 us -> 41.4 us  [the longest x13 35.6 us: give(): return [lax.ppermute(v, 'tile', p) for v, p in zip(values, lists)]]
  transfers between devices with their start and end apart: 28 -> 25, of which waited for: 14 -> 12; matrix products, arithmetic and copies ran while one was open for 1% -> 1% of each run, Pallas kernels for 9% -> 14%
where the time goes in v2:
time: 114 us; the launch traced here: 112 us
  waiting for transfers between devices  41.5 us (36%)
  starting transfers between devices  41.4 us (36%)
  Pallas kernels  21.8 us (19%)
  local copies, waits for them, and re-layouts  6.8 us (6%)
    ppermute x13, starting transfers between devices, give(): return [lax.ppermute(v, 'tile', p) for v, p in zip(values, lists)]  35.6 us
    ppermute x13, waiting for transfers between devices, give(): return [lax.ppermute(v, 'tile', p) for v, p in zip(values, lists)]  22 us
    pallas_call x10, Pallas kernels, call(): pl.pallas_call(kernel, out_shape=list(outs), in_specs=[pl.BlockSpec(memor...  21.8 us
    ppermute x6, waiting for transfers between devices, trade(): return lax.ppermute(value, ('tile', 'chan'), pairs)  13.8 us
    unnamed x24, local copies, waits for them, and re-layouts  6.8 us
    ppermute x6, waiting for transfers between devices, swap_part(): return lax.ppermute(value, 'chan', [(i, i ^ bits) for i in range(4)])  5.69 us
    ppermute x6, starting transfers between devices, swap_part(): return lax.ppermute(value, 'chan', [(i, i ^ bits) for i in range(4)])  3.32 us
    ppermute x6, starting transfers between devices, trade(): return lax.ppermute(value, ('tile', 'chan'), pairs)  2.5 us
  transfers between devices with their start and end apart: 25, of which 12 were waited for; matrix products, arithmetic and copies ran while one was open for 1% of the time, Pallas kernels for 14%

profile of v2, /device:TPU:2, one launch (start us, length us, event | category | flops | bytes accessed | tf_op | source)
XLA Modules:
  0.0 112.5 jit_solution(827159238909068049)
XLA Ops:
  9.0 2.6 %collective-permute-start.8 = (bf16[2,4,48,128]{3,2,1,0:T(8,128)(2,1)S(1)}, bf16[2,4,48,128]{3,2,1,0:T(8,128)(2,1)S(1)}, u32[]{:S(2)}, u32[]{:S(2)}) collective-permute-start(bf16[2,4,48,128]{3,2,1,0:T(8,128)(2,1)S(1)} %get-tuple-element.84), channel_id=1, source_target_pairs={{16,0},{20,4},{24,8},{28,12},{0,16},{4,20},{8,24},{12,28},{17,1},{... | collective-permute-start | bytes 294920 | tf_op jit(solution)/shard_map/ppermute | solution.py:383
  11.6 3.2 %collective-permute-start.9 = (bf16[2,4,48,128]{3,2,1,0:T(8,128)(2,1)S(1)}, bf16[2,4,48,128]{3,2,1,0:T(8,128)(2,1)S(1)}, u32[]{:S(2)}, u32[]{:S(2)}) collective-permute-start(bf16[2,4,48,128]{3,2,1,0:T(8,128)(2,1)S(1)} %get-tuple-element.85), channel_id=1, source_target_pairs={{20,0},{24,4},{28,8},{0,20},{4,24},{8,28},{21,1},{25,5},{29,9},{1,... | collective-permute-start | bytes 294920 | tf_op jit(solution)/shard_map/ppermute | solution.py:383
  14.8 1.9 %collective-permute-start.10 = (bf16[2,4,48,128]{3,2,1,0:T(8,128)(2,1)S(1)}, bf16[2,4,48,128]{3,2,1,0:T(8,128)(2,1)S(1)}, u32[]{:S(2)}, u32[]{:S(2)}) collective-permute-start(bf16[2,4,48,128]{3,2,1,0:T(8,128)(2,1)S(1)} %get-tuple-element.86), channel_id=1, source_target_pairs={{16,4},{20,8},{24,12},{4,16},{8,20},{12,24},{17,5},{21,9},{25,13},... | collective-permute-start | bytes 294920 | tf_op jit(solution)/shard_map/ppermute | solution.py:383
  19.5 5.1 %partial_sums.2 = (f32[16,48,128]{2,1,0:T(8,128)S(1)}, bf16[3,4,48,128]{3,2,1,0:T(8,128)(2,1)S(1)}, bf16[3,4,48,128]{3,2,1,0:T(8,128)(2,1)S(1)}, bf16[1,4,48,128...) custom-call(s32[1,27,16]{2,1,0:T(8,128)S(1)} %copy.16.pin_ref, ...), custom_call_target="tpu_custom_call" | custom-call | flops 1019215872 | bytes 2318336 | tf_op jit(solution)/shard_map/partial_sums/pallas_call | solution.py:25
  24.7 7.2 %collective-permute-start.4 = (bf16[3,4,48,128]{3,2,1,0:T(8,128)(2,1)S(1)}, bf16[3,4,48,128]{3,2,1,0:T(8,128)(2,1)S(1)}, u32[]{:S(2)}, u32[]{:S(2)}) collective-permute-start(bf16[3,4,48,128]{3,2,1,0:T(8,128)(2,1)S(1)} %get-tuple-element.80), channel_id=1, source_target_pairs={{8,4},{24,20},{4,8},{20,24},{9,5},{25,21},{5,9},{21,25},{10,6},{26... | collective-permute-start | bytes 442376 | tf_op jit(solution)/shard_map/ppermute | solution.py:383
  32.0 4.2 %collective-permute-start.6 = (bf16[1,4,48,128]{3,2,1,0:T(8,128)(2,1)S(1)}, bf16[1,4,48,128]{3,2,1,0:T(8,128)(2,1)S(1)}, u32[]{:S(2)}, u32[]{:S(2)}) collective-permute-start(bf16[1,4,48,128]{3,2,1,0:T(8,128)(2,1)S(1)} %get-tuple-element.82), channel_id=1, source_target_pairs={{0,20},{4,24},{8,28},{20,0},{24,4},{28,8},{1,21},{5,25},{9,29},{21... | collective-permute-start | bytes 147464 | tf_op jit(solution)/shard_map/ppermute | solution.py:383
  36.3 1.9 %collective-permute-start.7 = (bf16[1,4,48,128]{3,2,1,0:T(8,128)(2,1)S(1)}, bf16[1,4,48,128]{3,2,1,0:T(8,128)(2,1)S(1)}, u32[]{:S(2)}, u32[]{:S(2)}) collective-permute-start(bf16[1,4,48,128]{3,2,1,0:T(8,128)(2,1)S(1)} %get-tuple-element.83), channel_id=1, source_target_pairs={{4,16},{8,20},{12,24},{16,4},{20,8},{24,12},{5,17},{9,21},{13,25},... | collective-permute-start | bytes 147464 | tf_op jit(solution)/shard_map/ppermute | solution.py:383
  38.2 2.9 %collective-permute-done.6.refs_3_ = bf16[1,4,48,128]{3,2,1,0:T(8,128)(2,1)S(1)} collective-permute-done((bf16[1,4,48,128]{3,2,1,0:T(8,128)(2,1)S(1)}, bf16[1,4,48,128]{3,2,1,0:T(8,128)(2,1)S(1)}, u32[]{:S(2)}, u32[]{:S(2)}) %collective-permute-start.6) | collective-permute-done | bytes 49184 | tf_op jit(solution)/shard_map/ppermute | solution.py:383
  41.2 2.9 %collective-permute-done.7.refs_4_ = bf16[1,4,48,128]{3,2,1,0:T(8,128)(2,1)S(1)} collective-permute-done((bf16[1,4,48,128]{3,2,1,0:T(8,128)(2,1)S(1)}, bf16[1,4,48,128]{3,2,1,0:T(8,128)(2,1)S(1)}, u32[]{:S(2)}, u32[]{:S(2)}) %collective-permute-start.7) | collective-permute-done | bytes 49184 | tf_op jit(solution)/shard_map/ppermute | solution.py:383
  46.7 3.3 %weight_sums.2 = (f32[1,1024,128]{2,1,0:T(8,128)S(1)}, bf16[1,1024,128]{2,1,0:T(8,128)(2,1)S(1)}) custom-call(s32[1,27,16]{2,1,0:T(8,128)S(1)} %copy.16.pin_ref, s32[5,2,8]{2,1,0:T(2,128)S(1)} %copy-done.8, bf16[48,2048]{1,0:T(8,128)(2,1)S(1)} %copy-done.3, bf16[48,2048]{1,0:T(8,128)(2,1)S(1)} %collective-permute-done.1.refs_1_, ...), custom_call_target="tpu_custom_call" | custom-call | flops 1019215872 | bytes 2361344 | tf_op jit(solution)/shard_map/weight_sums/pallas_call | solution.py:25
  49.9 2.4 %collective-permute-done.11.refs_2_ = bf16[48,2048]{1,0:T(8,128)(2,1)S(1)} collective-permute-done((bf16[48,2048]{1,0:T(8,128)(2,1)S(1)}, bf16[48,2048]{1,0:T(8,128)(2,1)S(1)}, u32[]{:S(2)}, u32[]{:S(2)}) %collective-permute-start.11) | collective-permute-done | bytes 196640 | tf_op jit(solution)/shard_map/ppermute | solution.py:366
  53.8 3.3 %weight_sums.3 = (f32[2,1024,128]{2,1,0:T(8,128)S(1)}, bf16[2,1024,128]{2,1,0:T(8,128)(2,1)S(1)}) custom-call(s32[1,27,16]{2,1,0:T(8,128)S(1)} %copy.16.pin_ref, s32[5,2,8]{2,1,0:T(2,128)S(1)} %copy-done.8, bf16[48,2048]{1,0:T(8,128)(2,1)S(1)} %settle.2.refs_0_, bf16[48,2048]{1,0:T(8,128)(2,1)S(1)} %collective-permute-done.12.refs_1_, ...), custom_call_target="tpu_custom_call" | custom-call | flops 1019215872 | bytes 3934208 | tf_op jit(solution)/shard_map/weight_sums/pallas_call | solution.py:25
  57.3 4.9 %partial_sums.3 = (f32[16,48,128]{2,1,0:T(8,128)S(1)}, bf16[1,4,48,128]{3,2,1,0:T(8,128)(2,1)S(1)}, bf16[1,4,48,128]{3,2,1,0:T(8,128)(2,1)S(1)}, bf16[1,4,48,128...) custom-call(s32[1,27,16]{2,1,0:T(8,128)S(1)} %copy.16.pin_ref, ...), custom_call_target="tpu_custom_call" | custom-call | flops 1019215872 | bytes 1925120 | tf_op jit(solution)/shard_map/partial_sums/pallas_call | solution.py:25
  62.2 4.2 %collective-permute-done.14.got_ref = bf16[2,1024,128]{2,1,0:T(8,128)(2,1)S(1)} collective-permute-done((bf16[2,1024,128]{2,1,0:T(8,128)(2,1)S(1)}, bf16[2,1024,128]{2,1,0:T(8,128)(2,1)S(1)}, u32[]{:S(2)}, u32[]{:S(2)}) %collective-permute-start.14) | collective-permute-done | bytes 524320 | tf_op jit(solution)/shard_map/ppermute | solution.py:305
  68.1 3.6 %collective-permute-done.16.refs_2_ = bf16[1,4,48,128]{3,2,1,0:T(8,128)(2,1)S(1)} collective-permute-done((bf16[1,4,48,128]{3,2,1,0:T(8,128)(2,1)S(1)}, bf16[1,4,48,128]{3,2,1,0:T(8,128)(2,1)S(1)}, u32[]{:S(2)}, u32[]{:S(2)}) %collective-permute-start.16) | collective-permute-done | bytes 49184 | tf_op jit(solution)/shard_map/ppermute | solution.py:383
  71.8 1.9 %collective-permute-done.15.got_ref = bf16[2,512,128]{2,1,0:T(8,128)(2,1)S(1)} collective-permute-done((bf16[2,512,128]{2,1,0:T(8,128)(2,1)S(1)}, bf16[2,512,128]{2,1,0:T(8,128)(2,1)S(1)}, u32[]{:S(2)}, u32[]{:S(2)}) %collective-permute-start.15) | collective-permute-done | bytes 262176 | tf_op jit(solution)/shard_map/ppermute | solution.py:305
  74.6 4.2 %collective-permute-start.18 = (bf16[1,4,48,128]{3,2,1,0:T(8,128)(2,1)S(1)}, bf16[1,4,48,128]{3,2,1,0:T(8,128)(2,1)S(1)}, u32[]{:S(2)}, u32[]{:S(2)}) collective-permute-start(bf16[1,4,48,128]{3,2,1,0:T(8,128)(2,1)S(1)} %get-tuple-element.121), channel_id=1, source_target_pairs={{0,20},{4,24},{8,28},{20,0},{24,4},{28,8},{1,21},{5,25},{9,29},{21... | collective-permute-start | bytes 147464 | tf_op jit(solution)/shard_map/ppermute | solution.py:383
  78.8 4.4 %collective-permute-done.18.refs_3_ = bf16[1,4,48,128]{3,2,1,0:T(8,128)(2,1)S(1)} collective-permute-done((bf16[1,4,48,128]{3,2,1,0:T(8,128)(2,1)S(1)}, bf16[1,4,48,128]{3,2,1,0:T(8,128)(2,1)S(1)}, u32[]{:S(2)}, u32[]{:S(2)}) %collective-permute-start.18) | collective-permute-done | bytes 49184 | tf_op jit(solution)/shard_map/ppermute | solution.py:383
  84.6 3.2 %collective-permute-start.20 = (bf16[1,4,48,128]{3,2,1,0:T(8,128)(2,1)S(1)}, bf16[1,4,48,128]{3,2,1,0:T(8,128)(2,1)S(1)}, u32[]{:S(2)}, u32[]{:S(2)}) collective-permute-start(bf16[1,4,48,128]{3,2,1,0:T(8,128)(2,1)S(1)} %get-tuple-element.123), channel_id=1, source_target_pairs={{4,16},{8,20},{12,24},{16,4},{20,8},{24,12},{5,17},{9,21},{13,25},... | collective-permute-start | bytes 147464 | tf_op jit(solution)/shard_map/ppermute | solution.py:383
  87.8 5.0 %collective-permute-done.20.refs_4_ = bf16[1,4,48,128]{3,2,1,0:T(8,128)(2,1)S(1)} collective-permute-done((bf16[1,4,48,128]{3,2,1,0:T(8,128)(2,1)S(1)}, bf16[1,4,48,128]{3,2,1,0:T(8,128)(2,1)S(1)}, u32[]{:S(2)}, u32[]{:S(2)}) %collective-permute-start.20) | collective-permute-done | bytes 49184 | tf_op jit(solution)/shard_map/ppermute | solution.py:383
  93.9 4.3 %collective-permute-start.23 = (bf16[1,4,48,128]{3,2,1,0:T(8,128)(2,1)S(1)}, bf16[1,4,48,128]{3,2,1,0:T(8,128)(2,1)S(1)}, u32[]{:S(2)}, u32[]{:S(2)}) collective-permute-start(bf16[1,4,48,128]{3,2,1,0:T(8,128)(2,1)S(1)} %get-tuple-element.126), channel_id=1, source_target_pairs={{8,4},{24,20},{4,8},{20,24},{9,5},{25,21},{5,9},{21,25},{10,6},{26... | collective-permute-start | bytes 147464 | tf_op jit(solution)/shard_map/ppermute | solution.py:383
  98.3 3.1 %collective-permute-done.23.refs_1_ = bf16[1,4,48,128]{3,2,1,0:T(8,128)(2,1)S(1)} collective-permute-done((bf16[1,4,48,128]{3,2,1,0:T(8,128)(2,1)S(1)}, bf16[1,4,48,128]{3,2,1,0:T(8,128)(2,1)S(1)}, u32[]{:S(2)}, u32[]{:S(2)}) %collective-permute-start.23) | collective-permute-done | bytes 49184 | tf_op jit(solution)/shard_map/ppermute | solution.py:383
  103.1 7.6 %collective-permute-done.24.got_ref = bf16[4,2,256,128]{3,2,1,0:T(8,128)(2,1)S(1)} collective-permute-done((bf16[4,2,256,128]{3,2,1,0:T(8,128)(2,1)S(1)}, bf16[4,2,256,128]{3,2,1,0:T(8,128)(2,1)S(1)}, u32[]{:S(2)}, u32[]{:S(2)}) %collective-permute-start.24) | collective-permute-done | bytes 524320 | tf_op jit(solution)/shard_map/ppermute | solution.py:305
  110.7 1.8 %unpack_sums.1 = (f32[1296,192]{1,0:T(8,128)}, f32[1296,192]{1,0:T(8,128)}) custom-call(bf16[4,2,256,128]{3,2,1,0:T(8,128)(2,1)S(1)} %pad_maximum_fusion.own_ref, bf16[4,2,256,128]{3,2,1,0:T(8,128)(2,1)S(1)} %collective-permute-done.24.got_ref), custom_call_target="tpu_custom_call" | custom-call | bytes 3039232 | tf_op jit(solution)/shard_map/unpack_sums/pallas_call | solution.py:25
  (63 shorter events, 22.1 us)
Async XLA Ops:
  0.6 5.8 %collective-permute-start.1 = (bf16[48,2048]{1,0:T(8,128)(2,1)}, bf16[48,2048]{1,0:T(8,128)(2,1)S(1)}, u32[]{:S(2)}, u32[]{:S(2)}) collective-permute-start(bf16[48,2048]{1,0:T(8,128)(2,1)} %other_ref.3), channel_id=1, source_target_pairs={{0,1},{1,0},{2,3},{3,2},{4,5},{5,4},{6,7},{7,6},{8,9},{9,8},{10,11... | collective-permute-start | bytes 589832 | tf_op jit(solution)/shard_map/ppermute | solution.py:366
  0.7 7.5 %collective-permute-start = (bf16[48,2048]{1,0:T(8,128)(2,1)}, bf16[48,2048]{1,0:T(8,128)(2,1)S(1)}, u32[]{:S(2)}, u32[]{:S(2)}) collective-permute-start(bf16[48,2048]{1,0:T(8,128)(2,1)} %other_ref.3), channel_id=1, source_target_pairs={{0,2},{1,3},{2,0},{3,1},{4,6},{5,7},{6,4},{7,5},{8,10},{9,11},{10,... | collective-permute-start | bytes 589832 | tf_op jit(solution)/shard_map/ppermute | solution.py:366
  8.2 8.5 %collective-permute-start.2 = (bf16[48,2048]{1,0:T(8,128)(2,1)S(1)}, bf16[48,2048]{1,0:T(8,128)(2,1)S(1)}, u32[]{:S(2)}, u32[]{:S(2)}) collective-permute-start(bf16[48,2048]{1,0:T(8,128)(2,1)S(1)} %collective-permute-done.refs_2_), channel_id=1, source_target_pairs={{0,1},{1,0},{2,3},{3,2},{4,5},{5,4},{6,7},{7,6},{8,9},{9,8},{10,11... | collective-permute-start | bytes 589832 | tf_op jit(solution)/shard_map/ppermute | solution.py:366
  9.0 22.9 %collective-permute-start.8 = (bf16[2,4,48,128]{3,2,1,0:T(8,128)(2,1)S(1)}, bf16[2,4,48,128]{3,2,1,0:T(8,128)(2,1)S(1)}, u32[]{:S(2)}, u32[]{:S(2)}) collective-permute-start(bf16[2,4,48,128]{3,2,1,0:T(8,128)(2,1)S(1)} %get-tuple-element.84), channel_id=1, source_target_pairs={{16,0},{20,4},{24,8},{28,12},{0,16},{4,20},{8,24},{12,28},{17,1},{... | collective-permute-start | bytes 294920 | tf_op jit(solution)/shard_map/ppermute | solution.py:383
  11.6 20.4 %collective-permute-start.9 = (bf16[2,4,48,128]{3,2,1,0:T(8,128)(2,1)S(1)}, bf16[2,4,48,128]{3,2,1,0:T(8,128)(2,1)S(1)}, u32[]{:S(2)}, u32[]{:S(2)}) collective-permute-start(bf16[2,4,48,128]{3,2,1,0:T(8,128)(2,1)S(1)} %get-tuple-element.85), channel_id=1, source_target_pairs={{20,0},{24,4},{28,8},{0,20},{4,24},{8,28},{21,1},{25,5},{29,9},{1,... | collective-permute-start | bytes 294920 | tf_op jit(solution)/shard_map/ppermute | solution.py:383
  14.8 21.5 %collective-permute-start.10 = (bf16[2,4,48,128]{3,2,1,0:T(8,128)(2,1)S(1)}, bf16[2,4,48,128]{3,2,1,0:T(8,128)(2,1)S(1)}, u32[]{:S(2)}, u32[]{:S(2)}) collective-permute-start(bf16[2,4,48,128]{3,2,1,0:T(8,128)(2,1)S(1)} %get-tuple-element.86), channel_id=1, source_target_pairs={{16,4},{20,8},{24,12},{4,16},{8,20},{12,24},{17,5},{21,9},{25,13},... | collective-permute-start | bytes 294920 | tf_op jit(solution)/shard_map/ppermute | solution.py:383
  24.6 19.5 %collective-permute-start.3 = (bf16[3,4,48,128]{3,2,1,0:T(8,128)(2,1)S(1)}, bf16[3,4,48,128]{3,2,1,0:T(8,128)(2,1)S(1)}, u32[]{:S(2)}, u32[]{:S(2)}) collective-permute-start(bf16[3,4,48,128]{3,2,1,0:T(8,128)(2,1)S(1)} %get-tuple-element.79), channel_id=1, source_target_pairs={{4,0},{12,8},{20,16},{28,24},{0,4},{8,12},{16,20},{24,28},{5,1},{1... | collective-permute-start | bytes 442376 | tf_op jit(solution)/shard_map/ppermute | solution.py:383
  24.7 19.4 %collective-permute-start.4 = (bf16[3,4,48,128]{3,2,1,0:T(8,128)(2,1)S(1)}, bf16[3,4,48,128]{3,2,1,0:T(8,128)(2,1)S(1)}, u32[]{:S(2)}, u32[]{:S(2)}) collective-permute-start(bf16[3,4,48,128]{3,2,1,0:T(8,128)(2,1)S(1)} %get-tuple-element.80), channel_id=1, source_target_pairs={{8,4},{24,20},{4,8},{20,24},{9,5},{25,21},{5,9},{21,25},{10,6},{26... | collective-permute-start | bytes 442376 | tf_op jit(solution)/shard_map/ppermute | solution.py:383
  31.9 6.3 %collective-permute-start.5 = (bf16[1,4,48,128]{3,2,1,0:T(8,128)(2,1)S(1)}, bf16[1,4,48,128]{3,2,1,0:T(8,128)(2,1)S(1)}, u32[]{:S(2)}, u32[]{:S(2)}) collective-permute-start(bf16[1,4,48,128]{3,2,1,0:T(8,128)(2,1)S(1)} %get-tuple-element.81), channel_id=1, source_target_pairs={{0,16},{4,20},{8,24},{12,28},{16,0},{20,4},{24,8},{28,12},{1,17},{... | collective-permute-start | bytes 147464 | tf_op jit(solution)/shard_map/ppermute | solution.py:383
  32.0 9.1 %collective-permute-start.6 = (bf16[1,4,48,128]{3,2,1,0:T(8,128)(2,1)S(1)}, bf16[1,4,48,128]{3,2,1,0:T(8,128)(2,1)S(1)}, u32[]{:S(2)}, u32[]{:S(2)}) collective-permute-start(bf16[1,4,48,128]{3,2,1,0:T(8,128)(2,1)S(1)} %get-tuple-element.82), channel_id=1, source_target_pairs={{0,20},{4,24},{8,28},{20,0},{24,4},{28,8},{1,21},{5,25},{9,29},{21... | collective-permute-start | bytes 147464 | tf_op jit(solution)/shard_map/ppermute | solution.py:383
  36.3 7.8 %collective-permute-start.7 = (bf16[1,4,48,128]{3,2,1,0:T(8,128)(2,1)S(1)}, bf16[1,4,48,128]{3,2,1,0:T(8,128)(2,1)S(1)}, u32[]{:S(2)}, u32[]{:S(2)}) collective-permute-start(bf16[1,4,48,128]{3,2,1,0:T(8,128)(2,1)S(1)} %get-tuple-element.83), channel_id=1, source_target_pairs={{4,16},{8,20},{12,24},{16,4},{20,8},{24,12},{5,17},{9,21},{13,25},... | collective-permute-start | bytes 147464 | tf_op jit(solution)/shard_map/ppermute | solution.py:383
  45.0 4.9 %collective-permute-start.12 = (bf16[48,2048]{1,0:T(8,128)(2,1)S(1)}, bf16[48,2048]{1,0:T(8,128)(2,1)S(1)}, u32[]{:S(2)}, u32[]{:S(2)}) collective-permute-start(bf16[48,2048]{1,0:T(8,128)(2,1)S(1)} %settle.2.refs_0_), channel_id=1, source_target_pairs={{0,1},{1,0},{2,3},{3,2},{4,5},{5,4},{6,7},{7,6},{8,9},{9,8},{10,11... | collective-permute-start | bytes 589832 | tf_op jit(solution)/shard_map/ppermute | solution.py:366
  45.1 7.3 %collective-permute-start.11 = (bf16[48,2048]{1,0:T(8,128)(2,1)S(1)}, bf16[48,2048]{1,0:T(8,128)(2,1)S(1)}, u32[]{:S(2)}, u32[]{:S(2)}) collective-permute-start(bf16[48,2048]{1,0:T(8,128)(2,1)S(1)} %settle.2.refs_0_), channel_id=1, source_target_pairs={{0,2},{1,3},{2,0},{3,1},{4,6},{5,7},{6,4},{7,5},{8,10},{9,11},{10,... | collective-permute-start | bytes 589832 | tf_op jit(solution)/shard_map/ppermute | solution.py:366
  57.2 9.2 %collective-permute-start.14 = (bf16[2,1024,128]{2,1,0:T(8,128)(2,1)S(1)}, bf16[2,1024,128]{2,1,0:T(8,128)(2,1)S(1)}, u32[]{:S(2)}, u32[]{:S(2)}) collective-permute-start(bf16[2,1024,128]{2,1,0:T(8,128)(2,1)S(1)} %get-tuple-element.108), channel_id=1, source_target_pairs={{0,4},{1,9},{2,6},{3,11},{4,0},{5,13},{6,2},{7,15},{8,12},{9,1},{1... | collective-permute-start | bytes 1572872 | tf_op jit(solution)/shard_map/ppermute | solution.py:305
  66.5 7.1 %collective-permute-start.15 = (bf16[2,512,128]{2,1,0:T(8,128)(2,1)S(1)}, bf16[2,512,128]{2,1,0:T(8,128)(2,1)S(1)}, u32[]{:S(2)}, u32[]{:S(2)}) collective-permute-start(bf16[2,512,128]{2,1,0:T(8,128)(2,1)S(1)} %get-tuple-element.116), channel_id=1, source_target_pairs={{0,8},{1,5},{2,10},{3,7},{4,12},{5,1},{6,14},{7,3},{8,0},{9,13},{1... | collective-permute-start | bytes 786440 | tf_op jit(solution)/shard_map/ppermute | solution.py:305
  66.6 5.2 %collective-permute-start.16 = (bf16[1,4,48,128]{3,2,1,0:T(8,128)(2,1)S(1)}, bf16[1,4,48,128]{3,2,1,0:T(8,128)(2,1)S(1)}, u32[]{:S(2)}, u32[]{:S(2)}) collective-permute-start(bf16[1,4,48,128]{3,2,1,0:T(8,128)(2,1)S(1)} %get-tuple-element.117), channel_id=1, source_target_pairs={{0,16},{4,20},{8,24},{12,28},{16,0},{20,4},{24,8},{28,12},{1,17},{... | collective-permute-start | bytes 147464 | tf_op jit(solution)/shard_map/ppermute | solution.py:383
  73.7 9.6 %collective-permute-start.17 = (bf16[2,256,128]{2,1,0:T(8,128)(2,1)S(1)}, bf16[2,256,128]{2,1,0:T(8,128)(2,1)S(1)}, u32[]{:S(2)}, u32[]{:S(2)}) collective-permute-start(bf16[2,256,128]{2,1,0:T(8,128)(2,1)S(1)} %get-tuple-element.120), channel_id=1, source_target_pairs={{0,16},{1,17},{2,18},{3,19},{4,20},{5,21},{6,22},{7,23},{8,24},{9,... | collective-permute-start | bytes 393224 | tf_op jit(solution)/shard_map/ppermute | solution.py:305
  74.6 8.7 %collective-permute-start.18 = (bf16[1,4,48,128]{3,2,1,0:T(8,128)(2,1)S(1)}, bf16[1,4,48,128]{3,2,1,0:T(8,128)(2,1)S(1)}, u32[]{:S(2)}, u32[]{:S(2)}) collective-permute-start(bf16[1,4,48,128]{3,2,1,0:T(8,128)(2,1)S(1)} %get-tuple-element.121), channel_id=1, source_target_pairs={{0,20},{4,24},{8,28},{20,0},{24,4},{28,8},{1,21},{5,25},{9,29},{21... | collective-permute-start | bytes 147464 | tf_op jit(solution)/shard_map/ppermute | solution.py:383
  83.3 9.5 %collective-permute-start.19 = (bf16[1,2,256,128]{3,2,1,0:T(8,128)(2,1)S(1)}, bf16[1,2,256,128]{3,2,1,0:T(8,128)(2,1)S(1)}, u32[]{:S(2)}, u32[]{:S(2)}) collective-permute-start(bf16[1,2,256,128]{3,2,1,0:T(8,128)(2,1)S(1)} %fusion), channel_id=1, source_target_pairs={{0,16},{1,17},{2,18},{3,19},{4,20},{5,21},{6,22},{7,23},{8,24},{9,... | collective-permute-start | bytes 393224 | tf_op jit(solution)/shard_map/ppermute | solution.py:305
  84.6 8.2 %collective-permute-start.20 = (bf16[1,4,48,128]{3,2,1,0:T(8,128)(2,1)S(1)}, bf16[1,4,48,128]{3,2,1,0:T(8,128)(2,1)S(1)}, u32[]{:S(2)}, u32[]{:S(2)}) collective-permute-start(bf16[1,4,48,128]{3,2,1,0:T(8,128)(2,1)S(1)} %get-tuple-element.123), channel_id=1, source_target_pairs={{4,16},{8,20},{12,24},{16,4},{20,8},{24,12},{5,17},{9,21},{13,25},... | collective-permute-start | bytes 147464 | tf_op jit(solution)/shard_map/ppermute | solution.py:383
  92.8 8.6 %collective-permute-start.21 = (bf16[2,2,256,128]{3,2,1,0:T(8,128)(2,1)S(1)}, bf16[2,2,256,128]{3,2,1,0:T(8,128)(2,1)S(1)}, u32[]{:S(2)}, u32[]{:S(2)}) collective-permute-start(bf16[2,2,256,128]{3,2,1,0:T(8,128)(2,1)S(1)} %pad_maximum_fusion.1), channel_id=1, source_target_pairs={{0,8},{1,5},{2,10},{3,7},{4,12},{5,1},{6,14},{7,3},{8,0},{9,13},{1... | collective-permute-start | bytes 786440 | tf_op jit(solution)/shard_map/ppermute | solution.py:305
  92.9 5.3 %collective-permute-start.22 = (bf16[1,4,48,128]{3,2,1,0:T(8,128)(2,1)S(1)}, bf16[1,4,48,128]{3,2,1,0:T(8,128)(2,1)S(1)}, u32[]{:S(2)}, u32[]{:S(2)}) collective-permute-start(bf16[1,4,48,128]{3,2,1,0:T(8,128)(2,1)S(1)} %get-tuple-element.125), channel_id=1, source_target_pairs={{4,0},{12,8},{20,16},{28,24},{0,4},{8,12},{16,20},{24,28},{5,1},{1... | collective-permute-start | bytes 147464 | tf_op jit(solution)/shard_map/ppermute | solution.py:383
  93.9 7.5 %collective-permute-start.23 = (bf16[1,4,48,128]{3,2,1,0:T(8,128)(2,1)S(1)}, bf16[1,4,48,128]{3,2,1,0:T(8,128)(2,1)S(1)}, u32[]{:S(2)}, u32[]{:S(2)}) collective-permute-start(bf16[1,4,48,128]{3,2,1,0:T(8,128)(2,1)S(1)} %get-tuple-element.126), channel_id=1, source_target_pairs={{8,4},{24,20},{4,8},{20,24},{9,5},{25,21},{5,9},{21,25},{10,6},{26... | collective-permute-start | bytes 147464 | tf_op jit(solution)/shard_map/ppermute | solution.py:383
  101.4 9.2 %collective-permute-start.24 = (bf16[4,2,256,128]{3,2,1,0:T(8,128)(2,1)S(1)}, bf16[4,2,256,128]{3,2,1,0:T(8,128)(2,1)S(1)}, u32[]{:S(2)}, u32[]{:S(2)}) collective-permute-start(bf16[4,2,256,128]{3,2,1,0:T(8,128)(2,1)S(1)} %pad_maximum_fusion.own_ref), channel_id=1, source_target_pairs={{0,4},{1,9},{2,6},{3,11},{4,0},{5,13},{6,2},{7,15},{8,12},{9,1},{1... | collective-permute-start | bytes 1572872 | tf_op jit(solution)/shard_map/ppermute | solution.py:305
  (12 other events, 99.3 us)

commit v3 on v2

--- a/solution.py
+++ b/solution.py
@@ -19,20 +19,25 @@
 F32 = jnp.float32
 
 
-def call(kernel, name, outs, smem_count, args, scratch=(), flops=0, vmem_mib=4):
+def call(kernel, name, outs, spaces, args, scratch=(), flops=0, vmem_mib=4):
+    memory = {"S": SMEM, "H": pltpu.HBM, "V": VMEM}
+    spaces = spaces + "V" * (len(args) - len(spaces))
     moved = sum(a.size * a.dtype.itemsize for a in args)
     moved += sum(o.size * o.dtype.itemsize for o in outs)
     return pl.pallas_call(
         kernel,
         out_shape=list(outs),
-        in_specs=[pl.BlockSpec(memory_space=SMEM)] * smem_count
-        + [pl.BlockSpec(memory_space=VMEM)] * (len(args) - smem_count),
+        in_specs=[pl.BlockSpec(memory_space=memory[space]) for space in spaces],
         out_specs=[pl.BlockSpec(memory_space=VMEM)] * len(outs),
         scratch_shapes=list(scratch),
         name=name,
         cost_estimate=pl.CostEstimate(flops=flops, bytes_accessed=moved, transcendentals=0),
         compiler_params=pltpu.CompilerParams(vmem_limit_bytes=vmem_mib << 20),
-    )(*args)
+    )(*(keep_in_hbm(a) if space == "H" else a for a, space in zip(args, spaces)))
+
+
+def keep_in_hbm(value):
+    return pltpu.with_memory_space_constraint(value, pltpu.HBM)
 
 
 def struct(shape, dtype):
@@ -76,86 +81,125 @@
     return [[(s, t) for s, t, _ in g] for g in groups], plan
 
 
-def pack_kernel(lists_ref, plan_ref, pre_ref, feat_ref, *out_refs):
+def here(values):
     me = lax.axis_index("tile")
+    common = int(np.bincount(values).argmax())
+    found = jnp.int32(common)
+    for tile, value in enumerate(values):
+        if value != common:
+            found = jnp.where(me == tile, jnp.int32(int(value)), found)
+    return found
+
+
+def pack_kernel(plan, lists_ref, *refs):
+    count = plan.shape[0]
+    sources, refs = refs[:4], refs[4:]
+    out_refs, copied, sems = refs[:count], refs[count:-1], refs[-1]
+    copies = [
+        pltpu.make_async_copy(source, target, sems.at[index])
+        for index, (source, target) in enumerate(zip(sources, copied))
+    ]
+    for copy in copies:
+        copy.start()
+    pre_ref, feat_ref = copied[:2]
+    copies[0].wait()
+    copies[1].wait()
     last = pre_ref.shape[1] // 128 - 1
     for index, out_ref in enumerate(out_refs):
-        direction = plan_ref[index, 0, me]
+        direction = here(plan[index, 0])
         for slot in range(out_ref.shape[1]):
             block = jnp.minimum(lists_ref[0, direction, slot], last)
             lanes = pl.ds(pl.multiple_of(block * 128, 128), 128)
             out_ref[0, slot] = jnp.maximum(pre_ref[:, lanes], 0)
             out_ref[1, slot] = feat_ref[:, lanes]
-
-
-def pack(lists, plan, pre_act, features):
-    shape = struct((2, lists.shape[2], features.shape[0], 128), BF16)
-    return call(
-        pack_kernel, "pack_sends", [shape] * plan.shape[0], 2, (lists, plan, pre_act, features)
-    )
+    copies[2].wait()
+    copies[3].wait()
+
+
+def pack(lists, plan, *sources):
+    shape = struct((2, lists.shape[2], sources[0].shape[0], 128), BF16)
+    result = call(
+        functools.partial(pack_kernel, plan),
+        "pack_sends",
+        [shape] * plan.shape[0] + [struct(s.shape, s.dtype) for s in sources],
+        "SHHHH",
+        (lists, *sources),
+        [pltpu.SemaphoreType.DMA((4,))],
+    )
+    return result[: plan.shape[0]], result[plan.shape[0] :]
 
 
 def gather_full(parts, full):
     me = lax.axis_index("chan")
     width = parts[0].shape[0]
     for step, part in enumerate(parts):
-        place = pl.multiple_of((me ^ step) * width, 16)
-        full[pl.ds(place, width), :] = part[...]
-
-
-def partial_kernel(group_count, ride_count, pin_ref, plan_ref, *refs):
+        full[pl.ds(pl.multiple_of((me ^ step) * width, 16), width), :] = part[...]
+
+
+def partial_kernel(plan, riders, pin_ref, weight_ref, *refs):
+    group_count = plan.shape[0]
     parts, refs = refs[:4], refs[4:]
-    weight_ref, refs = refs[0], refs[1:]
-    ride_refs, refs = refs[:ride_count], refs[ride_count:]
+    ride_refs, refs = refs[: len(riders)], refs[len(riders) :]
     local_ref = refs[0]
     back_refs = refs[1 : 1 + group_count]
-    full, product, total = refs[1 + group_count :]
-    me = lax.axis_index("tile")
+    full, even_product, odd_product, even, odd = refs[1 + group_count :]
     offset_count, block_count = pin_ref.shape[1:]
     width = local_ref.shape[1]
     gather_full(parts, full)
-    total[...] = jnp.zeros_like(total)
-
-    def two_blocks(turn, _):
+    even[...] = jnp.zeros_like(even)
+    odd[...] = jnp.zeros_like(odd)
+
+    def multiply(turn, product):
         lanes = pl.ds(pl.multiple_of(turn * 256, 256), 256)
         product[...] = jnp.dot(weight_ref[...], full[:, lanes], preferred_element_type=F32)
+
+    def land(turn, product):
         for offset in range(offset_count):
-            for half in range(2):
+            for half, total in enumerate((even, odd)):
                 entry = pin_ref[0, offset, turn * 2 + half]
                 total[entry] += product[
                     offset * width : (offset + 1) * width, half * 128 : (half + 1) * 128
                 ]
+
+    turns = block_count // 2
+    multiply(0, even_product)
+
+    def two_turns(step, _):
+        multiply(2 * step + 1, odd_product)
+        land(2 * step, even_product)
+        multiply(jnp.minimum(2 * step + 2, turns - 1), even_product)
+        land(2 * step + 1, odd_product)
         return 0
 
-    lax.fori_loop(0, block_count // 2, two_blocks, 0)
-    local_ref[...] = total[:block_count]
+    lax.fori_loop(0, turns // 2, two_turns, 0)
+    local_ref[...] = even[:block_count] + odd[:block_count]
     for index, back_ref in enumerate(back_refs):
-        base = plan_ref[index, 1, me]
+        base = here(plan[index, 1])
         for slot in range(back_ref.shape[1]):
-            back_ref[0, slot] = total[base + slot].astype(BF16)
-    for ride_ref, back_ref in zip(ride_refs, back_refs):
-        back_ref[1:] = ride_ref[...]
-
-
-def partial_sums(pin, plan, parts, weight, slot_count, rides=()):
+            back_ref[0, slot] = (even[base + slot] + odd[base + slot]).astype(BF16)
+    for index, ride_ref in zip(riders, ride_refs):
+        back_refs[index][1:] = ride_ref[...]
+
+
+def partial_sums(pin, plan, parts, weight, slot_count, riders=(), rides=()):
     width, voxels = parts[0].shape
     offset_count, block_count = pin.shape[1:]
-    group_count = plan.shape[0]
     entries = block_count + 9 * slot_count + 1
-    back = (slot_count, width, 128)
     outs = [struct((block_count, width, 128), F32)]
-    outs += [struct((3,) + back, BF16) for _ in rides]
-    outs += [struct((1,) + back, BF16)] * (group_count - len(rides))
+    for group in range(plan.shape[0]):
+        outs.append(struct((3 if group in riders else 1, slot_count, width, 128), BF16))
     flat = weight.reshape(offset_count * width, 4 * width)
     result = call(
-        functools.partial(partial_kernel, group_count, len(rides)),
+        functools.partial(partial_kernel, plan, riders),
         "partial_sums",
         outs,
-        2,
-        (pin, plan, *parts, flat, *rides),
+        "S",
+        (pin, flat, *parts, *rides),
         [
             VMEM((4 * width, voxels), BF16),
             VMEM((offset_count * width, 256), F32),
+            VMEM((offset_count * width, 256), F32),
+            VMEM((entries, width, 128), F32),
             VMEM((entries, width, 128), F32),
         ],
         flops=2 * weight.size * voxels,
@@ -169,13 +213,10 @@
     return -(-(rows + rows // 2) // step) * step
 
 
-def weight_kernel(group_count, which, factor, joined, pin_ref, plan_ref, *refs):
+def weight_kernel(plan, which, factor, pin_ref, own_ref, *refs):
     parts, refs = refs[:4], refs[4:]
-    own_ref, refs = refs[0], refs[1:]
-    ghost_refs, refs = refs[:group_count], refs[group_count:]
-    other_refs, refs = refs[: 2 * joined], refs[2 * joined :]
+    ghost_refs, refs = refs[: plan.shape[0]], refs[plan.shape[0] :]
     keep_ref, send_ref, full, extended, gathered, wide, tall = refs
-    me = lax.axis_index("tile")
     offset_count, block_count = pin_ref.shape[1:]
     width = own_ref.shape[0]
     gather_full(parts, full)
@@ -183,10 +224,9 @@
         value = own_ref[:, block * 128 : (block + 1) * 128]
         extended[block] = jnp.maximum(value, 0) if which == 0 else value
     for index, ghost_ref in enumerate(ghost_refs):
-        base = plan_ref[index, 1, me]
-        lead = ghost_ref.shape[0] - 2 + which
+        base = here(plan[index, 1])
         for slot in range(ghost_ref.shape[1]):
-            extended[base + slot] = ghost_ref[lead, slot]
+            extended[base + slot] = ghost_ref[ghost_ref.shape[0] - 2 + which, slot]
     empty = block_count + 8 * ghost_refs[0].shape[1]
     extended[empty] = jnp.zeros_like(extended[empty])
     chunk = gathered.shape[0] // width
@@ -202,8 +242,7 @@
             gathered[...], full[...], (((1,), (1,)), ((), ())), preferred_element_type=F32
         )
         rows = chunk * width
-        here = pl.ds(pl.multiple_of(turn * rows, 16), rows)
-        wide[here, : grads.shape[1]] = grads * factor
+        wide[pl.ds(pl.multiple_of(turn * rows, 16), rows), : grads.shape[1]] = grads * factor
         return 0
 
     lax.fori_loop(0, offset_count // chunk, some_offsets, 0)
@@ -215,14 +254,11 @@
         tall[rows + half :] = jnp.zeros((tall.shape[0] - rows - half, 128), F32)
     bit = exchange_bit(0)
     split = tall.shape[0] // 2
-    if joined:
-        keep_ref[:1] = other_refs[0][...]
-        send_ref[:1] = other_refs[1][...]
-    keep_ref[joined] = tall[pl.ds(pl.multiple_of(bit * split, 16), split), :]
-    send_ref[joined] = tall[pl.ds(pl.multiple_of((1 - bit) * split, 16), split), :].astype(BF16)
-
-
-def weight_sums(pin, plan, parts, own, ghosts, which, factor, tile_count, others=()):
+    keep_ref[...] = tall[pl.ds(pl.multiple_of(bit * split, 16), split), :]
+    send_ref[...] = tall[pl.ds(pl.multiple_of((1 - bit) * split, 16), split), :].astype(BF16)
+
+
+def weight_sums(pin, plan, parts, own, ghosts, which, factor, tile_count):
     width, voxels = own.shape
     offset_count, block_count = pin.shape[1:]
     slot_count = ghosts[0].shape[1]
@@ -230,14 +266,13 @@
     chunk = 9 if offset_count % 9 == 0 else 1
     rows = offset_count * width
     tall = packed_rows(rows, tile_count)
-    joined = 1 if others else 0
-    shape = (1 + joined, tall // 2, 128)
+    shape = (tall // 2, 128)
     return call(
-        functools.partial(weight_kernel, len(ghosts), which, factor, joined),
+        functools.partial(weight_kernel, plan, which, factor),
         "weight_sums",
         [struct(shape, F32), struct(shape, BF16)],
-        2,
-        (pin, plan, *parts, own, *ghosts, *others),
+        "S",
+        (pin, own, *parts, *ghosts),
         [
             VMEM((4 * width, voxels), BF16),
             VMEM((entries, width, 128), BF16),
@@ -246,17 +281,16 @@
             VMEM((tall, 128), F32),
         ],
         flops=2 * rows * 4 * width * voxels,
-        vmem_mib=16,
-    )
-
-
-def settle_kernel(first, lists_ref, plan_ref, local_ref, other_ref, *refs):
+        vmem_mib=14,
+    )
+
+
+def settle_kernel(plan, first, lists_ref, other_ref, local_ref, *refs):
     *back_refs, out_ref, total = refs
-    me = lax.axis_index("tile")
     block_count = local_ref.shape[0]
     total[:block_count] = local_ref[...]
     for index, back_ref in enumerate(back_refs):
-        direction = plan_ref[index, 0, me]
+        direction = here(plan[index, 0])
         for slot in range(back_ref.shape[1]):
             block = lists_ref[0, direction, slot]
             total[block] += back_ref[0, slot].astype(F32)
@@ -273,11 +307,11 @@
 def settle(first, lists, plan, local, other, backs):
     block_count, width, _ = local.shape
     return call(
-        functools.partial(settle_kernel, first),
+        functools.partial(settle_kernel, plan, first),
         "settle",
         [struct(other.shape, BF16)],
-        2,
-        (lists, plan, local, other, *backs),
+        "S",
+        (lists, other, local, *backs),
         [VMEM((block_count + 1, width, 128), F32)],
         flops=local.size,
     )[0]
@@ -305,27 +339,30 @@
     return lax.ppermute(value, ("tile", "chan"), pairs)
 
 
-def halve_kernel(step, keep_ref, got_ref, next_ref, send_ref):
+def halve_kernel(step, *refs):
+    *pair_refs, next_ref, send_ref = refs
     bit = exchange_bit(step)
     split = next_ref.shape[1]
     mine = pl.ds(pl.multiple_of(bit * split, 16), split)
     theirs = pl.ds(pl.multiple_of((1 - bit) * split, 16), split)
-    for index in range(keep_ref.shape[0]):
-        next_ref[index] = keep_ref[index, mine, :] + got_ref[index, mine, :].astype(F32)
-        send_ref[index] = (
-            keep_ref[index, theirs, :] + got_ref[index, theirs, :].astype(F32)
-        ).astype(BF16)
-
-
-def halve(step, keep, got):
-    shape = (keep.shape[0], keep.shape[1] // 2, 128)
+    for index in range(2):
+        if len(pair_refs) == 4:
+            keep, got = pair_refs[2 * index : 2 * index + 2]
+        else:
+            keep, got = (ref.at[index] for ref in pair_refs)
+        next_ref[index] = keep[mine, :] + got[mine, :].astype(F32)
+        send_ref[index] = (keep[theirs, :] + got[theirs, :].astype(F32)).astype(BF16)
+
+
+def halve(step, *pairs):
+    shape = (2, pairs[0].shape[-2] // 2, 128)
     return call(
         functools.partial(halve_kernel, step),
         "halve",
         [struct(shape, F32), struct(shape, BF16)],
-        0,
-        (keep, got),
-        flops=keep.size,
+        "",
+        pairs,
+        flops=2 * pairs[0].size,
     )
 
 
@@ -355,7 +392,7 @@
         functools.partial(unpack_kernel, tile_count),
         "unpack_sums",
         [struct((rows, columns), F32)] * own.shape[1],
-        0,
+        "",
         (own, got),
         [VMEM((tile_count * own.shape[2], 128), F32)],
         vmem_mib=8,
@@ -375,7 +412,6 @@
     rows = offset_count * width
     steps = tile_count.bit_length() - 1
     pair_lists, plan = ghost_plan(tile_count, block_count, slot_count)
-    plan = jnp.asarray(plan)
     factor = 1.0 / math.sqrt(tile_count * voxels)
     tie = lambda *values: lax.optimization_barrier(values)
 
@@ -384,50 +420,55 @@
 
     back_lists = [[(t, s) for s, t in p] for p in pair_lists]
 
-    sends = pack(send_list, plan, pre_act, features)
-    far, near = swap_part(cotangent, 2), swap_part(cotangent, 1)
-    far, near, sends = tie(far, near, sends)
-    cot_parts = (cotangent, near, far, swap_part(far, 1))
-    ghosts = give(sends[2:], pair_lists[2:])
-
-    local_two, backs = partial_sums(pair_in, plan, cot_parts, weight_two, slot_count, sends[:2])
-    backs = give(backs, back_lists)
-    backs, ghosts = tie(backs, ghosts)
-    ghosts = list(backs[:2]) + list(ghosts)
+    early = range(2, min(4, len(pair_lists)))
+    riders = [g for g in range(len(pair_lists)) if g not in early]
+
+    far, near, last = (swap_part(cotangent, bits) for bits in (2, 1, 3))
+    sends, here_now = pack(send_list, plan, pre_act, features, cotangent, weight_two)
+    pre_act, features, cotangent, weight_two = here_now
+    soon = give([sends[g] for g in early], [pair_lists[g] for g in early])
+    cot_parts = (cotangent, near, far, last)
+    local_two, backs = partial_sums(
+        pair_in, plan, cot_parts, weight_two, slot_count, riders, [sends[g] for g in riders]
+    )
+    backs, soon = tie(give(backs, back_lists), soon)
     grad_pre = settle(True, send_list, plan, local_two, pre_act, backs)
 
+    ghosts = list(backs)
+    for group, ghost in zip(early, soon):
+        ghosts[group] = ghost
     far, near = swap_part(grad_pre, 2), swap_part(grad_pre, 1)
-    split_two = weight_sums(
-        pair_in, plan, cot_parts, pre_act, ghosts, 0, factor, tile_count
-    )
-    far, near, split_two = tie(far, near, split_two)
+    keep_two, send = weight_sums(pair_in, plan, cot_parts, pre_act, ghosts, 0, factor, tile_count)
+    far, near, send = tie(far, near, send)
+    got_two = trade(send, 0)
     pre_parts = (grad_pre, near, far, swap_part(far, 1))
-    keep, send = weight_sums(
-        pair_in, plan, pre_parts, features, ghosts, 1, factor, tile_count, split_two
-    )
+    keep_one, send = weight_sums(
+        pair_in, plan, pre_parts, features, ghosts, 1, factor, tile_count
+    )
+    got_two, send = tie(got_two, send)
     got = trade(send, 0)
-    pre_parts, keep = tie(pre_parts, keep)
+    pre_parts, keep_one = tie(pre_parts, keep_one)
     local_one, backs = partial_sums(pair_in, plan, pre_parts, weight_one, slot_count)
     got, backs = tie(got, backs)
-    order = list(range(2, len(backs))) + [0, 1]
-    waits = 2 * steps - 2
+    shares = [[0, 1]] + [[g] for g in range(2, len(backs))]
     returned = [None] * len(backs)
 
-    def beside(value, wait):
-        share = order[wait * len(order) // waits : (wait + 1) * len(order) // waits]
-        if not share:
-            return value
-        value, mine = tie(value, give([backs[g] for g in share], [back_lists[g] for g in share]))
-        for group, back in zip(share, mine):
+    def beside(value, step):
+        share = shares.pop(0) if shares else []
+        value, mine = tie(value, [backs[g] for g in share])
+        got, landed = tie(trade(value, step), give(mine, [back_lists[g] for g in share]))
+        for group, back in zip(share, landed):
             returned[group] = back
-        return value
-
+        return got
+
+    arrived = (keep_two, got_two, keep_one, got)
     for step in range(1, steps):
-        keep, send = halve(step, keep, got)
-        got = beside(trade(send, step), step - 1)
+        keep, send = halve(step, *arrived)
+        got = beside(send, step)
+        arrived = (keep, got)
     chunk = (keep + got.astype(F32)).astype(BF16)[None]
     for step in reversed(range(1, steps)):
-        got = beside(trade(chunk, step), 2 * steps - 2 - step)
+        got = beside(chunk, step)
         chunk = jnp.concatenate([chunk, got], axis=0)
     got = trade(chunk, 0)
     grad_features = settle(False, send_list, plan, local_one, cotangent, returned)

time: 114 us -> 103 us (0.904)
  waiting for transfers between devices: 41.5 us -> 31.6 us
  starting transfers between devices: 41.4 us -> 47.8 us
  local copies, waits for them, and re-layouts: 6.8 us -> 1.54 us
  Pallas kernels: 21.8 us -> 20.2 us
    unnamed x24 -> x4, local copies, waits for them, and re-layouts: 6.8 us -> 1.54 us
    ppermute x6 -> x7, starting transfers between devices: 2.5 us -> 7.55 us  [trade(): return lax.ppermute(value, ('tile', 'chan'), pairs)]
    ppermute x13 -> x12, waiting for transfers between devices: 22 us -> 17.8 us  [give(): return [lax.ppermute(v, 'tile', p) for v, p in zip(values, lists)]]
    ppermute x6 -> x7, waiting for transfers between devices: 13.8 us -> 10.9 us  [trade(): return lax.ppermute(value, ('tile', 'chan'), pairs)]
    ppermute x6, waiting for transfers between devices: 5.69 us -> 2.88 us  [swap_part(): return lax.ppermute(value, 'chan', [(i, i ^ bits) for i in range(4)])]
    pallas_call x10, Pallas kernels: 21.8 us -> 20.2 us  [call(): pl.pallas_call(kernel, out_shape=list(outs), in_specs=[pl.BlockSpec(memor...]
    ppermute x13 -> x12, starting transfers between devices: 35.6 us -> 36.4 us  [give(): return [lax.ppermute(v, 'tile', p) for v, p in zip(values, lists)]]
  transfers between devices with their start and end apart: 25 -> 25, of which waited for: 12 -> 13; matrix products, arithmetic and copies ran while one was open for 1% -> 2% of each run, Pallas kernels for 14% -> 17%
where the time goes in v3:
time: 103 us; the launch traced here: 102 us
  starting transfers between devices  47.8 us (46%)
  waiting for transfers between devices  31.6 us (31%)
  Pallas kernels  20.2 us (20%)
  local copies, waits for them, and re-layouts  1.54 us (1%)
    ppermute x12, starting transfers between devices, give(): return [lax.ppermute(v, 'tile', p) for v, p in zip(values, lists)]  36.4 us
    pallas_call x10, Pallas kernels, call(): pl.pallas_call(kernel, out_shape=list(outs), in_specs=[pl.BlockSpec(memor...  20.2 us
    ppermute x12, waiting for transfers between devices, give(): return [lax.ppermute(v, 'tile', p) for v, p in zip(values, lists)]  17.8 us
    ppermute x7, waiting for transfers between devices, trade(): return lax.ppermute(value, ('tile', 'chan'), pairs)  10.9 us
    ppermute x7, starting transfers between devices, trade(): return lax.ppermute(value, ('tile', 'chan'), pairs)  7.55 us
    ppermute x6, starting transfers between devices, swap_part(): return lax.ppermute(value, 'chan', [(i, i ^ bits) for i in range(4)])  3.87 us
    ppermute x6, waiting for transfers between devices, swap_part(): return lax.ppermute(value, 'chan', [(i, i ^ bits) for i in range(4)])  2.88 us
  transfers between devices with their start and end apart: 25, of which 13 were waited for; matrix products, arithmetic and copies ran while one was open for 2% of the time, Pallas kernels for 17%

profile of v3, /device:TPU:2, one launch (start us, length us, event | category | flops | bytes accessed | tf_op | source)
XLA Modules:
  0.0 102.0 jit_solution(1255956448409703721)
XLA Ops:
  3.6 2.0 %pack_sends.1 = (bf16[2,4,48,128]{3,2,1,0:T(8,128)(2,1)S(1)}, bf16[2,4,48,128]{3,2,1,0:T(8,128)(2,1)S(1)}, bf16[2,4,48,128]{3,2,1,0:T(8,128)(2,1)S(1)}, bf16[2,4...) custom-call(s32[1,8,4]{2,1,0:T(8,128)S(1)} %copy.16.lists_ref, ...), custom_call_target="tpu_custom_call" | custom-call | bytes 2666624 | tf_op jit(solution)/shard_map/pack_sends/pallas_call | solution.py:27
  5.6 2.7 %collective-permute-start.8 = (bf16[2,4,48,128]{3,2,1,0:T(8,128)(2,1)S(1)}, bf16[2,4,48,128]{3,2,1,0:T(8,128)(2,1)S(1)}, u32[]{:S(2)}, u32[]{:S(2)}) collective-permute-start(bf16[2,4,48,128]{3,2,1,0:T(8,128)(2,1)S(1)} %get-tuple-element.87), channel_id=1, source_target_pairs={{16,0},{20,4},{24,8},{28,12},{0,16},{4,20},{8,24},{12,28},{17,1},{... | collective-permute-start | bytes 294920 | tf_op jit(solution)/shard_map/ppermute | solution.py:419
  8.3 3.2 %collective-permute-start.9 = (bf16[2,4,48,128]{3,2,1,0:T(8,128)(2,1)S(1)}, bf16[2,4,48,128]{3,2,1,0:T(8,128)(2,1)S(1)}, u32[]{:S(2)}, u32[]{:S(2)}) collective-permute-start(bf16[2,4,48,128]{3,2,1,0:T(8,128)(2,1)S(1)} %get-tuple-element.88), channel_id=1, source_target_pairs={{20,0},{24,4},{28,8},{0,20},{4,24},{8,28},{21,1},{25,5},{29,9},{1,... | collective-permute-start | bytes 294920 | tf_op jit(solution)/shard_map/ppermute | solution.py:419
  12.4 3.8 %partial_sums.2 = (f32[16,48,128]{2,1,0:T(8,128)S(1)}, bf16[3,4,48,128]{3,2,1,0:T(8,128)(2,1)S(1)}, bf16[3,4,48,128]{3,2,1,0:T(8,128)(2,1)S(1)}, bf16[1,4,48,128...) custom-call(s32[1,27,16]{2,1,0:T(8,128)S(1)} %copy.15.pin_ref, ...), custom_call_target="tpu_custom_call" | custom-call | flops 1019215872 | bytes 2514624 | tf_op jit(solution)/shard_map/partial_sums/pallas_call | solution.py:27
  16.7 4.5 %collective-permute-start.4 = (bf16[3,4,48,128]{3,2,1,0:T(8,128)(2,1)S(1)}, bf16[3,4,48,128]{3,2,1,0:T(8,128)(2,1)S(1)}, u32[]{:S(2)}, u32[]{:S(2)}) collective-permute-start(bf16[3,4,48,128]{3,2,1,0:T(8,128)(2,1)S(1)} %get-tuple-element.83), channel_id=1, source_target_pairs={{8,4},{24,20},{4,8},{20,24},{9,5},{25,21},{5,9},{21,25},{10,6},{26... | collective-permute-start | bytes 442376 | tf_op jit(solution)/shard_map/ppermute | solution.py:419
  21.2 1.9 %collective-permute-start.7 = (bf16[3,4,48,128]{3,2,1,0:T(8,128)(2,1)S(1)}, bf16[3,4,48,128]{3,2,1,0:T(8,128)(2,1)S(1)}, u32[]{:S(2)}, u32[]{:S(2)}) collective-permute-start(bf16[3,4,48,128]{3,2,1,0:T(8,128)(2,1)S(1)} %get-tuple-element.86), channel_id=1, source_target_pairs={{4,16},{8,20},{12,24},{16,4},{20,8},{24,12},{5,17},{9,21},{13,25},... | collective-permute-start | bytes 442376 | tf_op jit(solution)/shard_map/ppermute | solution.py:419
  23.1 2.6 %collective-permute-start.5 = (bf16[1,4,48,128]{3,2,1,0:T(8,128)(2,1)S(1)}, bf16[1,4,48,128]{3,2,1,0:T(8,128)(2,1)S(1)}, u32[]{:S(2)}, u32[]{:S(2)}) collective-permute-start(bf16[1,4,48,128]{3,2,1,0:T(8,128)(2,1)S(1)} %get-tuple-element.84), channel_id=1, source_target_pairs={{0,16},{4,20},{8,24},{12,28},{16,0},{20,4},{24,8},{28,12},{1,17},{... | collective-permute-start | bytes 147464 | tf_op jit(solution)/shard_map/ppermute | solution.py:419
  25.7 5.7 %collective-permute-start.6 = (bf16[1,4,48,128]{3,2,1,0:T(8,128)(2,1)S(1)}, bf16[1,4,48,128]{3,2,1,0:T(8,128)(2,1)S(1)}, u32[]{:S(2)}, u32[]{:S(2)}) collective-permute-start(bf16[1,4,48,128]{3,2,1,0:T(8,128)(2,1)S(1)} %get-tuple-element.85), channel_id=1, source_target_pairs={{0,20},{4,24},{8,28},{20,0},{24,4},{28,8},{1,21},{5,25},{9,29},{21... | collective-permute-start | bytes 147464 | tf_op jit(solution)/shard_map/ppermute | solution.py:419
  31.7 2.8 %collective-permute-done.6.refs_3_ = bf16[1,4,48,128]{3,2,1,0:T(8,128)(2,1)S(1)} collective-permute-done((bf16[1,4,48,128]{3,2,1,0:T(8,128)(2,1)S(1)}, bf16[1,4,48,128]{3,2,1,0:T(8,128)(2,1)S(1)}, u32[]{:S(2)}, u32[]{:S(2)}) %collective-permute-start.6) | collective-permute-done | bytes 49184 | tf_op jit(solution)/shard_map/ppermute | solution.py:419
  37.4 3.2 %weight_sums.2 = (f32[1024,128]{1,0:T(8,128)S(1)}, bf16[1024,128]{1,0:T(8,128)(2,1)S(1)}) custom-call(s32[1,27,16]{2,1,0:T(8,128)S(1)} %copy.15.pin_ref, bf16[48,2048]{1,0:T(8,128)(2,1)S(1)} %get-tuple-element.76.other_ref.own_ref, bf16[48,2048]{1,0:T(8,128)(2,1)S(1)} %get-tuple-element.75.refs_0_.other_ref, ...), custom_call_target="tpu_custom_call" | custom-call | flops 1019215872 | bytes 2410176 | tf_op jit(solution)/shard_map/weight_sums/pallas_call | solution.py:27
  40.6 2.5 %collective-permute-done.10.refs_2_ = bf16[48,2048]{1,0:T(8,128)(2,1)S(1)} collective-permute-done((bf16[48,2048]{1,0:T(8,128)(2,1)S(1)}, bf16[48,2048]{1,0:T(8,128)(2,1)S(1)}, u32[]{:S(2)}, u32[]{:S(2)}) %collective-permute-start.10) | collective-permute-done | bytes 196640 | tf_op jit(solution)/shard_map/ppermute | solution.py:403
  44.5 3.2 %weight_sums.3 = (f32[1024,128]{1,0:T(8,128)S(1)}, bf16[1024,128]{1,0:T(8,128)(2,1)S(1)}) custom-call(s32[1,27,16]{2,1,0:T(8,128)S(1)} %copy.15.pin_ref, bf16[48,2048]{1,0:T(8,128)(2,1)S(1)} %get-tuple-element.99.own_ref, bf16[48,2048]{1,0:T(8,128)(2,1)S(1)} %settle.2.refs_0_, bf16[48,2048]{1,0:T(8,128)(2,1)S(1)} %collective-permute-done.11.refs_1_, ...), custom_call_target="tpu_custom_call" | custom-call | flops 1019215872 | bytes 2410176 | tf_op jit(solution)/shard_map/weight_sums/pallas_call | solution.py:27
  47.8 1.7 %collective-permute-done.13.refs_1_ = bf16[1024,128]{1,0:T(8,128)(2,1)S(1)} collective-permute-done((bf16[1024,128]{1,0:T(8,128)(2,1)S(1)}, bf16[1024,128]{1,0:T(8,128)(2,1)S(1)}, u32[]{:S(2)}, u32[]{:S(2)}) %collective-permute-start.13) | collective-permute-done | bytes 262176 | tf_op jit(solution)/shard_map/ppermute | solution.py:339
  50.6 3.7 %partial_sums.3 = (f32[16,48,128]{2,1,0:T(8,128)S(1)}, bf16[1,4,48,128]{3,2,1,0:T(8,128)(2,1)S(1)}, bf16[1,4,48,128]{3,2,1,0:T(8,128)(2,1)S(1)}, bf16[1,4,48,128...) custom-call(s32[1,27,16]{2,1,0:T(8,128)S(1)} %copy.15.pin_ref, ...), custom_call_target="tpu_custom_call" | custom-call | flops 1019215872 | bytes 1924800 | tf_op jit(solution)/shard_map/partial_sums/pallas_call | solution.py:27
  57.2 4.2 %collective-permute-start.17 = (bf16[1,4,48,128]{3,2,1,0:T(8,128)(2,1)S(1)}, bf16[1,4,48,128]{3,2,1,0:T(8,128)(2,1)S(1)}, u32[]{:S(2)}, u32[]{:S(2)}) collective-permute-start(bf16[1,4,48,128]{3,2,1,0:T(8,128)(2,1)S(1)} %get-tuple-element.123), channel_id=1, source_target_pairs={{8,4},{24,20},{4,8},{20,24},{9,5},{25,21},{5,9},{21,25},{10,6},{26... | collective-permute-start | bytes 147464 | tf_op jit(solution)/shard_map/ppermute | solution.py:419
  61.4 2.7 %collective-permute-done.17.refs_1_ = bf16[1,4,48,128]{3,2,1,0:T(8,128)(2,1)S(1)} collective-permute-done((bf16[1,4,48,128]{3,2,1,0:T(8,128)(2,1)S(1)}, bf16[1,4,48,128]{3,2,1,0:T(8,128)(2,1)S(1)}, u32[]{:S(2)}, u32[]{:S(2)}) %collective-permute-start.17) | collective-permute-done | bytes 49184 | tf_op jit(solution)/shard_map/ppermute | solution.py:419
  64.1 3.6 %collective-permute-start.18 = (bf16[2,256,128]{2,1,0:T(8,128)(2,1)S(1)}, bf16[2,256,128]{2,1,0:T(8,128)(2,1)S(1)}, u32[]{:S(2)}, u32[]{:S(2)}) collective-permute-start(bf16[2,256,128]{2,1,0:T(8,128)(2,1)S(1)} %get-tuple-element.130), channel_id=1, source_target_pairs={{0,16},{1,17},{2,18},{3,19},{4,20},{5,21},{6,22},{7,23},{8,24},{9,... | collective-permute-start | bytes 393224 | tf_op jit(solution)/shard_map/ppermute | solution.py:339
  67.8 4.9 %collective-permute-done.19.refs_2_ = bf16[1,4,48,128]{3,2,1,0:T(8,128)(2,1)S(1)} collective-permute-done((bf16[1,4,48,128]{3,2,1,0:T(8,128)(2,1)S(1)}, bf16[1,4,48,128]{3,2,1,0:T(8,128)(2,1)S(1)}, u32[]{:S(2)}, u32[]{:S(2)}) %collective-permute-start.19) | collective-permute-done | bytes 49184 | tf_op jit(solution)/shard_map/ppermute | solution.py:419
  74.2 4.6 %collective-permute-start.21 = (bf16[1,4,48,128]{3,2,1,0:T(8,128)(2,1)S(1)}, bf16[1,4,48,128]{3,2,1,0:T(8,128)(2,1)S(1)}, u32[]{:S(2)}, u32[]{:S(2)}) collective-permute-start(bf16[1,4,48,128]{3,2,1,0:T(8,128)(2,1)S(1)} %get-tuple-element.137), channel_id=1, source_target_pairs={{0,20},{4,24},{8,28},{20,0},{24,4},{28,8},{1,21},{5,25},{9,29},{21... | collective-permute-start | bytes 147464 | tf_op jit(solution)/shard_map/ppermute | solution.py:419
  78.8 4.1 %collective-permute-done.21.refs_3_ = bf16[1,4,48,128]{3,2,1,0:T(8,128)(2,1)S(1)} collective-permute-done((bf16[1,4,48,128]{3,2,1,0:T(8,128)(2,1)S(1)}, bf16[1,4,48,128]{3,2,1,0:T(8,128)(2,1)S(1)}, u32[]{:S(2)}, u32[]{:S(2)}) %collective-permute-start.21) | collective-permute-done | bytes 49184 | tf_op jit(solution)/shard_map/ppermute | solution.py:419
  83.0 5.2 %collective-permute-start.23 = (bf16[1,4,48,128]{3,2,1,0:T(8,128)(2,1)S(1)}, bf16[1,4,48,128]{3,2,1,0:T(8,128)(2,1)S(1)}, u32[]{:S(2)}, u32[]{:S(2)}) collective-permute-start(bf16[1,4,48,128]{3,2,1,0:T(8,128)(2,1)S(1)} %get-tuple-element.142), channel_id=1, source_target_pairs={{4,16},{8,20},{12,24},{16,4},{20,8},{24,12},{5,17},{9,21},{13,25},... | collective-permute-start | bytes 147464 | tf_op jit(solution)/shard_map/ppermute | solution.py:419
  88.3 2.6 %collective-permute-done.23.refs_4_ = bf16[1,4,48,128]{3,2,1,0:T(8,128)(2,1)S(1)} collective-permute-done((bf16[1,4,48,128]{3,2,1,0:T(8,128)(2,1)S(1)}, bf16[1,4,48,128]{3,2,1,0:T(8,128)(2,1)S(1)}, u32[]{:S(2)}, u32[]{:S(2)}) %collective-permute-start.23) | collective-permute-done | bytes 49184 | tf_op jit(solution)/shard_map/ppermute | solution.py:419
  92.5 7.7 %collective-permute-done.24.got_ref = bf16[4,2,256,128]{3,2,1,0:T(8,128)(2,1)S(1)} collective-permute-done((bf16[4,2,256,128]{3,2,1,0:T(8,128)(2,1)S(1)}, bf16[4,2,256,128]{3,2,1,0:T(8,128)(2,1)S(1)}, u32[]{:S(2)}, u32[]{:S(2)}) %collective-permute-start.24) | collective-permute-done | bytes 524320 | tf_op jit(solution)/shard_map/ppermute | solution.py:339
  100.2 1.8 %unpack_sums.1 = (f32[1296,192]{1,0:T(8,128)}, f32[1296,192]{1,0:T(8,128)}) custom-call(bf16[4,2,256,128]{3,2,1,0:T(8,128)(2,1)S(1)} %pad_maximum_fusion.own_ref, bf16[4,2,256,128]{3,2,1,0:T(8,128)(2,1)S(1)} %collective-permute-done.24.got_ref), custom_call_target="tpu_custom_call" | custom-call | bytes 3039232 | tf_op jit(solution)/shard_map/unpack_sums/pallas_call | solution.py:27
  (43 shorter events, 16.2 us)
Async XLA Ops:
  0.6 11.7 %collective-permute-start = (bf16[48,2048]{1,0:T(8,128)(2,1)}, bf16[48,2048]{1,0:T(8,128)(2,1)S(1)}, u32[]{:S(2)}, u32[]{:S(2)}) collective-permute-start(bf16[48,2048]{1,0:T(8,128)(2,1)} %refs_2_.1), channel_id=1, source_target_pairs={{0,1},{1,0},{2,3},{3,2},{4,5},{5,4},{6,7},{7,6},{8,9},{9,8},{10,11... | collective-permute-start | bytes 589832 | tf_op jit(solution)/shard_map/ppermute | solution.py:403
  0.7 11.6 %collective-permute-start.2 = (bf16[48,2048]{1,0:T(8,128)(2,1)}, bf16[48,2048]{1,0:T(8,128)(2,1)S(1)}, u32[]{:S(2)}, u32[]{:S(2)}) collective-permute-start(bf16[48,2048]{1,0:T(8,128)(2,1)} %refs_2_.1), channel_id=1, source_target_pairs={{0,3},{1,2},{2,1},{3,0},{4,7},{5,6},{6,5},{7,4},{8,11},{9,10},{10,... | collective-permute-start | bytes 589832 | tf_op jit(solution)/shard_map/ppermute | solution.py:403
  2.3 10.1 %collective-permute-start.1 = (bf16[48,2048]{1,0:T(8,128)(2,1)}, bf16[48,2048]{1,0:T(8,128)(2,1)S(1)}, u32[]{:S(2)}, u32[]{:S(2)}) collective-permute-start(bf16[48,2048]{1,0:T(8,128)(2,1)} %refs_2_.1), channel_id=1, source_target_pairs={{0,2},{1,3},{2,0},{3,1},{4,6},{5,7},{6,4},{7,5},{8,10},{9,11},{10,... | collective-permute-start | bytes 589832 | tf_op jit(solution)/shard_map/ppermute | solution.py:403
  5.6 17.5 %collective-permute-start.8 = (bf16[2,4,48,128]{3,2,1,0:T(8,128)(2,1)S(1)}, bf16[2,4,48,128]{3,2,1,0:T(8,128)(2,1)S(1)}, u32[]{:S(2)}, u32[]{:S(2)}) collective-permute-start(bf16[2,4,48,128]{3,2,1,0:T(8,128)(2,1)S(1)} %get-tuple-element.87), channel_id=1, source_target_pairs={{16,0},{20,4},{24,8},{28,12},{0,16},{4,20},{8,24},{12,28},{17,1},{... | collective-permute-start | bytes 294920 | tf_op jit(solution)/shard_map/ppermute | solution.py:419
  8.3 17.4 %collective-permute-start.9 = (bf16[2,4,48,128]{3,2,1,0:T(8,128)(2,1)S(1)}, bf16[2,4,48,128]{3,2,1,0:T(8,128)(2,1)S(1)}, u32[]{:S(2)}, u32[]{:S(2)}) collective-permute-start(bf16[2,4,48,128]{3,2,1,0:T(8,128)(2,1)S(1)} %get-tuple-element.88), channel_id=1, source_target_pairs={{20,0},{24,4},{28,8},{0,20},{4,24},{8,28},{21,1},{25,5},{29,9},{1,... | collective-permute-start | bytes 294920 | tf_op jit(solution)/shard_map/ppermute | solution.py:419
  16.2 18.3 %collective-permute-start.3 = (bf16[3,4,48,128]{3,2,1,0:T(8,128)(2,1)S(1)}, bf16[3,4,48,128]{3,2,1,0:T(8,128)(2,1)S(1)}, u32[]{:S(2)}, u32[]{:S(2)}) collective-permute-start(bf16[3,4,48,128]{3,2,1,0:T(8,128)(2,1)S(1)} %get-tuple-element.82), channel_id=1, source_target_pairs={{4,0},{12,8},{20,16},{28,24},{0,4},{8,12},{16,20},{24,28},{5,1},{1... | collective-permute-start | bytes 442376 | tf_op jit(solution)/shard_map/ppermute | solution.py:419
  16.7 17.8 %collective-permute-start.4 = (bf16[3,4,48,128]{3,2,1,0:T(8,128)(2,1)S(1)}, bf16[3,4,48,128]{3,2,1,0:T(8,128)(2,1)S(1)}, u32[]{:S(2)}, u32[]{:S(2)}) collective-permute-start(bf16[3,4,48,128]{3,2,1,0:T(8,128)(2,1)S(1)} %get-tuple-element.83), channel_id=1, source_target_pairs={{8,4},{24,20},{4,8},{20,24},{9,5},{25,21},{5,9},{21,25},{10,6},{26... | collective-permute-start | bytes 442376 | tf_op jit(solution)/shard_map/ppermute | solution.py:419
  21.2 13.7 %collective-permute-start.7 = (bf16[3,4,48,128]{3,2,1,0:T(8,128)(2,1)S(1)}, bf16[3,4,48,128]{3,2,1,0:T(8,128)(2,1)S(1)}, u32[]{:S(2)}, u32[]{:S(2)}) collective-permute-start(bf16[3,4,48,128]{3,2,1,0:T(8,128)(2,1)S(1)} %get-tuple-element.86), channel_id=1, source_target_pairs={{4,16},{8,20},{12,24},{16,4},{20,8},{24,12},{5,17},{9,21},{13,25},... | collective-permute-start | bytes 442376 | tf_op jit(solution)/shard_map/ppermute | solution.py:419
  23.1 8.6 %collective-permute-start.5 = (bf16[1,4,48,128]{3,2,1,0:T(8,128)(2,1)S(1)}, bf16[1,4,48,128]{3,2,1,0:T(8,128)(2,1)S(1)}, u32[]{:S(2)}, u32[]{:S(2)}) collective-permute-start(bf16[1,4,48,128]{3,2,1,0:T(8,128)(2,1)S(1)} %get-tuple-element.84), channel_id=1, source_target_pairs={{0,16},{4,20},{8,24},{12,28},{16,0},{20,4},{24,8},{28,12},{1,17},{... | collective-permute-start | bytes 147464 | tf_op jit(solution)/shard_map/ppermute | solution.py:419
  25.7 8.8 %collective-permute-start.6 = (bf16[1,4,48,128]{3,2,1,0:T(8,128)(2,1)S(1)}, bf16[1,4,48,128]{3,2,1,0:T(8,128)(2,1)S(1)}, u32[]{:S(2)}, u32[]{:S(2)}) collective-permute-start(bf16[1,4,48,128]{3,2,1,0:T(8,128)(2,1)S(1)} %get-tuple-element.85), channel_id=1, source_target_pairs={{0,20},{4,24},{8,28},{20,0},{24,4},{28,8},{1,21},{5,25},{9,29},{21... | collective-permute-start | bytes 147464 | tf_op jit(solution)/shard_map/ppermute | solution.py:419
  35.7 4.9 %collective-permute-start.11 = (bf16[48,2048]{1,0:T(8,128)(2,1)S(1)}, bf16[48,2048]{1,0:T(8,128)(2,1)S(1)}, u32[]{:S(2)}, u32[]{:S(2)}) collective-permute-start(bf16[48,2048]{1,0:T(8,128)(2,1)S(1)} %settle.2.refs_0_), channel_id=1, source_target_pairs={{0,1},{1,0},{2,3},{3,2},{4,5},{5,4},{6,7},{7,6},{8,9},{9,8},{10,11... | collective-permute-start | bytes 589832 | tf_op jit(solution)/shard_map/ppermute | solution.py:403
  35.8 7.3 %collective-permute-start.10 = (bf16[48,2048]{1,0:T(8,128)(2,1)S(1)}, bf16[48,2048]{1,0:T(8,128)(2,1)S(1)}, u32[]{:S(2)}, u32[]{:S(2)}) collective-permute-start(bf16[48,2048]{1,0:T(8,128)(2,1)S(1)} %settle.2.refs_0_), channel_id=1, source_target_pairs={{0,2},{1,3},{2,0},{3,1},{4,6},{5,7},{6,4},{7,5},{8,10},{9,11},{10,... | collective-permute-start | bytes 589832 | tf_op jit(solution)/shard_map/ppermute | solution.py:403
  43.1 6.4 %collective-permute-start.13 = (bf16[1024,128]{1,0:T(8,128)(2,1)S(1)}, bf16[1024,128]{1,0:T(8,128)(2,1)S(1)}, u32[]{:S(2)}, u32[]{:S(2)}) collective-permute-start(bf16[1024,128]{1,0:T(8,128)(2,1)S(1)} %get-tuple-element.107), channel_id=1, source_target_pairs={{0,4},{1,9},{2,6},{3,11},{4,0},{5,13},{6,2},{7,15},{8,12},{9,1},{1... | collective-permute-start | bytes 786440 | tf_op jit(solution)/shard_map/ppermute | solution.py:339
  49.5 6.4 %collective-permute-start.14 = (bf16[1024,128]{1,0:T(8,128)(2,1)S(1)}, bf16[1024,128]{1,0:T(8,128)(2,1)S(1)}, u32[]{:S(2)}, u32[]{:S(2)}) collective-permute-start(bf16[1024,128]{1,0:T(8,128)(2,1)S(1)} %get-tuple-element.111), channel_id=1, source_target_pairs={{0,4},{1,9},{2,6},{3,11},{4,0},{5,13},{6,2},{7,15},{8,12},{9,1},{1... | collective-permute-start | bytes 786440 | tf_op jit(solution)/shard_map/ppermute | solution.py:339
  55.9 8.2 %collective-permute-start.15 = (bf16[2,512,128]{2,1,0:T(8,128)(2,1)S(1)}, bf16[2,512,128]{2,1,0:T(8,128)(2,1)S(1)}, u32[]{:S(2)}, u32[]{:S(2)}) collective-permute-start(bf16[2,512,128]{2,1,0:T(8,128)(2,1)S(1)} %get-tuple-element.121), channel_id=1, source_target_pairs={{0,8},{1,5},{2,10},{3,7},{4,12},{5,1},{6,14},{7,3},{8,0},{9,13},{1... | collective-permute-start | bytes 786440 | tf_op jit(solution)/shard_map/ppermute | solution.py:339
  56.0 5.4 %collective-permute-start.16 = (bf16[1,4,48,128]{3,2,1,0:T(8,128)(2,1)S(1)}, bf16[1,4,48,128]{3,2,1,0:T(8,128)(2,1)S(1)}, u32[]{:S(2)}, u32[]{:S(2)}) collective-permute-start(bf16[1,4,48,128]{3,2,1,0:T(8,128)(2,1)S(1)} %get-tuple-element.122), channel_id=1, source_target_pairs={{4,0},{12,8},{20,16},{28,24},{0,4},{8,12},{16,20},{24,28},{5,1},{1... | collective-permute-start | bytes 147464 | tf_op jit(solution)/shard_map/ppermute | solution.py:419
  57.2 6.9 %collective-permute-start.17 = (bf16[1,4,48,128]{3,2,1,0:T(8,128)(2,1)S(1)}, bf16[1,4,48,128]{3,2,1,0:T(8,128)(2,1)S(1)}, u32[]{:S(2)}, u32[]{:S(2)}) collective-permute-start(bf16[1,4,48,128]{3,2,1,0:T(8,128)(2,1)S(1)} %get-tuple-element.123), channel_id=1, source_target_pairs={{8,4},{24,20},{4,8},{20,24},{9,5},{25,21},{5,9},{21,25},{10,6},{26... | collective-permute-start | bytes 147464 | tf_op jit(solution)/shard_map/ppermute | solution.py:419
  64.1 8.6 %collective-permute-start.18 = (bf16[2,256,128]{2,1,0:T(8,128)(2,1)S(1)}, bf16[2,256,128]{2,1,0:T(8,128)(2,1)S(1)}, u32[]{:S(2)}, u32[]{:S(2)}) collective-permute-start(bf16[2,256,128]{2,1,0:T(8,128)(2,1)S(1)} %get-tuple-element.130), channel_id=1, source_target_pairs={{0,16},{1,17},{2,18},{3,19},{4,20},{5,21},{6,22},{7,23},{8,24},{9,... | collective-permute-start | bytes 393224 | tf_op jit(solution)/shard_map/ppermute | solution.py:339
  67.7 5.0 %collective-permute-start.19 = (bf16[1,4,48,128]{3,2,1,0:T(8,128)(2,1)S(1)}, bf16[1,4,48,128]{3,2,1,0:T(8,128)(2,1)S(1)}, u32[]{:S(2)}, u32[]{:S(2)}) collective-permute-start(bf16[1,4,48,128]{3,2,1,0:T(8,128)(2,1)S(1)} %get-tuple-element.131), channel_id=1, source_target_pairs={{0,16},{4,20},{8,24},{12,28},{16,0},{20,4},{24,8},{28,12},{1,17},{... | collective-permute-start | bytes 147464 | tf_op jit(solution)/shard_map/ppermute | solution.py:419
  72.8 10.2 %collective-permute-start.20 = (bf16[1,2,256,128]{3,2,1,0:T(8,128)(2,1)S(1)}, bf16[1,2,256,128]{3,2,1,0:T(8,128)(2,1)S(1)}, u32[]{:S(2)}, u32[]{:S(2)}) collective-permute-start(bf16[1,2,256,128]{3,2,1,0:T(8,128)(2,1)S(1)} %fusion), channel_id=1, source_target_pairs={{0,16},{1,17},{2,18},{3,19},{4,20},{5,21},{6,22},{7,23},{8,24},{9,... | collective-permute-start | bytes 393224 | tf_op jit(solution)/shard_map/ppermute | solution.py:339
  74.2 8.7 %collective-permute-start.21 = (bf16[1,4,48,128]{3,2,1,0:T(8,128)(2,1)S(1)}, bf16[1,4,48,128]{3,2,1,0:T(8,128)(2,1)S(1)}, u32[]{:S(2)}, u32[]{:S(2)}) collective-permute-start(bf16[1,4,48,128]{3,2,1,0:T(8,128)(2,1)S(1)} %get-tuple-element.137), channel_id=1, source_target_pairs={{0,20},{4,24},{8,28},{20,0},{24,4},{28,8},{1,21},{5,25},{9,29},{21... | collective-permute-start | bytes 147464 | tf_op jit(solution)/shard_map/ppermute | solution.py:419
  83.0 8.0 %collective-permute-start.22 = (bf16[2,2,256,128]{3,2,1,0:T(8,128)(2,1)S(1)}, bf16[2,2,256,128]{3,2,1,0:T(8,128)(2,1)S(1)}, u32[]{:S(2)}, u32[]{:S(2)}) collective-permute-start(bf16[2,2,256,128]{3,2,1,0:T(8,128)(2,1)S(1)} %pad_maximum_fusion.1), channel_id=1, source_target_pairs={{0,8},{1,5},{2,10},{3,7},{4,12},{5,1},{6,14},{7,3},{8,0},{9,13},{1... | collective-permute-start | bytes 786440 | tf_op jit(solution)/shard_map/ppermute | solution.py:339
  83.0 7.9 %collective-permute-start.23 = (bf16[1,4,48,128]{3,2,1,0:T(8,128)(2,1)S(1)}, bf16[1,4,48,128]{3,2,1,0:T(8,128)(2,1)S(1)}, u32[]{:S(2)}, u32[]{:S(2)}) collective-permute-start(bf16[1,4,48,128]{3,2,1,0:T(8,128)(2,1)S(1)} %get-tuple-element.142), channel_id=1, source_target_pairs={{4,16},{8,20},{12,24},{16,4},{20,8},{24,12},{5,17},{9,21},{13,25},... | collective-permute-start | bytes 147464 | tf_op jit(solution)/shard_map/ppermute | solution.py:419
  91.0 9.2 %collective-permute-start.24 = (bf16[4,2,256,128]{3,2,1,0:T(8,128)(2,1)S(1)}, bf16[4,2,256,128]{3,2,1,0:T(8,128)(2,1)S(1)}, u32[]{:S(2)}, u32[]{:S(2)}) collective-permute-start(bf16[4,2,256,128]{3,2,1,0:T(8,128)(2,1)S(1)} %pad_maximum_fusion.own_ref), channel_id=1, source_target_pairs={{0,4},{1,9},{2,6},{3,11},{4,0},{5,13},{6,2},{7,15},{8,12},{9,1},{1... | collective-permute-start | bytes 1572872 | tf_op jit(solution)/shard_map/ppermute | solution.py:339
  (2 other events, 7.5 us)

commit v4 on v3

--- a/solution.py
+++ b/solution.py
@@ -213,10 +213,11 @@
     return -(-(rows + rows // 2) // step) * step
 
 
-def weight_kernel(plan, which, factor, pin_ref, own_ref, *refs):
+def weight_kernel(plan, which, factor, pieces, pin_ref, own_ref, *refs):
     parts, refs = refs[:4], refs[4:]
     ghost_refs, refs = refs[: plan.shape[0]], refs[plan.shape[0] :]
-    keep_ref, send_ref, full, extended, gathered, wide, tall = refs
+    piece_refs, refs = refs[:pieces], refs[pieces:]
+    full, extended, gathered, wide, tall = refs
     offset_count, block_count = pin_ref.shape[1:]
     width = own_ref.shape[0]
     gather_full(parts, full)
@@ -252,13 +253,14 @@
     tall[rows : rows + half, 64:] = wide[half:, 128:192]
     if tall.shape[0] > rows + half:
         tall[rows + half :] = jnp.zeros((tall.shape[0] - rows - half, 128), F32)
-    bit = exchange_bit(0)
-    split = tall.shape[0] // 2
-    keep_ref[...] = tall[pl.ds(pl.multiple_of(bit * split, 16), split), :]
-    send_ref[...] = tall[pl.ds(pl.multiple_of((1 - bit) * split, 16), split), :].astype(BF16)
-
-
-def weight_sums(pin, plan, parts, own, ghosts, which, factor, tile_count):
+    split = tall.shape[0] // pieces
+    mine = exchange_bit(0) if pieces == 2 else 2 * exchange_bit(0) + exchange_bit(1)
+    for index, piece_ref in enumerate(piece_refs):
+        piece = tall[pl.ds(pl.multiple_of((mine ^ index) * split, 16), split), :]
+        piece_ref[...] = piece.astype(piece_ref.dtype)
+
+
+def weight_sums(pin, plan, parts, own, ghosts, which, factor, tile_count, pieces):
     width, voxels = own.shape
     offset_count, block_count = pin.shape[1:]
     slot_count = ghosts[0].shape[1]
@@ -266,11 +268,11 @@
     chunk = 9 if offset_count % 9 == 0 else 1
     rows = offset_count * width
     tall = packed_rows(rows, tile_count)
-    shape = (tall // 2, 128)
+    shape = (tall // pieces, 128)
     return call(
-        functools.partial(weight_kernel, plan, which, factor),
+        functools.partial(weight_kernel, plan, which, factor, pieces),
         "weight_sums",
-        [struct(shape, F32), struct(shape, BF16)],
+        [struct(shape, F32)] + [struct(shape, BF16)] * (pieces - 1),
         "S",
         (pin, own, *parts, *ghosts),
         [
@@ -328,57 +330,74 @@
     return lax.shift_right_logical(lax.axis_index("tile"), exchange_dim(step)) & 1
 
 
-def trade(value, step):
+def trade(value, *steps):
     tile_count = lax.axis_size("tile")
     chan_count = lax.axis_size("chan")
     pairs = []
     for tile in range(tile_count):
         for chan in range(chan_count):
-            dim = (1 - step if chan % 2 else step) if step < 2 else step
-            pairs.append((tile * chan_count + chan, (tile ^ (1 << dim)) * chan_count + chan))
+            dims = [(1 - step if chan % 2 else step) if step < 2 else step for step in steps]
+            other = tile ^ sum(1 << dim for dim in dims)
+            pairs.append((tile * chan_count + chan, other * chan_count + chan))
     return lax.ppermute(value, ("tile", "chan"), pairs)
 
 
-def halve_kernel(step, *refs):
-    *pair_refs, next_ref, send_ref = refs
+def halve_kernel(step, sources, *refs):
+    *_, next_ref, send_ref = refs
     bit = exchange_bit(step)
     split = next_ref.shape[1]
     mine = pl.ds(pl.multiple_of(bit * split, 16), split)
     theirs = pl.ds(pl.multiple_of((1 - bit) * split, 16), split)
-    for index in range(2):
-        if len(pair_refs) == 4:
-            keep, got = pair_refs[2 * index : 2 * index + 2]
-        else:
-            keep, got = (ref.at[index] for ref in pair_refs)
-        next_ref[index] = keep[mine, :] + got[mine, :].astype(F32)
-        send_ref[index] = (keep[theirs, :] + got[theirs, :].astype(F32)).astype(BF16)
-
-
-def halve(step, *pairs):
-    shape = (2, pairs[0].shape[-2] // 2, 128)
+    for index, terms in enumerate(sources):
+        views = [refs[term] if part is None else refs[term].at[part] for term, part in terms]
+        next_ref[index] = sum(view[mine, :].astype(F32) for view in views)
+        send_ref[index] = sum(view[theirs, :].astype(F32) for view in views).astype(BF16)
+
+
+def halve(step, sources, *args):
+    shape = (len(sources), args[0].shape[-2] // 2, 128)
     return call(
-        functools.partial(halve_kernel, step),
+        functools.partial(halve_kernel, step, sources),
         "halve",
         [struct(shape, F32), struct(shape, BF16)],
         "",
-        pairs,
-        flops=2 * pairs[0].size,
-    )
-
-
-def unpack_kernel(tile_count, own_ref, got_ref, *refs):
-    *out_refs, tall = refs
+        args,
+        flops=2 * args[0].size,
+    )
+
+
+def merge_kernel(keep_ref, got_ref, other_ref, next_ref, send_ref):
+    bit = exchange_bit(1)
+    split = next_ref.shape[0]
+    mine = pl.ds(pl.multiple_of(bit * split, 16), split)
+    theirs = pl.ds(pl.multiple_of((1 - bit) * split, 16), split)
+    next_ref[...] = keep_ref[mine, :] + got_ref[mine, :].astype(F32)
+    send_ref[0] = (keep_ref[theirs, :] + got_ref[theirs, :].astype(F32)).astype(BF16)
+    send_ref[1] = other_ref[...]
+
+
+def merge(keep, got, other):
+    return call(
+        merge_kernel,
+        "merge_sends",
+        [struct(other.shape, F32), struct((2,) + other.shape, BF16)],
+        "",
+        (keep, got, other),
+        flops=keep.size,
+    )
+
+
+def unpack_kernel(tile_count, *refs):
+    quarters, out_refs, tall = refs[:4], refs[4:-1], refs[-1]
     steps = tile_count.bit_length() - 1
-    chunk = own_ref.shape[2]
+    count, _, chunk, _ = quarters[0].shape
     mine = 0
     for step in range(steps):
         mine = mine * 2 + exchange_bit(step)
-    half_count = tile_count // 2
     for part, out_ref in enumerate(out_refs):
         for index in range(tile_count):
-            source = own_ref if index < half_count else got_ref
             rows = pl.ds(pl.multiple_of((mine ^ index) * chunk, 16), chunk)
-            tall[rows, :] = source[index % half_count, part].astype(F32)
+            tall[rows, :] = quarters[index // count][index % count, part].astype(F32)
         rows = out_ref.shape[0]
         half = rows // 2
         out_ref[:, :128] = tall[:rows]
@@ -386,15 +405,15 @@
         out_ref[half:, 128:192] = tall[rows : rows + half, 64:]
 
 
-def unpack(own, got, rows, columns):
-    tile_count = 2 * own.shape[0]
+def unpack(quarters, rows, columns):
+    tile_count = 4 * quarters[0].shape[0]
     return call(
         functools.partial(unpack_kernel, tile_count),
         "unpack_sums",
-        [struct((rows, columns), F32)] * own.shape[1],
+        [struct((rows, columns), F32)] * quarters[0].shape[1],
         "",
-        (own, got),
-        [VMEM((tile_count * own.shape[2], 128), F32)],
+        quarters,
+        [VMEM((tile_count * quarters[0].shape[2], 128), F32)],
         vmem_mib=8,
     )
 
@@ -438,19 +457,23 @@
     for group, ghost in zip(early, soon):
         ghosts[group] = ghost
     far, near = swap_part(grad_pre, 2), swap_part(grad_pre, 1)
-    keep_two, send = weight_sums(pair_in, plan, cot_parts, pre_act, ghosts, 0, factor, tile_count)
-    far, near, send = tie(far, near, send)
+    keep_two, send = weight_sums(
+        pair_in, plan, cot_parts, pre_act, ghosts, 0, factor, tile_count, 2
+    )
     got_two = trade(send, 0)
+    far, near, sent = tie(far, near, send)
     pre_parts = (grad_pre, near, far, swap_part(far, 1))
-    keep_one, send = weight_sums(
-        pair_in, plan, pre_parts, features, ghosts, 1, factor, tile_count
-    )
-    got_two, send = tie(got_two, send)
-    got = trade(send, 0)
+    keep_one, across_one, across_zero, across_both = weight_sums(
+        pair_in, plan, pre_parts, features, ghosts, 1, factor, tile_count, 4
+    )
+    got_two, across_one = tie(got_two, across_one)
+    got_zero, got_both = trade(across_zero, 0), trade(across_both, 0, 1)
+    keep_two, send = merge(keep_two, got_two, across_one)
+    got_one = trade(send, 1)
     pre_parts, keep_one = tie(pre_parts, keep_one)
     local_one, backs = partial_sums(pair_in, plan, pre_parts, weight_one, slot_count)
-    got, backs = tie(got, backs)
-    shares = [[0, 1]] + [[g] for g in range(2, len(backs))]
+    got_one, backs = tie(got_one, backs)
+    shares = [[0, 1], [2], list(range(3, len(backs)))]
     returned = [None] * len(backs)
 
     def beside(value, step):
@@ -461,18 +484,23 @@
             returned[group] = back
         return got
 
-    arrived = (keep_two, got_two, keep_one, got)
-    for step in range(1, steps):
-        keep, send = halve(step, *arrived)
+    arrived = (keep_two, got_one, keep_one, got_zero, got_both)
+    sources = (((0, None), (1, 0)), ((2, None), (1, 1), (3, None), (4, None)))
+    for step in range(2, steps):
+        keep, send = halve(step, sources, *arrived)
         got = beside(send, step)
-        arrived = (keep, got)
+        arrived, sources = (keep, got), tuple(((0, part), (1, part)) for part in range(2))
     chunk = (keep + got.astype(F32)).astype(BF16)[None]
-    for step in reversed(range(1, steps)):
+    for step in reversed(range(2, steps)):
         got = beside(chunk, step)
         chunk = jnp.concatenate([chunk, got], axis=0)
-    got = trade(chunk, 0)
+    share = sum(shares, [])
+    chunk, mine = tie(chunk, [backs[g] for g in share])
+    quarters = (chunk, trade(chunk, 1), trade(chunk, 0), trade(chunk, 0, 1))
+    for group, back in zip(share, give(mine, [back_lists[g] for g in share])):
+        returned[group] = back
     grad_features = settle(False, send_list, plan, local_one, cotangent, returned)
-    sum_two, sum_one = unpack(chunk, got, rows, columns)
+    sum_two, sum_one = unpack(quarters, rows, columns)
     shape = (offset_count, width, columns)
     return grad_features, sum_one.reshape(shape), sum_two.reshape(shape)
 

time: 103 us -> 96.7 us (0.939)
  waiting for transfers between devices: 31.6 us -> 24.5 us
  starting transfers between devices: 47.8 us -> 49.1 us
    ppermute x7 -> x9, waiting for transfers between devices: 10.9 us -> 4.92 us  [trade(): return lax.ppermute(value, ('tile', 'chan'), pairs)]
    ppermute x7 -> x9, starting transfers between devices: 7.55 us -> 11.4 us  [trade(): return lax.ppermute(value, ('tile', 'chan'), pairs)]
    ppermute x12, starting transfers between devices: 36.4 us -> 33.8 us  [give(): return [lax.ppermute(v, 'tile', p) for v, p in zip(values, lists)]]
    ppermute x12, waiting for transfers between devices: 17.8 us -> 16.7 us  [give(): return [lax.ppermute(v, 'tile', p) for v, p in zip(values, lists)]]
  transfers between devices with their start and end apart: 25 -> 27, of which waited for: 13 -> 13; matrix products, arithmetic and copies ran while one was open for 2% -> 2% of each run, Pallas kernels for 17% -> 18%
where the time goes in v4:
time: 96.7 us; the launch traced here: 96.3 us
  starting transfers between devices  49.1 us (51%)
  waiting for transfers between devices  24.5 us (25%)
  Pallas kernels  20.2 us (21%)
  local copies, waits for them, and re-layouts  1.54 us (2%)
    ppermute x12, starting transfers between devices, give(): return [lax.ppermute(v, 'tile', p) for v, p in zip(values, lists)]  33.8 us
    pallas_call x10, Pallas kernels, call(): pl.pallas_call(kernel, out_shape=list(outs), in_specs=[pl.BlockSpec(memor...  20.2 us
    ppermute x12, waiting for transfers between devices, give(): return [lax.ppermute(v, 'tile', p) for v, p in zip(values, lists)]  16.7 us
    ppermute x9, starting transfers between devices, trade(): return lax.ppermute(value, ('tile', 'chan'), pairs)  11.4 us
    ppermute x9, waiting for transfers between devices, trade(): return lax.ppermute(value, ('tile', 'chan'), pairs)  4.92 us
    ppermute x6, starting transfers between devices, swap_part(): return lax.ppermute(value, 'chan', [(i, i ^ bits) for i in range(4)])  3.87 us
    ppermute x6, waiting for transfers between devices, swap_part(): return lax.ppermute(value, 'chan', [(i, i ^ bits) for i in range(4)])  2.87 us
  transfers between devices with their start and end apart: 27, of which 13 were waited for; matrix products, arithmetic and copies ran while one was open for 2% of the time, Pallas kernels for 18%

profile of v4, /device:TPU:2, one launch (start us, length us, event | category | flops | bytes accessed | tf_op | source)
XLA Modules:
  0.0 96.3 jit_solution(2368488859171502805)
XLA Ops:
  3.6 2.0 %pack_sends.1 = (bf16[2,4,48,128]{3,2,1,0:T(8,128)(2,1)S(1)}, bf16[2,4,48,128]{3,2,1,0:T(8,128)(2,1)S(1)}, bf16[2,4,48,128]{3,2,1,0:T(8,128)(2,1)S(1)}, bf16[2,4...) custom-call(s32[1,8,4]{2,1,0:T(8,128)S(1)} %copy.16.lists_ref, ...), custom_call_target="tpu_custom_call" | custom-call | bytes 2666624 | tf_op jit(solution)/shard_map/pack_sends/pallas_call | solution.py:27
  5.6 2.7 %collective-permute-start.8 = (bf16[2,4,48,128]{3,2,1,0:T(8,128)(2,1)S(1)}, bf16[2,4,48,128]{3,2,1,0:T(8,128)(2,1)S(1)}, u32[]{:S(2)}, u32[]{:S(2)}) collective-permute-start(bf16[2,4,48,128]{3,2,1,0:T(8,128)(2,1)S(1)} %get-tuple-element.83), channel_id=1, source_target_pairs={{16,0},{20,4},{24,8},{28,12},{0,16},{4,20},{8,24},{12,28},{17,1},{... | collective-permute-start | bytes 294920 | tf_op jit(solution)/shard_map/ppermute | solution.py:438
  8.3 3.2 %collective-permute-start.9 = (bf16[2,4,48,128]{3,2,1,0:T(8,128)(2,1)S(1)}, bf16[2,4,48,128]{3,2,1,0:T(8,128)(2,1)S(1)}, u32[]{:S(2)}, u32[]{:S(2)}) collective-permute-start(bf16[2,4,48,128]{3,2,1,0:T(8,128)(2,1)S(1)} %get-tuple-element.84), channel_id=1, source_target_pairs={{20,0},{24,4},{28,8},{0,20},{4,24},{8,28},{21,1},{25,5},{29,9},{1,... | collective-permute-start | bytes 294920 | tf_op jit(solution)/shard_map/ppermute | solution.py:438
  12.4 3.8 %partial_sums.2 = (f32[16,48,128]{2,1,0:T(8,128)S(1)}, bf16[3,4,48,128]{3,2,1,0:T(8,128)(2,1)S(1)}, bf16[3,4,48,128]{3,2,1,0:T(8,128)(2,1)S(1)}, bf16[1,4,48,128...) custom-call(s32[1,27,16]{2,1,0:T(8,128)S(1)} %copy.15.pin_ref, ...), custom_call_target="tpu_custom_call" | custom-call | flops 1019215872 | bytes 2514624 | tf_op jit(solution)/shard_map/partial_sums/pallas_call | solution.py:27
  16.6 4.5 %collective-permute-start.4 = (bf16[3,4,48,128]{3,2,1,0:T(8,128)(2,1)S(1)}, bf16[3,4,48,128]{3,2,1,0:T(8,128)(2,1)S(1)}, u32[]{:S(2)}, u32[]{:S(2)}) collective-permute-start(bf16[3,4,48,128]{3,2,1,0:T(8,128)(2,1)S(1)} %get-tuple-element.79), channel_id=1, source_target_pairs={{8,4},{24,20},{4,8},{20,24},{9,5},{25,21},{5,9},{21,25},{10,6},{26... | collective-permute-start | bytes 442376 | tf_op jit(solution)/shard_map/ppermute | solution.py:438
  21.1 1.9 %collective-permute-start.7 = (bf16[3,4,48,128]{3,2,1,0:T(8,128)(2,1)S(1)}, bf16[3,4,48,128]{3,2,1,0:T(8,128)(2,1)S(1)}, u32[]{:S(2)}, u32[]{:S(2)}) collective-permute-start(bf16[3,4,48,128]{3,2,1,0:T(8,128)(2,1)S(1)} %get-tuple-element.82), channel_id=1, source_target_pairs={{4,16},{8,20},{12,24},{16,4},{20,8},{24,12},{5,17},{9,21},{13,25},... | collective-permute-start | bytes 442376 | tf_op jit(solution)/shard_map/ppermute | solution.py:438
  23.0 2.7 %collective-permute-start.5 = (bf16[1,4,48,128]{3,2,1,0:T(8,128)(2,1)S(1)}, bf16[1,4,48,128]{3,2,1,0:T(8,128)(2,1)S(1)}, u32[]{:S(2)}, u32[]{:S(2)}) collective-permute-start(bf16[1,4,48,128]{3,2,1,0:T(8,128)(2,1)S(1)} %get-tuple-element.80), channel_id=1, source_target_pairs={{0,16},{4,20},{8,24},{12,28},{16,0},{20,4},{24,8},{28,12},{1,17},{... | collective-permute-start | bytes 147464 | tf_op jit(solution)/shard_map/ppermute | solution.py:438
  25.7 5.7 %collective-permute-start.6 = (bf16[1,4,48,128]{3,2,1,0:T(8,128)(2,1)S(1)}, bf16[1,4,48,128]{3,2,1,0:T(8,128)(2,1)S(1)}, u32[]{:S(2)}, u32[]{:S(2)}) collective-permute-start(bf16[1,4,48,128]{3,2,1,0:T(8,128)(2,1)S(1)} %get-tuple-element.81), channel_id=1, source_target_pairs={{0,20},{4,24},{8,28},{20,0},{24,4},{28,8},{1,21},{5,25},{9,29},{21... | collective-permute-start | bytes 147464 | tf_op jit(solution)/shard_map/ppermute | solution.py:438
  31.8 2.8 %collective-permute-done.6.refs_3_ = bf16[1,4,48,128]{3,2,1,0:T(8,128)(2,1)S(1)} collective-permute-done((bf16[1,4,48,128]{3,2,1,0:T(8,128)(2,1)S(1)}, bf16[1,4,48,128]{3,2,1,0:T(8,128)(2,1)S(1)}, u32[]{:S(2)}, u32[]{:S(2)}) %collective-permute-start.6) | collective-permute-done | bytes 49184 | tf_op jit(solution)/shard_map/ppermute | solution.py:438
  37.3 3.3 %weight_sums.2 = (f32[1024,128]{1,0:T(8,128)S(1)}, bf16[1024,128]{1,0:T(8,128)(2,1)S(1)}) custom-call(s32[1,27,16]{2,1,0:T(8,128)S(1)} %copy.15.pin_ref, bf16[48,2048]{1,0:T(8,128)(2,1)S(1)} %get-tuple-element.72.other_ref.own_ref, bf16[48,2048]{1,0:T(8,128)(2,1)S(1)} %get-tuple-element.71.refs_0_.other_ref, ...), custom_call_target="tpu_custom_call" | custom-call | flops 1019215872 | bytes 2410176 | tf_op jit(solution)/shard_map/weight_sums/pallas_call | solution.py:27
  40.5 2.4 %collective-permute-done.10.refs_2_ = bf16[48,2048]{1,0:T(8,128)(2,1)S(1)} collective-permute-done((bf16[48,2048]{1,0:T(8,128)(2,1)S(1)}, bf16[48,2048]{1,0:T(8,128)(2,1)S(1)}, u32[]{:S(2)}, u32[]{:S(2)}) %collective-permute-start.10) | collective-permute-done | bytes 196640 | tf_op jit(solution)/shard_map/ppermute | solution.py:422
  44.4 3.2 %weight_sums.3 = (f32[512,128]{1,0:T(8,128)S(1)}, bf16[512,128]{1,0:T(8,128)(2,1)S(1)}, bf16[512,128]{1,0:T(8,128)(2,1)S(1)}, bf16[512,128]{1,0:T(8,128)(2,1)S(1)}) custom-call(s32[1,27,16]{2,1,0:T(8,128)S(1)} %copy.15.pin_ref, bf16[48,2048]{1,0:T(8,128)(2,1)S(1)} %get-tuple-element.95.own_ref, bf16[48,2048]{1,0:T(8,128)(2,1)S(1)} %settle.2.refs_0_, ...), custom_call_target="tpu_custom_call" | custom-call | flops 1019215872 | bytes 2279104 | tf_op jit(solution)/shard_map/weight_sums/pallas_call | solution.py:27
  50.7 2.3 %collective-permute-start.16 = (bf16[512,128]{1,0:T(8,128)(2,1)S(1)}, bf16[512,128]{1,0:T(8,128)(2,1)S(1)}, u32[]{:S(2)}, u32[]{:S(2)}) collective-permute-start(bf16[512,128]{1,0:T(8,128)(2,1)S(1)} %get-tuple-element.116), channel_id=1, source_target_pairs={{0,12},{1,13},{2,14},{3,15},{4,8},{5,9},{6,10},{7,11},{8,4},{9,5},... | collective-permute-start | bytes 393224 | tf_op jit(solution)/shard_map/ppermute | solution.py:342
  53.0 3.8 %partial_sums.3 = (f32[16,48,128]{2,1,0:T(8,128)S(1)}, bf16[1,4,48,128]{3,2,1,0:T(8,128)(2,1)S(1)}, bf16[1,4,48,128]{3,2,1,0:T(8,128)(2,1)S(1)}, bf16[1,4,48,128...) custom-call(s32[1,27,16]{2,1,0:T(8,128)S(1)} %copy.15.pin_ref, ...), custom_call_target="tpu_custom_call" | custom-call | flops 1019215872 | bytes 1924800 | tf_op jit(solution)/shard_map/partial_sums/pallas_call | solution.py:27
  62.2 4.1 %collective-permute-start.19 = (bf16[1,4,48,128]{3,2,1,0:T(8,128)(2,1)S(1)}, bf16[1,4,48,128]{3,2,1,0:T(8,128)(2,1)S(1)}, u32[]{:S(2)}, u32[]{:S(2)}) collective-permute-start(bf16[1,4,48,128]{3,2,1,0:T(8,128)(2,1)S(1)} %get-tuple-element.122), channel_id=1, source_target_pairs={{8,4},{24,20},{4,8},{20,24},{9,5},{25,21},{5,9},{21,25},{10,6},{26... | collective-permute-start | bytes 147464 | tf_op jit(solution)/shard_map/ppermute | solution.py:438
  66.4 2.7 %collective-permute-done.19.refs_1_ = bf16[1,4,48,128]{3,2,1,0:T(8,128)(2,1)S(1)} collective-permute-done((bf16[1,4,48,128]{3,2,1,0:T(8,128)(2,1)S(1)}, bf16[1,4,48,128]{3,2,1,0:T(8,128)(2,1)S(1)}, u32[]{:S(2)}, u32[]{:S(2)}) %collective-permute-start.19) | collective-permute-done | bytes 49184 | tf_op jit(solution)/shard_map/ppermute | solution.py:438
  69.1 2.0 %collective-permute-start.20 = (bf16[1,2,256,128]{3,2,1,0:T(8,128)(2,1)S(1)}, bf16[1,2,256,128]{3,2,1,0:T(8,128)(2,1)S(1)}, u32[]{:S(2)}, u32[]{:S(2)}) collective-permute-start(bf16[1,2,256,128]{3,2,1,0:T(8,128)(2,1)S(1)} %fusion), channel_id=1, source_target_pairs={{0,16},{1,17},{2,18},{3,19},{4,20},{5,21},{6,22},{7,23},{8,24},{9,... | collective-permute-start | bytes 393224 | tf_op jit(solution)/shard_map/ppermute | solution.py:342
  72.1 4.8 %collective-permute-done.21.refs_2_ = bf16[1,4,48,128]{3,2,1,0:T(8,128)(2,1)S(1)} collective-permute-done((bf16[1,4,48,128]{3,2,1,0:T(8,128)(2,1)S(1)}, bf16[1,4,48,128]{3,2,1,0:T(8,128)(2,1)S(1)}, u32[]{:S(2)}, u32[]{:S(2)}) %collective-permute-start.21) | collective-permute-done | bytes 49184 | tf_op jit(solution)/shard_map/ppermute | solution.py:438
  77.0 1.7 %collective-permute-start.26 = (bf16[2,2,256,128]{3,2,1,0:T(8,128)(2,1)S(1)}, bf16[2,2,256,128]{3,2,1,0:T(8,128)(2,1)S(1)}, u32[]{:S(2)}, u32[]{:S(2)}) collective-permute-start(bf16[2,2,256,128]{3,2,1,0:T(8,128)(2,1)S(1)} %pad_maximum_fusion.refs_0_), channel_id=1, source_target_pairs={{0,12},{1,13},{2,14},{3,15},{4,8},{5,9},{6,10},{7,11},{8,4},{9,5},... | collective-permute-start | bytes 786440 | tf_op jit(solution)/shard_map/ppermute | solution.py:342
  78.7 1.8 %collective-permute-start.24 = (bf16[2,2,256,128]{3,2,1,0:T(8,128)(2,1)S(1)}, bf16[2,2,256,128]{3,2,1,0:T(8,128)(2,1)S(1)}, u32[]{:S(2)}, u32[]{:S(2)}) collective-permute-start(bf16[2,2,256,128]{3,2,1,0:T(8,128)(2,1)S(1)} %pad_maximum_fusion.refs_0_), channel_id=1, source_target_pairs={{0,8},{1,5},{2,10},{3,7},{4,12},{5,1},{6,14},{7,3},{8,0},{9,13},{1... | collective-permute-start | bytes 786440 | tf_op jit(solution)/shard_map/ppermute | solution.py:342
  80.6 4.7 %collective-permute-start.22 = (bf16[1,4,48,128]{3,2,1,0:T(8,128)(2,1)S(1)}, bf16[1,4,48,128]{3,2,1,0:T(8,128)(2,1)S(1)}, u32[]{:S(2)}, u32[]{:S(2)}) collective-permute-start(bf16[1,4,48,128]{3,2,1,0:T(8,128)(2,1)S(1)} %get-tuple-element.134), channel_id=1, source_target_pairs={{0,20},{4,24},{8,28},{20,0},{24,4},{28,8},{1,21},{5,25},{9,29},{21... | collective-permute-start | bytes 147464 | tf_op jit(solution)/shard_map/ppermute | solution.py:438
  85.3 1.9 %collective-permute-start.23 = (bf16[1,4,48,128]{3,2,1,0:T(8,128)(2,1)S(1)}, bf16[1,4,48,128]{3,2,1,0:T(8,128)(2,1)S(1)}, u32[]{:S(2)}, u32[]{:S(2)}) collective-permute-start(bf16[1,4,48,128]{3,2,1,0:T(8,128)(2,1)S(1)} %get-tuple-element.135), channel_id=1, source_target_pairs={{4,16},{8,20},{12,24},{16,4},{20,8},{24,12},{5,17},{9,21},{13,25},... | collective-permute-start | bytes 147464 | tf_op jit(solution)/shard_map/ppermute | solution.py:438
  87.2 4.7 %collective-permute-done.22.refs_3_ = bf16[1,4,48,128]{3,2,1,0:T(8,128)(2,1)S(1)} collective-permute-done((bf16[1,4,48,128]{3,2,1,0:T(8,128)(2,1)S(1)}, bf16[1,4,48,128]{3,2,1,0:T(8,128)(2,1)S(1)}, u32[]{:S(2)}, u32[]{:S(2)}) %collective-permute-start.22) | collective-permute-done | bytes 49184 | tf_op jit(solution)/shard_map/ppermute | solution.py:438
  94.5 1.8 %unpack_sums.1 = (f32[1296,192]{1,0:T(8,128)}, f32[1296,192]{1,0:T(8,128)}) custom-call(bf16[2,2,256,128]{3,2,1,0:T(8,128)(2,1)S(1)} %pad_maximum_fusion.refs_0_, bf16[2,2,256,128]{3,2,1,0:T(8,128)(2,1)S(1)} %collective-permute-done.24.refs_1_, bf16[2,2,256,128]{3,2,1,0:T(8,128)(2,1)S(1)} %collective-permute-done.25.refs_2_, ...), custom_call_target="tpu_custom_call" | custom-call | bytes 3039232 | tf_op jit(solution)/shard_map/unpack_sums/pallas_call | solution.py:27
  (46 shorter events, 20.9 us)
Async XLA Ops:
  0.6 11.7 %collective-permute-start = (bf16[48,2048]{1,0:T(8,128)(2,1)}, bf16[48,2048]{1,0:T(8,128)(2,1)S(1)}, u32[]{:S(2)}, u32[]{:S(2)}) collective-permute-start(bf16[48,2048]{1,0:T(8,128)(2,1)} %refs_2_.1), channel_id=1, source_target_pairs={{0,1},{1,0},{2,3},{3,2},{4,5},{5,4},{6,7},{7,6},{8,9},{9,8},{10,11... | collective-permute-start | bytes 589832 | tf_op jit(solution)/shard_map/ppermute | solution.py:422
  0.7 11.6 %collective-permute-start.2 = (bf16[48,2048]{1,0:T(8,128)(2,1)}, bf16[48,2048]{1,0:T(8,128)(2,1)S(1)}, u32[]{:S(2)}, u32[]{:S(2)}) collective-permute-start(bf16[48,2048]{1,0:T(8,128)(2,1)} %refs_2_.1), channel_id=1, source_target_pairs={{0,3},{1,2},{2,1},{3,0},{4,7},{5,6},{6,5},{7,4},{8,11},{9,10},{10,... | collective-permute-start | bytes 589832 | tf_op jit(solution)/shard_map/ppermute | solution.py:422
  2.3 10.1 %collective-permute-start.1 = (bf16[48,2048]{1,0:T(8,128)(2,1)}, bf16[48,2048]{1,0:T(8,128)(2,1)S(1)}, u32[]{:S(2)}, u32[]{:S(2)}) collective-permute-start(bf16[48,2048]{1,0:T(8,128)(2,1)} %refs_2_.1), channel_id=1, source_target_pairs={{0,2},{1,3},{2,0},{3,1},{4,6},{5,7},{6,4},{7,5},{8,10},{9,11},{10,... | collective-permute-start | bytes 589832 | tf_op jit(solution)/shard_map/ppermute | solution.py:422
  5.6 17.4 %collective-permute-start.8 = (bf16[2,4,48,128]{3,2,1,0:T(8,128)(2,1)S(1)}, bf16[2,4,48,128]{3,2,1,0:T(8,128)(2,1)S(1)}, u32[]{:S(2)}, u32[]{:S(2)}) collective-permute-start(bf16[2,4,48,128]{3,2,1,0:T(8,128)(2,1)S(1)} %get-tuple-element.83), channel_id=1, source_target_pairs={{16,0},{20,4},{24,8},{28,12},{0,16},{4,20},{8,24},{12,28},{17,1},{... | collective-permute-start | bytes 294920 | tf_op jit(solution)/shard_map/ppermute | solution.py:438
  8.3 17.5 %collective-permute-start.9 = (bf16[2,4,48,128]{3,2,1,0:T(8,128)(2,1)S(1)}, bf16[2,4,48,128]{3,2,1,0:T(8,128)(2,1)S(1)}, u32[]{:S(2)}, u32[]{:S(2)}) collective-permute-start(bf16[2,4,48,128]{3,2,1,0:T(8,128)(2,1)S(1)} %get-tuple-element.84), channel_id=1, source_target_pairs={{20,0},{24,4},{28,8},{0,20},{4,24},{8,28},{21,1},{25,5},{29,9},{1,... | collective-permute-start | bytes 294920 | tf_op jit(solution)/shard_map/ppermute | solution.py:438
  16.2 18.3 %collective-permute-start.3 = (bf16[3,4,48,128]{3,2,1,0:T(8,128)(2,1)S(1)}, bf16[3,4,48,128]{3,2,1,0:T(8,128)(2,1)S(1)}, u32[]{:S(2)}, u32[]{:S(2)}) collective-permute-start(bf16[3,4,48,128]{3,2,1,0:T(8,128)(2,1)S(1)} %get-tuple-element.78), channel_id=1, source_target_pairs={{4,0},{12,8},{20,16},{28,24},{0,4},{8,12},{16,20},{24,28},{5,1},{1... | collective-permute-start | bytes 442376 | tf_op jit(solution)/shard_map/ppermute | solution.py:438
  16.6 17.9 %collective-permute-start.4 = (bf16[3,4,48,128]{3,2,1,0:T(8,128)(2,1)S(1)}, bf16[3,4,48,128]{3,2,1,0:T(8,128)(2,1)S(1)}, u32[]{:S(2)}, u32[]{:S(2)}) collective-permute-start(bf16[3,4,48,128]{3,2,1,0:T(8,128)(2,1)S(1)} %get-tuple-element.79), channel_id=1, source_target_pairs={{8,4},{24,20},{4,8},{20,24},{9,5},{25,21},{5,9},{21,25},{10,6},{26... | collective-permute-start | bytes 442376 | tf_op jit(solution)/shard_map/ppermute | solution.py:438
  21.1 13.7 %collective-permute-start.7 = (bf16[3,4,48,128]{3,2,1,0:T(8,128)(2,1)S(1)}, bf16[3,4,48,128]{3,2,1,0:T(8,128)(2,1)S(1)}, u32[]{:S(2)}, u32[]{:S(2)}) collective-permute-start(bf16[3,4,48,128]{3,2,1,0:T(8,128)(2,1)S(1)} %get-tuple-element.82), channel_id=1, source_target_pairs={{4,16},{8,20},{12,24},{16,4},{20,8},{24,12},{5,17},{9,21},{13,25},... | collective-permute-start | bytes 442376 | tf_op jit(solution)/shard_map/ppermute | solution.py:438
  23.0 8.7 %collective-permute-start.5 = (bf16[1,4,48,128]{3,2,1,0:T(8,128)(2,1)S(1)}, bf16[1,4,48,128]{3,2,1,0:T(8,128)(2,1)S(1)}, u32[]{:S(2)}, u32[]{:S(2)}) collective-permute-start(bf16[1,4,48,128]{3,2,1,0:T(8,128)(2,1)S(1)} %get-tuple-element.80), channel_id=1, source_target_pairs={{0,16},{4,20},{8,24},{12,28},{16,0},{20,4},{24,8},{28,12},{1,17},{... | collective-permute-start | bytes 147464 | tf_op jit(solution)/shard_map/ppermute | solution.py:438
  25.7 8.8 %collective-permute-start.6 = (bf16[1,4,48,128]{3,2,1,0:T(8,128)(2,1)S(1)}, bf16[1,4,48,128]{3,2,1,0:T(8,128)(2,1)S(1)}, u32[]{:S(2)}, u32[]{:S(2)}) collective-permute-start(bf16[1,4,48,128]{3,2,1,0:T(8,128)(2,1)S(1)} %get-tuple-element.81), channel_id=1, source_target_pairs={{0,20},{4,24},{8,28},{20,0},{24,4},{28,8},{1,21},{5,25},{9,29},{21... | collective-permute-start | bytes 147464 | tf_op jit(solution)/shard_map/ppermute | solution.py:438
  35.7 7.3 %collective-permute-start.10 = (bf16[48,2048]{1,0:T(8,128)(2,1)S(1)}, bf16[48,2048]{1,0:T(8,128)(2,1)S(1)}, u32[]{:S(2)}, u32[]{:S(2)}) collective-permute-start(bf16[48,2048]{1,0:T(8,128)(2,1)S(1)} %settle.2.refs_0_), channel_id=1, source_target_pairs={{0,2},{1,3},{2,0},{3,1},{4,6},{5,7},{6,4},{7,5},{8,10},{9,11},{10,... | collective-permute-start | bytes 589832 | tf_op jit(solution)/shard_map/ppermute | solution.py:422
  43.0 6.4 %collective-permute-start.13 = (bf16[1024,128]{1,0:T(8,128)(2,1)S(1)}, bf16[1024,128]{1,0:T(8,128)(2,1)S(1)}, u32[]{:S(2)}, u32[]{:S(2)}) collective-permute-start(bf16[1024,128]{1,0:T(8,128)(2,1)S(1)} %get-tuple-element.92), channel_id=1, source_target_pairs={{0,4},{1,9},{2,6},{3,11},{4,0},{5,13},{6,2},{7,15},{8,12},{9,1},{1... | collective-permute-start | bytes 786440 | tf_op jit(solution)/shard_map/ppermute | solution.py:342
  49.4 8.8 %collective-permute-start.14 = (bf16[2,512,128]{2,1,0:T(8,128)(2,1)S(1)}, bf16[2,512,128]{2,1,0:T(8,128)(2,1)S(1)}, u32[]{:S(2)}, u32[]{:S(2)}) collective-permute-start(bf16[2,512,128]{2,1,0:T(8,128)(2,1)S(1)} %get-tuple-element.107), channel_id=1, source_target_pairs={{0,8},{1,5},{2,10},{3,7},{4,12},{5,1},{6,14},{7,3},{8,0},{9,13},{1... | collective-permute-start | bytes 786440 | tf_op jit(solution)/shard_map/ppermute | solution.py:342
  49.5 8.7 %collective-permute-start.15 = (bf16[512,128]{1,0:T(8,128)(2,1)S(1)}, bf16[512,128]{1,0:T(8,128)(2,1)S(1)}, u32[]{:S(2)}, u32[]{:S(2)}) collective-permute-start(bf16[512,128]{1,0:T(8,128)(2,1)S(1)} %get-tuple-element.115), channel_id=1, source_target_pairs={{0,4},{1,9},{2,6},{3,11},{4,0},{5,13},{6,2},{7,15},{8,12},{9,1},{1... | collective-permute-start | bytes 393224 | tf_op jit(solution)/shard_map/ppermute | solution.py:342
  50.7 9.2 %collective-permute-start.16 = (bf16[512,128]{1,0:T(8,128)(2,1)S(1)}, bf16[512,128]{1,0:T(8,128)(2,1)S(1)}, u32[]{:S(2)}, u32[]{:S(2)}) collective-permute-start(bf16[512,128]{1,0:T(8,128)(2,1)S(1)} %get-tuple-element.116), channel_id=1, source_target_pairs={{0,12},{1,13},{2,14},{3,15},{4,8},{5,9},{6,10},{7,11},{8,4},{9,5},... | collective-permute-start | bytes 393224 | tf_op jit(solution)/shard_map/ppermute | solution.py:342
  60.0 9.1 %collective-permute-start.17 = (bf16[2,256,128]{2,1,0:T(8,128)(2,1)S(1)}, bf16[2,256,128]{2,1,0:T(8,128)(2,1)S(1)}, u32[]{:S(2)}, u32[]{:S(2)}) collective-permute-start(bf16[2,256,128]{2,1,0:T(8,128)(2,1)S(1)} %get-tuple-element.120), channel_id=1, source_target_pairs={{0,16},{1,17},{2,18},{3,19},{4,20},{5,21},{6,22},{7,23},{8,24},{9,... | collective-permute-start | bytes 393224 | tf_op jit(solution)/shard_map/ppermute | solution.py:342
  62.2 6.9 %collective-permute-start.19 = (bf16[1,4,48,128]{3,2,1,0:T(8,128)(2,1)S(1)}, bf16[1,4,48,128]{3,2,1,0:T(8,128)(2,1)S(1)}, u32[]{:S(2)}, u32[]{:S(2)}) collective-permute-start(bf16[1,4,48,128]{3,2,1,0:T(8,128)(2,1)S(1)} %get-tuple-element.122), channel_id=1, source_target_pairs={{8,4},{24,20},{4,8},{20,24},{9,5},{25,21},{5,9},{21,25},{10,6},{26... | collective-permute-start | bytes 147464 | tf_op jit(solution)/shard_map/ppermute | solution.py:438
  69.1 7.8 %collective-permute-start.20 = (bf16[1,2,256,128]{3,2,1,0:T(8,128)(2,1)S(1)}, bf16[1,2,256,128]{3,2,1,0:T(8,128)(2,1)S(1)}, u32[]{:S(2)}, u32[]{:S(2)}) collective-permute-start(bf16[1,2,256,128]{3,2,1,0:T(8,128)(2,1)S(1)} %fusion), channel_id=1, source_target_pairs={{0,16},{1,17},{2,18},{3,19},{4,20},{5,21},{6,22},{7,23},{8,24},{9,... | collective-permute-start | bytes 393224 | tf_op jit(solution)/shard_map/ppermute | solution.py:342
  71.1 5.8 %collective-permute-start.21 = (bf16[1,4,48,128]{3,2,1,0:T(8,128)(2,1)S(1)}, bf16[1,4,48,128]{3,2,1,0:T(8,128)(2,1)S(1)}, u32[]{:S(2)}, u32[]{:S(2)}) collective-permute-start(bf16[1,4,48,128]{3,2,1,0:T(8,128)(2,1)S(1)} %get-tuple-element.129), channel_id=1, source_target_pairs={{0,16},{4,20},{8,24},{12,28},{16,0},{20,4},{24,8},{28,12},{1,17},{... | collective-permute-start | bytes 147464 | tf_op jit(solution)/shard_map/ppermute | solution.py:438
  77.0 17.5 %collective-permute-start.26 = (bf16[2,2,256,128]{3,2,1,0:T(8,128)(2,1)S(1)}, bf16[2,2,256,128]{3,2,1,0:T(8,128)(2,1)S(1)}, u32[]{:S(2)}, u32[]{:S(2)}) collective-permute-start(bf16[2,2,256,128]{3,2,1,0:T(8,128)(2,1)S(1)} %pad_maximum_fusion.refs_0_), channel_id=1, source_target_pairs={{0,12},{1,13},{2,14},{3,15},{4,8},{5,9},{6,10},{7,11},{8,4},{9,5},... | collective-permute-start | bytes 786440 | tf_op jit(solution)/shard_map/ppermute | solution.py:342
  78.7 15.8 %collective-permute-start.25 = (bf16[2,2,256,128]{3,2,1,0:T(8,128)(2,1)S(1)}, bf16[2,2,256,128]{3,2,1,0:T(8,128)(2,1)S(1)}, u32[]{:S(2)}, u32[]{:S(2)}) collective-permute-start(bf16[2,2,256,128]{3,2,1,0:T(8,128)(2,1)S(1)} %pad_maximum_fusion.refs_0_), channel_id=1, source_target_pairs={{0,4},{1,9},{2,6},{3,11},{4,0},{5,13},{6,2},{7,15},{8,12},{9,1},{1... | collective-permute-start | bytes 786440 | tf_op jit(solution)/shard_map/ppermute | solution.py:342
  78.7 15.8 %collective-permute-start.24 = (bf16[2,2,256,128]{3,2,1,0:T(8,128)(2,1)S(1)}, bf16[2,2,256,128]{3,2,1,0:T(8,128)(2,1)S(1)}, u32[]{:S(2)}, u32[]{:S(2)}) collective-permute-start(bf16[2,2,256,128]{3,2,1,0:T(8,128)(2,1)S(1)} %pad_maximum_fusion.refs_0_), channel_id=1, source_target_pairs={{0,8},{1,5},{2,10},{3,7},{4,12},{5,1},{6,14},{7,3},{8,0},{9,13},{1... | collective-permute-start | bytes 786440 | tf_op jit(solution)/shard_map/ppermute | solution.py:342
  80.6 11.4 %collective-permute-start.22 = (bf16[1,4,48,128]{3,2,1,0:T(8,128)(2,1)S(1)}, bf16[1,4,48,128]{3,2,1,0:T(8,128)(2,1)S(1)}, u32[]{:S(2)}, u32[]{:S(2)}) collective-permute-start(bf16[1,4,48,128]{3,2,1,0:T(8,128)(2,1)S(1)} %get-tuple-element.134), channel_id=1, source_target_pairs={{0,20},{4,24},{8,28},{20,0},{24,4},{28,8},{1,21},{5,25},{9,29},{21... | collective-permute-start | bytes 147464 | tf_op jit(solution)/shard_map/ppermute | solution.py:438
  85.3 7.8 %collective-permute-start.23 = (bf16[1,4,48,128]{3,2,1,0:T(8,128)(2,1)S(1)}, bf16[1,4,48,128]{3,2,1,0:T(8,128)(2,1)S(1)}, u32[]{:S(2)}, u32[]{:S(2)}) collective-permute-start(bf16[1,4,48,128]{3,2,1,0:T(8,128)(2,1)S(1)} %get-tuple-element.135), channel_id=1, source_target_pairs={{4,16},{8,20},{12,24},{16,4},{20,8},{24,12},{5,17},{9,21},{13,25},... | collective-permute-start | bytes 147464 | tf_op jit(solution)/shard_map/ppermute | solution.py:438
  (4 other events, 20.1 us)

commit v5 on v4

--- a/solution.py
+++ b/solution.py
@@ -19,7 +19,7 @@
 F32 = jnp.float32
 
 
-def call(kernel, name, outs, spaces, args, scratch=(), flops=0, vmem_mib=4):
+def call(kernel, name, outs, spaces, args, scratch=(), flops=0, vmem_mib=4, out_space="V"):
     memory = {"S": SMEM, "H": pltpu.HBM, "V": VMEM}
     spaces = spaces + "V" * (len(args) - len(spaces))
     moved = sum(a.size * a.dtype.itemsize for a in args)
@@ -28,7 +28,7 @@
         kernel,
         out_shape=list(outs),
         in_specs=[pl.BlockSpec(memory_space=memory[space]) for space in spaces],
-        out_specs=[pl.BlockSpec(memory_space=VMEM)] * len(outs),
+        out_specs=[pl.BlockSpec(memory_space=memory[out_space])] * len(outs),
         scratch_shapes=list(scratch),
         name=name,
         cost_estimate=pl.CostEstimate(flops=flops, bytes_accessed=moved, transcendentals=0),
@@ -57,10 +57,10 @@
         return found
 
     groups = [
+        pairs_of(4, lambda t: t % 2 == 1) + pairs_of(3, lambda t: t % 2 == 0),
         pairs_of(4, lambda t: t % 2 == 0) + pairs_of(3, lambda t: t % 2 == 1),
-        pairs_of(4, lambda t: t % 2 == 1) + pairs_of(3, lambda t: t % 2 == 0),
     ]
-    for direction in (1, 6, 0, 7, 2, 5):
+    for direction in (0, 7, 1, 6, 2, 5):
         pairs = pairs_of(direction)
         for group in groups[2:]:
             sources = {p[0] for p in group}
@@ -388,21 +388,33 @@
 
 
 def unpack_kernel(tile_count, *refs):
-    quarters, out_refs, tall = refs[:4], refs[4:-1], refs[-1]
+    quarters, out_hbm, (wide, tall, sems) = refs[:4], refs[4:6], refs[6:]
     steps = tile_count.bit_length() - 1
     count, _, chunk, _ = quarters[0].shape
+    rows = wide.shape[1]
+    half = rows // 2
     mine = 0
     for step in range(steps):
         mine = mine * 2 + exchange_bit(step)
-    for part, out_ref in enumerate(out_refs):
+    copies = []
+    for part in range(2):
         for index in range(tile_count):
-            rows = pl.ds(pl.multiple_of((mine ^ index) * chunk, 16), chunk)
-            tall[rows, :] = quarters[index // count][index % count, part].astype(F32)
-        rows = out_ref.shape[0]
-        half = rows // 2
-        out_ref[:, :128] = tall[:rows]
-        out_ref[:half, 128:192] = tall[rows : rows + half, :64]
-        out_ref[half:, 128:192] = tall[rows : rows + half, 64:]
+            place = pl.ds(pl.multiple_of((mine ^ index) * chunk, 16), chunk)
+            tall[place, :] = quarters[index // count][index % count, part].astype(F32)
+        for side in range(2):
+            here_rows = slice(side * half, (side + 1) * half)
+            wide[part, here_rows, :128] = tall[here_rows]
+            wide[part, here_rows, 128:192] = tall[rows : rows + half, side * 64 : side * 64 + 64]
+            copies.append(
+                pltpu.make_async_copy(
+                    wide.at[part, here_rows],
+                    out_hbm[part].at[here_rows],
+                    sems.at[2 * part + side],
+                )
+            )
+            copies[-1].start()
+    for copy in copies:
+        copy.wait()
 
 
 def unpack(quarters, rows, columns):
@@ -410,11 +422,16 @@
     return call(
         functools.partial(unpack_kernel, tile_count),
         "unpack_sums",
-        [struct((rows, columns), F32)] * quarters[0].shape[1],
+        [struct((rows, columns), F32)] * 2,
         "",
         quarters,
-        [VMEM((tile_count * quarters[0].shape[2], 128), F32)],
+        [
+            VMEM((2, rows, columns), F32),
+            VMEM((tile_count * quarters[0].shape[2], 128), F32),
+            pltpu.SemaphoreType.DMA((4,)),
+        ],
         vmem_mib=8,
+        out_space="H",
     )
 
 
@@ -473,7 +490,7 @@
     pre_parts, keep_one = tie(pre_parts, keep_one)
     local_one, backs = partial_sums(pair_in, plan, pre_parts, weight_one, slot_count)
     got_one, backs = tie(got_one, backs)
-    shares = [[0, 1], [2], list(range(3, len(backs)))]
+    shares = [[0, 1], [3], [2] + list(range(4, len(backs)))]
     returned = [None] * len(backs)
 
     def beside(value, step):

time: 96.7 us -> 95.9 us (level)
  starting transfers between devices: 49.1 us -> 44.3 us
  waiting for transfers between devices: 24.5 us -> 28.9 us
    ppermute x12, waiting for transfers between devices: 16.7 us -> 20 us  [give(): return [lax.ppermute(v, 'tile', p) for v, p in zip(values, lists)]]
    ppermute x12, starting transfers between devices: 33.8 us -> 30.9 us  [give(): return [lax.ppermute(v, 'tile', p) for v, p in zip(values, lists)]]
    ppermute x9, starting transfers between devices: 11.4 us -> 9.52 us  [trade(): return lax.ppermute(value, ('tile', 'chan'), pairs)]
    ppermute x6, waiting for transfers between devices: 2.87 us -> 4.25 us  [swap_part(): return lax.ppermute(value, 'chan', [(i, i ^ bits) for i in range(4)])]
  transfers between devices with their start and end apart: 27 -> 27, of which waited for: 13 -> 12; matrix products, arithmetic and copies ran while one was open for 2% -> 2% of each run, Pallas kernels for 18% -> 18%
where the time goes in v5:
time: 95.9 us; the launch traced here: 95.5 us
  starting transfers between devices  44.3 us (46%)
  waiting for transfers between devices  28.9 us (30%)
  Pallas kernels  19.9 us (21%)
  local copies, waits for them, and re-layouts  1.54 us (2%)
    ppermute x12, starting transfers between devices, give(): return [lax.ppermute(v, 'tile', p) for v, p in zip(values, lists)]  30.9 us
    ppermute x12, waiting for transfers between devices, give(): return [lax.ppermute(v, 'tile', p) for v, p in zip(values, lists)]  20 us
    pallas_call x10, Pallas kernels, call(): pl.pallas_call(kernel, out_shape=list(outs), in_specs=[pl.BlockSpec(memor...  19.9 us
    ppermute x9, starting transfers between devices, trade(): return lax.ppermute(value, ('tile', 'chan'), pairs)  9.52 us
    ppermute x9, waiting for transfers between devices, trade(): return lax.ppermute(value, ('tile', 'chan'), pairs)  4.63 us
    ppermute x6, waiting for transfers between devices, swap_part(): return lax.ppermute(value, 'chan', [(i, i ^ bits) for i in range(4)])  4.25 us
    ppermute x6, starting transfers between devices, swap_part(): return lax.ppermute(value, 'chan', [(i, i ^ bits) for i in range(4)])  3.87 us
  transfers between devices with their start and end apart: 27, of which 12 were waited for; matrix products, arithmetic and copies ran while one was open for 2% of the time, Pallas kernels for 18%

profile of v5, /device:TPU:2, one launch (start us, length us, event | category | flops | bytes accessed | tf_op | source)
XLA Modules:
  0.0 95.5 jit_solution(9103799749520234436)
XLA Ops:
  3.6 2.0 %pack_sends.1 = (bf16[2,4,48,128]{3,2,1,0:T(8,128)(2,1)S(1)}, bf16[2,4,48,128]{3,2,1,0:T(8,128)(2,1)S(1)}, bf16[2,4,48,128]{3,2,1,0:T(8,128)(2,1)S(1)}, bf16[2,4...) custom-call(s32[1,8,4]{2,1,0:T(8,128)S(1)} %copy.16.lists_ref, ...), custom_call_target="tpu_custom_call" | custom-call | bytes 2666624 | tf_op jit(solution)/shard_map/pack_sends/pallas_call | solution.py:27
  5.6 5.5 %collective-permute-start.8 = (bf16[2,4,48,128]{3,2,1,0:T(8,128)(2,1)S(1)}, bf16[2,4,48,128]{3,2,1,0:T(8,128)(2,1)S(1)}, u32[]{:S(2)}, u32[]{:S(2)}) collective-permute-start(bf16[2,4,48,128]{3,2,1,0:T(8,128)(2,1)S(1)} %get-tuple-element.83), channel_id=1, source_target_pairs={{20,0},{24,4},{28,8},{0,20},{4,24},{8,28},{21,1},{25,5},{29,9},{1,... | collective-permute-start | bytes 294920 | tf_op jit(solution)/shard_map/ppermute | solution.py:455
  12.4 3.7 %partial_sums.2 = (f32[16,48,128]{2,1,0:T(8,128)S(1)}, bf16[3,4,48,128]{3,2,1,0:T(8,128)(2,1)S(1)}, bf16[3,4,48,128]{3,2,1,0:T(8,128)(2,1)S(1)}, bf16[1,4,48,128...) custom-call(s32[1,27,16]{2,1,0:T(8,128)S(1)} %copy.15.pin_ref, ...), custom_call_target="tpu_custom_call" | custom-call | flops 1019215872 | bytes 2514624 | tf_op jit(solution)/shard_map/partial_sums/pallas_call | solution.py:27
  16.1 3.5 %collective-permute-start.3 = (bf16[3,4,48,128]{3,2,1,0:T(8,128)(2,1)S(1)}, bf16[3,4,48,128]{3,2,1,0:T(8,128)(2,1)S(1)}, u32[]{:S(2)}, u32[]{:S(2)}) collective-permute-start(bf16[3,4,48,128]{3,2,1,0:T(8,128)(2,1)S(1)} %get-tuple-element.78), channel_id=1, source_target_pairs={{8,4},{24,20},{4,8},{20,24},{9,5},{25,21},{5,9},{21,25},{10,6},{26... | collective-permute-start | bytes 442376 | tf_op jit(solution)/shard_map/ppermute | solution.py:455
  19.7 5.9 %collective-permute-start.7 = (bf16[3,4,48,128]{3,2,1,0:T(8,128)(2,1)S(1)}, bf16[3,4,48,128]{3,2,1,0:T(8,128)(2,1)S(1)}, u32[]{:S(2)}, u32[]{:S(2)}) collective-permute-start(bf16[3,4,48,128]{3,2,1,0:T(8,128)(2,1)S(1)} %get-tuple-element.82), channel_id=1, source_target_pairs={{4,16},{8,20},{12,24},{16,4},{20,8},{24,12},{5,17},{9,21},{13,25},... | collective-permute-start | bytes 442376 | tf_op jit(solution)/shard_map/ppermute | solution.py:455
  25.6 3.0 %collective-permute-start.5 = (bf16[1,4,48,128]{3,2,1,0:T(8,128)(2,1)S(1)}, bf16[1,4,48,128]{3,2,1,0:T(8,128)(2,1)S(1)}, u32[]{:S(2)}, u32[]{:S(2)}) collective-permute-start(bf16[1,4,48,128]{3,2,1,0:T(8,128)(2,1)S(1)} %get-tuple-element.80), channel_id=1, source_target_pairs={{0,20},{4,24},{8,28},{20,0},{24,4},{28,8},{1,21},{5,25},{9,29},{21... | collective-permute-start | bytes 147464 | tf_op jit(solution)/shard_map/ppermute | solution.py:455
  28.8 5.7 %collective-permute-done.5.refs_2_ = bf16[1,4,48,128]{3,2,1,0:T(8,128)(2,1)S(1)} collective-permute-done((bf16[1,4,48,128]{3,2,1,0:T(8,128)(2,1)S(1)}, bf16[1,4,48,128]{3,2,1,0:T(8,128)(2,1)S(1)}, u32[]{:S(2)}, u32[]{:S(2)}) %collective-permute-start.5) | collective-permute-done | bytes 49184 | tf_op jit(solution)/shard_map/ppermute | solution.py:455
  36.9 3.3 %weight_sums.2 = (f32[1024,128]{1,0:T(8,128)S(1)}, bf16[1024,128]{1,0:T(8,128)(2,1)S(1)}) custom-call(s32[1,27,16]{2,1,0:T(8,128)S(1)} %copy.15.pin_ref, bf16[48,2048]{1,0:T(8,128)(2,1)S(1)} %get-tuple-element.72.other_ref.own_ref, bf16[48,2048]{1,0:T(8,128)(2,1)S(1)} %get-tuple-element.71.refs_0_.other_ref, ...), custom_call_target="tpu_custom_call" | custom-call | flops 1019215872 | bytes 2410176 | tf_op jit(solution)/shard_map/weight_sums/pallas_call | solution.py:27
  40.2 2.4 %collective-permute-done.10.refs_2_ = bf16[48,2048]{1,0:T(8,128)(2,1)S(1)} collective-permute-done((bf16[48,2048]{1,0:T(8,128)(2,1)S(1)}, bf16[48,2048]{1,0:T(8,128)(2,1)S(1)}, u32[]{:S(2)}, u32[]{:S(2)}) %collective-permute-start.10) | collective-permute-done | bytes 196640 | tf_op jit(solution)/shard_map/ppermute | solution.py:439
  44.1 3.2 %weight_sums.3 = (f32[512,128]{1,0:T(8,128)S(1)}, bf16[512,128]{1,0:T(8,128)(2,1)S(1)}, bf16[512,128]{1,0:T(8,128)(2,1)S(1)}, bf16[512,128]{1,0:T(8,128)(2,1)S(1)}) custom-call(s32[1,27,16]{2,1,0:T(8,128)S(1)} %copy.15.pin_ref, bf16[48,2048]{1,0:T(8,128)(2,1)S(1)} %get-tuple-element.95.own_ref, bf16[48,2048]{1,0:T(8,128)(2,1)S(1)} %settle.2.refs_0_, ...), custom_call_target="tpu_custom_call" | custom-call | flops 1019215872 | bytes 2279104 | tf_op jit(solution)/shard_map/weight_sums/pallas_call | solution.py:27
  47.3 1.7 %collective-permute-done.13.got_ref = bf16[1024,128]{1,0:T(8,128)(2,1)S(1)} collective-permute-done((bf16[1024,128]{1,0:T(8,128)(2,1)S(1)}, bf16[1024,128]{1,0:T(8,128)(2,1)S(1)}, u32[]{:S(2)}, u32[]{:S(2)}) %collective-permute-start.13) | collective-permute-done | bytes 262176 | tf_op jit(solution)/shard_map/ppermute | solution.py:342
  50.8 1.8 %collective-permute-start.16 = (bf16[512,128]{1,0:T(8,128)(2,1)S(1)}, bf16[512,128]{1,0:T(8,128)(2,1)S(1)}, u32[]{:S(2)}, u32[]{:S(2)}) collective-permute-start(bf16[512,128]{1,0:T(8,128)(2,1)S(1)} %get-tuple-element.116), channel_id=1, source_target_pairs={{0,12},{1,13},{2,14},{3,15},{4,8},{5,9},{6,10},{7,11},{8,4},{9,5},... | collective-permute-start | bytes 393224 | tf_op jit(solution)/shard_map/ppermute | solution.py:342
  52.6 3.7 %partial_sums.3 = (f32[16,48,128]{2,1,0:T(8,128)S(1)}, bf16[1,4,48,128]{3,2,1,0:T(8,128)(2,1)S(1)}, bf16[1,4,48,128]{3,2,1,0:T(8,128)(2,1)S(1)}, bf16[1,4,48,128...) custom-call(s32[1,27,16]{2,1,0:T(8,128)S(1)} %copy.15.pin_ref, ...), custom_call_target="tpu_custom_call" | custom-call | flops 1019215872 | bytes 1924800 | tf_op jit(solution)/shard_map/partial_sums/pallas_call | solution.py:27
  57.1 2.1 %collective-permute-done.16.refs_4_ = bf16[512,128]{1,0:T(8,128)(2,1)S(1)} collective-permute-done((bf16[512,128]{1,0:T(8,128)(2,1)S(1)}, bf16[512,128]{1,0:T(8,128)(2,1)S(1)}, u32[]{:S(2)}, u32[]{:S(2)}) %collective-permute-start.16) | collective-permute-done | bytes 131104 | tf_op jit(solution)/shard_map/ppermute | solution.py:342
  59.3 2.1 %collective-permute-start.17 = (bf16[2,256,128]{2,1,0:T(8,128)(2,1)S(1)}, bf16[2,256,128]{2,1,0:T(8,128)(2,1)S(1)}, u32[]{:S(2)}, u32[]{:S(2)}) collective-permute-start(bf16[2,256,128]{2,1,0:T(8,128)(2,1)S(1)} %get-tuple-element.120), channel_id=1, source_target_pairs={{0,16},{1,17},{2,18},{3,19},{4,20},{5,21},{6,22},{7,23},{8,24},{9,... | collective-permute-start | bytes 393224 | tf_op jit(solution)/shard_map/ppermute | solution.py:342
  61.4 4.0 %collective-permute-start.18 = (bf16[1,4,48,128]{3,2,1,0:T(8,128)(2,1)S(1)}, bf16[1,4,48,128]{3,2,1,0:T(8,128)(2,1)S(1)}, u32[]{:S(2)}, u32[]{:S(2)}) collective-permute-start(bf16[1,4,48,128]{3,2,1,0:T(8,128)(2,1)S(1)} %get-tuple-element.121), channel_id=1, source_target_pairs={{8,4},{24,20},{4,8},{20,24},{9,5},{25,21},{5,9},{21,25},{10,6},{26... | collective-permute-start | bytes 147464 | tf_op jit(solution)/shard_map/ppermute | solution.py:455
  65.4 2.8 %collective-permute-done.18.refs_0_ = bf16[1,4,48,128]{3,2,1,0:T(8,128)(2,1)S(1)} collective-permute-done((bf16[1,4,48,128]{3,2,1,0:T(8,128)(2,1)S(1)}, bf16[1,4,48,128]{3,2,1,0:T(8,128)(2,1)S(1)}, u32[]{:S(2)}, u32[]{:S(2)}) %collective-permute-start.18) | collective-permute-done | bytes 49184 | tf_op jit(solution)/shard_map/ppermute | solution.py:455
  69.9 2.7 %collective-permute-start.21 = (bf16[1,4,48,128]{3,2,1,0:T(8,128)(2,1)S(1)}, bf16[1,4,48,128]{3,2,1,0:T(8,128)(2,1)S(1)}, u32[]{:S(2)}, u32[]{:S(2)}) collective-permute-start(bf16[1,4,48,128]{3,2,1,0:T(8,128)(2,1)S(1)} %get-tuple-element.129), channel_id=1, source_target_pairs={{0,16},{4,20},{8,24},{12,28},{16,0},{20,4},{24,8},{28,12},{1,17},{... | collective-permute-start | bytes 147464 | tf_op jit(solution)/shard_map/ppermute | solution.py:455
  72.6 4.4 %collective-permute-done.21.refs_3_ = bf16[1,4,48,128]{3,2,1,0:T(8,128)(2,1)S(1)} collective-permute-done((bf16[1,4,48,128]{3,2,1,0:T(8,128)(2,1)S(1)}, bf16[1,4,48,128]{3,2,1,0:T(8,128)(2,1)S(1)}, u32[]{:S(2)}, u32[]{:S(2)}) %collective-permute-start.21) | collective-permute-done | bytes 49184 | tf_op jit(solution)/shard_map/ppermute | solution.py:455
  78.2 2.3 %collective-permute-start.24 = (bf16[2,2,256,128]{3,2,1,0:T(8,128)(2,1)S(1)}, bf16[2,2,256,128]{3,2,1,0:T(8,128)(2,1)S(1)}, u32[]{:S(2)}, u32[]{:S(2)}) collective-permute-start(bf16[2,2,256,128]{3,2,1,0:T(8,128)(2,1)S(1)} %pad_maximum_fusion.refs_0_), channel_id=1, source_target_pairs={{0,8},{1,5},{2,10},{3,7},{4,12},{5,1},{6,14},{7,3},{8,0},{9,13},{1... | collective-permute-start | bytes 786440 | tf_op jit(solution)/shard_map/ppermute | solution.py:342
  80.5 4.1 %collective-permute-start.22 = (bf16[1,4,48,128]{3,2,1,0:T(8,128)(2,1)S(1)}, bf16[1,4,48,128]{3,2,1,0:T(8,128)(2,1)S(1)}, u32[]{:S(2)}, u32[]{:S(2)}) collective-permute-start(bf16[1,4,48,128]{3,2,1,0:T(8,128)(2,1)S(1)} %get-tuple-element.133), channel_id=1, source_target_pairs={{0,20},{4,24},{8,28},{20,0},{24,4},{28,8},{1,21},{5,25},{9,29},{21... | collective-permute-start | bytes 147464 | tf_op jit(solution)/shard_map/ppermute | solution.py:455
  84.6 1.9 %collective-permute-start.23 = (bf16[1,4,48,128]{3,2,1,0:T(8,128)(2,1)S(1)}, bf16[1,4,48,128]{3,2,1,0:T(8,128)(2,1)S(1)}, u32[]{:S(2)}, u32[]{:S(2)}) collective-permute-start(bf16[1,4,48,128]{3,2,1,0:T(8,128)(2,1)S(1)} %get-tuple-element.135), channel_id=1, source_target_pairs={{4,16},{8,20},{12,24},{16,4},{20,8},{24,12},{5,17},{9,21},{13,25},... | collective-permute-start | bytes 147464 | tf_op jit(solution)/shard_map/ppermute | solution.py:455
  86.6 4.2 %collective-permute-done.22.refs_2_ = bf16[1,4,48,128]{3,2,1,0:T(8,128)(2,1)S(1)} collective-permute-done((bf16[1,4,48,128]{3,2,1,0:T(8,128)(2,1)S(1)}, bf16[1,4,48,128]{3,2,1,0:T(8,128)(2,1)S(1)}, u32[]{:S(2)}, u32[]{:S(2)}) %collective-permute-start.22) | collective-permute-done | bytes 49184 | tf_op jit(solution)/shard_map/ppermute | solution.py:455
  93.9 1.7 %unpack_sums.1 = (f32[1296,192]{1,0:T(8,128)}, f32[1296,192]{1,0:T(8,128)}) custom-call(bf16[2,2,256,128]{3,2,1,0:T(8,128)(2,1)S(1)} %pad_maximum_fusion.refs_0_, bf16[2,2,256,128]{3,2,1,0:T(8,128)(2,1)S(1)} %collective-permute-done.24.refs_1_, bf16[2,2,256,128]{3,2,1,0:T(8,128)(2,1)S(1)} %collective-permute-done.25.refs_2_, ...), custom_call_target="tpu_custom_call" | custom-call | bytes 3039232 | tf_op jit(solution)/shard_map/unpack_sums/pallas_call | solution.py:27
  (46 shorter events, 17.0 us)
Async XLA Ops:
  0.6 11.4 %collective-permute-start = (bf16[48,2048]{1,0:T(8,128)(2,1)}, bf16[48,2048]{1,0:T(8,128)(2,1)S(1)}, u32[]{:S(2)}, u32[]{:S(2)}) collective-permute-start(bf16[48,2048]{1,0:T(8,128)(2,1)} %refs_2_.1), channel_id=1, source_target_pairs={{0,1},{1,0},{2,3},{3,2},{4,5},{5,4},{6,7},{7,6},{8,9},{9,8},{10,11... | collective-permute-start | bytes 589832 | tf_op jit(solution)/shard_map/ppermute | solution.py:439
  0.7 11.3 %collective-permute-start.2 = (bf16[48,2048]{1,0:T(8,128)(2,1)}, bf16[48,2048]{1,0:T(8,128)(2,1)S(1)}, u32[]{:S(2)}, u32[]{:S(2)}) collective-permute-start(bf16[48,2048]{1,0:T(8,128)(2,1)} %refs_2_.1), channel_id=1, source_target_pairs={{0,3},{1,2},{2,1},{3,0},{4,7},{5,6},{6,5},{7,4},{8,11},{9,10},{10,... | collective-permute-start | bytes 589832 | tf_op jit(solution)/shard_map/ppermute | solution.py:439
  2.3 10.1 %collective-permute-start.1 = (bf16[48,2048]{1,0:T(8,128)(2,1)}, bf16[48,2048]{1,0:T(8,128)(2,1)S(1)}, u32[]{:S(2)}, u32[]{:S(2)}) collective-permute-start(bf16[48,2048]{1,0:T(8,128)(2,1)} %refs_2_.1), channel_id=1, source_target_pairs={{0,2},{1,3},{2,0},{3,1},{4,6},{5,7},{6,4},{7,5},{8,10},{9,11},{10,... | collective-permute-start | bytes 589832 | tf_op jit(solution)/shard_map/ppermute | solution.py:439
  5.6 20.0 %collective-permute-start.8 = (bf16[2,4,48,128]{3,2,1,0:T(8,128)(2,1)S(1)}, bf16[2,4,48,128]{3,2,1,0:T(8,128)(2,1)S(1)}, u32[]{:S(2)}, u32[]{:S(2)}) collective-permute-start(bf16[2,4,48,128]{3,2,1,0:T(8,128)(2,1)S(1)} %get-tuple-element.83), channel_id=1, source_target_pairs={{20,0},{24,4},{28,8},{0,20},{4,24},{8,28},{21,1},{25,5},{29,9},{1,... | collective-permute-start | bytes 294920 | tf_op jit(solution)/shard_map/ppermute | solution.py:455
  11.1 17.5 %collective-permute-start.9 = (bf16[2,4,48,128]{3,2,1,0:T(8,128)(2,1)S(1)}, bf16[2,4,48,128]{3,2,1,0:T(8,128)(2,1)S(1)}, u32[]{:S(2)}, u32[]{:S(2)}) collective-permute-start(bf16[2,4,48,128]{3,2,1,0:T(8,128)(2,1)S(1)} %get-tuple-element.84), channel_id=1, source_target_pairs={{16,0},{20,4},{24,8},{28,12},{0,16},{4,20},{8,24},{12,28},{17,1},{... | collective-permute-start | bytes 294920 | tf_op jit(solution)/shard_map/ppermute | solution.py:455
  16.1 18.3 %collective-permute-start.3 = (bf16[3,4,48,128]{3,2,1,0:T(8,128)(2,1)S(1)}, bf16[3,4,48,128]{3,2,1,0:T(8,128)(2,1)S(1)}, u32[]{:S(2)}, u32[]{:S(2)}) collective-permute-start(bf16[3,4,48,128]{3,2,1,0:T(8,128)(2,1)S(1)} %get-tuple-element.78), channel_id=1, source_target_pairs={{8,4},{24,20},{4,8},{20,24},{9,5},{25,21},{5,9},{21,25},{10,6},{26... | collective-permute-start | bytes 442376 | tf_op jit(solution)/shard_map/ppermute | solution.py:455
  19.7 14.8 %collective-permute-start.4 = (bf16[3,4,48,128]{3,2,1,0:T(8,128)(2,1)S(1)}, bf16[3,4,48,128]{3,2,1,0:T(8,128)(2,1)S(1)}, u32[]{:S(2)}, u32[]{:S(2)}) collective-permute-start(bf16[3,4,48,128]{3,2,1,0:T(8,128)(2,1)S(1)} %get-tuple-element.79), channel_id=1, source_target_pairs={{4,0},{12,8},{20,16},{28,24},{0,4},{8,12},{16,20},{24,28},{5,1},{1... | collective-permute-start | bytes 442376 | tf_op jit(solution)/shard_map/ppermute | solution.py:455
  19.7 14.7 %collective-permute-start.7 = (bf16[3,4,48,128]{3,2,1,0:T(8,128)(2,1)S(1)}, bf16[3,4,48,128]{3,2,1,0:T(8,128)(2,1)S(1)}, u32[]{:S(2)}, u32[]{:S(2)}) collective-permute-start(bf16[3,4,48,128]{3,2,1,0:T(8,128)(2,1)S(1)} %get-tuple-element.82), channel_id=1, source_target_pairs={{4,16},{8,20},{12,24},{16,4},{20,8},{24,12},{5,17},{9,21},{13,25},... | collective-permute-start | bytes 442376 | tf_op jit(solution)/shard_map/ppermute | solution.py:455
  25.6 8.8 %collective-permute-start.5 = (bf16[1,4,48,128]{3,2,1,0:T(8,128)(2,1)S(1)}, bf16[1,4,48,128]{3,2,1,0:T(8,128)(2,1)S(1)}, u32[]{:S(2)}, u32[]{:S(2)}) collective-permute-start(bf16[1,4,48,128]{3,2,1,0:T(8,128)(2,1)S(1)} %get-tuple-element.80), channel_id=1, source_target_pairs={{0,20},{4,24},{8,28},{20,0},{24,4},{28,8},{1,21},{5,25},{9,29},{21... | collective-permute-start | bytes 147464 | tf_op jit(solution)/shard_map/ppermute | solution.py:455
  28.7 5.7 %collective-permute-start.6 = (bf16[1,4,48,128]{3,2,1,0:T(8,128)(2,1)S(1)}, bf16[1,4,48,128]{3,2,1,0:T(8,128)(2,1)S(1)}, u32[]{:S(2)}, u32[]{:S(2)}) collective-permute-start(bf16[1,4,48,128]{3,2,1,0:T(8,128)(2,1)S(1)} %get-tuple-element.81), channel_id=1, source_target_pairs={{0,16},{4,20},{8,24},{12,28},{16,0},{20,4},{24,8},{28,12},{1,17},{... | collective-permute-start | bytes 147464 | tf_op jit(solution)/shard_map/ppermute | solution.py:455
  35.3 7.3 %collective-permute-start.10 = (bf16[48,2048]{1,0:T(8,128)(2,1)S(1)}, bf16[48,2048]{1,0:T(8,128)(2,1)S(1)}, u32[]{:S(2)}, u32[]{:S(2)}) collective-permute-start(bf16[48,2048]{1,0:T(8,128)(2,1)S(1)} %settle.2.refs_0_), channel_id=1, source_target_pairs={{0,2},{1,3},{2,0},{3,1},{4,6},{5,7},{6,4},{7,5},{8,10},{9,11},{10,... | collective-permute-start | bytes 589832 | tf_op jit(solution)/shard_map/ppermute | solution.py:439
  42.6 6.4 %collective-permute-start.13 = (bf16[1024,128]{1,0:T(8,128)(2,1)S(1)}, bf16[1024,128]{1,0:T(8,128)(2,1)S(1)}, u32[]{:S(2)}, u32[]{:S(2)}) collective-permute-start(bf16[1024,128]{1,0:T(8,128)(2,1)S(1)} %get-tuple-element.92), channel_id=1, source_target_pairs={{0,4},{1,9},{2,6},{3,11},{4,0},{5,13},{6,2},{7,15},{8,12},{9,1},{1... | collective-permute-start | bytes 786440 | tf_op jit(solution)/shard_map/ppermute | solution.py:342
  49.1 8.0 %collective-permute-start.14 = (bf16[2,512,128]{2,1,0:T(8,128)(2,1)S(1)}, bf16[2,512,128]{2,1,0:T(8,128)(2,1)S(1)}, u32[]{:S(2)}, u32[]{:S(2)}) collective-permute-start(bf16[2,512,128]{2,1,0:T(8,128)(2,1)S(1)} %get-tuple-element.107), channel_id=1, source_target_pairs={{0,8},{1,5},{2,10},{3,7},{4,12},{5,1},{6,14},{7,3},{8,0},{9,13},{1... | collective-permute-start | bytes 786440 | tf_op jit(solution)/shard_map/ppermute | solution.py:342
  49.1 7.9 %collective-permute-start.15 = (bf16[512,128]{1,0:T(8,128)(2,1)S(1)}, bf16[512,128]{1,0:T(8,128)(2,1)S(1)}, u32[]{:S(2)}, u32[]{:S(2)}) collective-permute-start(bf16[512,128]{1,0:T(8,128)(2,1)S(1)} %get-tuple-element.115), channel_id=1, source_target_pairs={{0,4},{1,9},{2,6},{3,11},{4,0},{5,13},{6,2},{7,15},{8,12},{9,1},{1... | collective-permute-start | bytes 393224 | tf_op jit(solution)/shard_map/ppermute | solution.py:342
  50.8 8.4 %collective-permute-start.16 = (bf16[512,128]{1,0:T(8,128)(2,1)S(1)}, bf16[512,128]{1,0:T(8,128)(2,1)S(1)}, u32[]{:S(2)}, u32[]{:S(2)}) collective-permute-start(bf16[512,128]{1,0:T(8,128)(2,1)S(1)} %get-tuple-element.116), channel_id=1, source_target_pairs={{0,12},{1,13},{2,14},{3,15},{4,8},{5,9},{6,10},{7,11},{8,4},{9,5},... | collective-permute-start | bytes 393224 | tf_op jit(solution)/shard_map/ppermute | solution.py:342
  59.3 10.2 %collective-permute-start.17 = (bf16[2,256,128]{2,1,0:T(8,128)(2,1)S(1)}, bf16[2,256,128]{2,1,0:T(8,128)(2,1)S(1)}, u32[]{:S(2)}, u32[]{:S(2)}) collective-permute-start(bf16[2,256,128]{2,1,0:T(8,128)(2,1)S(1)} %get-tuple-element.120), channel_id=1, source_target_pairs={{0,16},{1,17},{2,18},{3,19},{4,20},{5,21},{6,22},{7,23},{8,24},{9,... | collective-permute-start | bytes 393224 | tf_op jit(solution)/shard_map/ppermute | solution.py:342
  61.4 6.9 %collective-permute-start.18 = (bf16[1,4,48,128]{3,2,1,0:T(8,128)(2,1)S(1)}, bf16[1,4,48,128]{3,2,1,0:T(8,128)(2,1)S(1)}, u32[]{:S(2)}, u32[]{:S(2)}) collective-permute-start(bf16[1,4,48,128]{3,2,1,0:T(8,128)(2,1)S(1)} %get-tuple-element.121), channel_id=1, source_target_pairs={{8,4},{24,20},{4,8},{20,24},{9,5},{25,21},{5,9},{21,25},{10,6},{26... | collective-permute-start | bytes 147464 | tf_op jit(solution)/shard_map/ppermute | solution.py:455
  69.6 7.4 %collective-permute-start.20 = (bf16[1,2,256,128]{3,2,1,0:T(8,128)(2,1)S(1)}, bf16[1,2,256,128]{3,2,1,0:T(8,128)(2,1)S(1)}, u32[]{:S(2)}, u32[]{:S(2)}) collective-permute-start(bf16[1,2,256,128]{3,2,1,0:T(8,128)(2,1)S(1)} %fusion), channel_id=1, source_target_pairs={{0,16},{1,17},{2,18},{3,19},{4,20},{5,21},{6,22},{7,23},{8,24},{9,... | collective-permute-start | bytes 393224 | tf_op jit(solution)/shard_map/ppermute | solution.py:342
  69.9 7.1 %collective-permute-start.21 = (bf16[1,4,48,128]{3,2,1,0:T(8,128)(2,1)S(1)}, bf16[1,4,48,128]{3,2,1,0:T(8,128)(2,1)S(1)}, u32[]{:S(2)}, u32[]{:S(2)}) collective-permute-start(bf16[1,4,48,128]{3,2,1,0:T(8,128)(2,1)S(1)} %get-tuple-element.129), channel_id=1, source_target_pairs={{0,16},{4,20},{8,24},{12,28},{16,0},{20,4},{24,8},{28,12},{1,17},{... | collective-permute-start | bytes 147464 | tf_op jit(solution)/shard_map/ppermute | solution.py:455
  77.0 16.9 %collective-permute-start.26 = (bf16[2,2,256,128]{3,2,1,0:T(8,128)(2,1)S(1)}, bf16[2,2,256,128]{3,2,1,0:T(8,128)(2,1)S(1)}, u32[]{:S(2)}, u32[]{:S(2)}) collective-permute-start(bf16[2,2,256,128]{3,2,1,0:T(8,128)(2,1)S(1)} %pad_maximum_fusion.refs_0_), channel_id=1, source_target_pairs={{0,12},{1,13},{2,14},{3,15},{4,8},{5,9},{6,10},{7,11},{8,4},{9,5},... | collective-permute-start | bytes 786440 | tf_op jit(solution)/shard_map/ppermute | solution.py:342
  77.6 16.3 %collective-permute-start.25 = (bf16[2,2,256,128]{3,2,1,0:T(8,128)(2,1)S(1)}, bf16[2,2,256,128]{3,2,1,0:T(8,128)(2,1)S(1)}, u32[]{:S(2)}, u32[]{:S(2)}) collective-permute-start(bf16[2,2,256,128]{3,2,1,0:T(8,128)(2,1)S(1)} %pad_maximum_fusion.refs_0_), channel_id=1, source_target_pairs={{0,4},{1,9},{2,6},{3,11},{4,0},{5,13},{6,2},{7,15},{8,12},{9,1},{1... | collective-permute-start | bytes 786440 | tf_op jit(solution)/shard_map/ppermute | solution.py:342
  78.2 15.6 %collective-permute-start.24 = (bf16[2,2,256,128]{3,2,1,0:T(8,128)(2,1)S(1)}, bf16[2,2,256,128]{3,2,1,0:T(8,128)(2,1)S(1)}, u32[]{:S(2)}, u32[]{:S(2)}) collective-permute-start(bf16[2,2,256,128]{3,2,1,0:T(8,128)(2,1)S(1)} %pad_maximum_fusion.refs_0_), channel_id=1, source_target_pairs={{0,8},{1,5},{2,10},{3,7},{4,12},{5,1},{6,14},{7,3},{8,0},{9,13},{1... | collective-permute-start | bytes 786440 | tf_op jit(solution)/shard_map/ppermute | solution.py:342
  80.5 10.3 %collective-permute-start.22 = (bf16[1,4,48,128]{3,2,1,0:T(8,128)(2,1)S(1)}, bf16[1,4,48,128]{3,2,1,0:T(8,128)(2,1)S(1)}, u32[]{:S(2)}, u32[]{:S(2)}) collective-permute-start(bf16[1,4,48,128]{3,2,1,0:T(8,128)(2,1)S(1)} %get-tuple-element.133), channel_id=1, source_target_pairs={{0,20},{4,24},{8,28},{20,0},{24,4},{28,8},{1,21},{5,25},{9,29},{21... | collective-permute-start | bytes 147464 | tf_op jit(solution)/shard_map/ppermute | solution.py:455
  84.6 7.8 %collective-permute-start.23 = (bf16[1,4,48,128]{3,2,1,0:T(8,128)(2,1)S(1)}, bf16[1,4,48,128]{3,2,1,0:T(8,128)(2,1)S(1)}, u32[]{:S(2)}, u32[]{:S(2)}) collective-permute-start(bf16[1,4,48,128]{3,2,1,0:T(8,128)(2,1)S(1)} %get-tuple-element.135), channel_id=1, source_target_pairs={{4,16},{8,20},{12,24},{16,4},{20,8},{24,12},{5,17},{9,21},{13,25},... | collective-permute-start | bytes 147464 | tf_op jit(solution)/shard_map/ppermute | solution.py:455
  (4 other events, 19.1 us)

commit v6 on v5

--- a/solution.py
+++ b/solution.py
@@ -209,7 +209,7 @@
 
 
 def packed_rows(rows, tile_count):
-    step = 16 * tile_count
+    step = 8 * tile_count
     return -(-(rows + rows // 2) // step) * step
 
 
@@ -256,7 +256,7 @@
     split = tall.shape[0] // pieces
     mine = exchange_bit(0) if pieces == 2 else 2 * exchange_bit(0) + exchange_bit(1)
     for index, piece_ref in enumerate(piece_refs):
-        piece = tall[pl.ds(pl.multiple_of((mine ^ index) * split, 16), split), :]
+        piece = tall[pl.ds(pl.multiple_of((mine ^ index) * split, 8), split), :]
         piece_ref[...] = piece.astype(piece_ref.dtype)
 
 
@@ -346,8 +346,8 @@
     *_, next_ref, send_ref = refs
     bit = exchange_bit(step)
     split = next_ref.shape[1]
-    mine = pl.ds(pl.multiple_of(bit * split, 16), split)
-    theirs = pl.ds(pl.multiple_of((1 - bit) * split, 16), split)
+    mine = pl.ds(pl.multiple_of(bit * split, 8), split)
+    theirs = pl.ds(pl.multiple_of((1 - bit) * split, 8), split)
     for index, terms in enumerate(sources):
         views = [refs[term] if part is None else refs[term].at[part] for term, part in terms]
         next_ref[index] = sum(view[mine, :].astype(F32) for view in views)
@@ -369,8 +369,8 @@
 def merge_kernel(keep_ref, got_ref, other_ref, next_ref, send_ref):
     bit = exchange_bit(1)
     split = next_ref.shape[0]
-    mine = pl.ds(pl.multiple_of(bit * split, 16), split)
-    theirs = pl.ds(pl.multiple_of((1 - bit) * split, 16), split)
+    mine = pl.ds(pl.multiple_of(bit * split, 8), split)
+    theirs = pl.ds(pl.multiple_of((1 - bit) * split, 8), split)
     next_ref[...] = keep_ref[mine, :] + got_ref[mine, :].astype(F32)
     send_ref[0] = (keep_ref[theirs, :] + got_ref[theirs, :].astype(F32)).astype(BF16)
     send_ref[1] = other_ref[...]
@@ -399,7 +399,7 @@
     copies = []
     for part in range(2):
         for index in range(tile_count):
-            place = pl.ds(pl.multiple_of((mine ^ index) * chunk, 16), chunk)
+            place = pl.ds(pl.multiple_of((mine ^ index) * chunk, 8), chunk)
             tall[place, :] = quarters[index // count][index % count, part].astype(F32)
         for side in range(2):
             here_rows = slice(side * half, (side + 1) * half)

time: 95.9 us -> 95.3 us (level)
  no operation moved by 1% of the time
where the time goes in v6:
time: 95.3 us; the launch traced here: 95.1 us
  starting transfers between devices  44.3 us (46%)
  waiting for transfers between devices  28.3 us (30%)
  Pallas kernels  20 us (21%)
  local copies, waits for them, and re-layouts  1.54 us (2%)
    ppermute x12, starting transfers between devices, give(): return [lax.ppermute(v, 'tile', p) for v, p in zip(values, lists)]  30.9 us
    pallas_call x10, Pallas kernels, call(): pl.pallas_call(kernel, out_shape=list(outs), in_specs=[pl.BlockSpec(memor...  20 us
    ppermute x12, waiting for transfers between devices, give(): return [lax.ppermute(v, 'tile', p) for v, p in zip(values, lists)]  19.8 us
    ppermute x9, starting transfers between devices, trade(): return lax.ppermute(value, ('tile', 'chan'), pairs)  9.52 us
    ppermute x6, waiting for transfers between devices, swap_part(): return lax.ppermute(value, 'chan', [(i, i ^ bits) for i in range(4)])  4.31 us
    ppermute x9, waiting for transfers between devices, trade(): return lax.ppermute(value, ('tile', 'chan'), pairs)  4.25 us
    ppermute x6, starting transfers between devices, swap_part(): return lax.ppermute(value, 'chan', [(i, i ^ bits) for i in range(4)])  3.87 us
  transfers between devices with their start and end apart: 27, of which 12 were waited for; matrix products, arithmetic and copies ran while one was open for 2% of the time, Pallas kernels for 18%

profile of v6, /device:TPU:2, one launch (start us, length us, event | category | flops | bytes accessed | tf_op | source)
XLA Modules:
  0.0 95.1 jit_solution(2928251443739999021)
XLA Ops:
  3.6 2.0 %pack_sends.1 = (bf16[2,4,48,128]{3,2,1,0:T(8,128)(2,1)S(1)}, bf16[2,4,48,128]{3,2,1,0:T(8,128)(2,1)S(1)}, bf16[2,4,48,128]{3,2,1,0:T(8,128)(2,1)S(1)}, bf16[2,4...) custom-call(s32[1,8,4]{2,1,0:T(8,128)S(1)} %copy.16.lists_ref, ...), custom_call_target="tpu_custom_call" | custom-call | bytes 2666624 | tf_op jit(solution)/shard_map/pack_sends/pallas_call | solution.py:27
  5.6 5.5 %collective-permute-start.8 = (bf16[2,4,48,128]{3,2,1,0:T(8,128)(2,1)S(1)}, bf16[2,4,48,128]{3,2,1,0:T(8,128)(2,1)S(1)}, u32[]{:S(2)}, u32[]{:S(2)}) collective-permute-start(bf16[2,4,48,128]{3,2,1,0:T(8,128)(2,1)S(1)} %get-tuple-element.83), channel_id=1, source_target_pairs={{20,0},{24,4},{28,8},{0,20},{4,24},{8,28},{21,1},{25,5},{29,9},{1,... | collective-permute-start | bytes 294920 | tf_op jit(solution)/shard_map/ppermute | solution.py:455
  12.4 3.8 %partial_sums.2 = (f32[16,48,128]{2,1,0:T(8,128)S(1)}, bf16[3,4,48,128]{3,2,1,0:T(8,128)(2,1)S(1)}, bf16[3,4,48,128]{3,2,1,0:T(8,128)(2,1)S(1)}, bf16[1,4,48,128...) custom-call(s32[1,27,16]{2,1,0:T(8,128)S(1)} %copy.15.pin_ref, ...), custom_call_target="tpu_custom_call" | custom-call | flops 1019215872 | bytes 2514624 | tf_op jit(solution)/shard_map/partial_sums/pallas_call | solution.py:27
  16.2 3.4 %collective-permute-start.3 = (bf16[3,4,48,128]{3,2,1,0:T(8,128)(2,1)S(1)}, bf16[3,4,48,128]{3,2,1,0:T(8,128)(2,1)S(1)}, u32[]{:S(2)}, u32[]{:S(2)}) collective-permute-start(bf16[3,4,48,128]{3,2,1,0:T(8,128)(2,1)S(1)} %get-tuple-element.78), channel_id=1, source_target_pairs={{8,4},{24,20},{4,8},{20,24},{9,5},{25,21},{5,9},{21,25},{10,6},{26... | collective-permute-start | bytes 442376 | tf_op jit(solution)/shard_map/ppermute | solution.py:455
  19.7 5.9 %collective-permute-start.7 = (bf16[3,4,48,128]{3,2,1,0:T(8,128)(2,1)S(1)}, bf16[3,4,48,128]{3,2,1,0:T(8,128)(2,1)S(1)}, u32[]{:S(2)}, u32[]{:S(2)}) collective-permute-start(bf16[3,4,48,128]{3,2,1,0:T(8,128)(2,1)S(1)} %get-tuple-element.82), channel_id=1, source_target_pairs={{4,16},{8,20},{12,24},{16,4},{20,8},{24,12},{5,17},{9,21},{13,25},... | collective-permute-start | bytes 442376 | tf_op jit(solution)/shard_map/ppermute | solution.py:455
  25.6 3.1 %collective-permute-start.5 = (bf16[1,4,48,128]{3,2,1,0:T(8,128)(2,1)S(1)}, bf16[1,4,48,128]{3,2,1,0:T(8,128)(2,1)S(1)}, u32[]{:S(2)}, u32[]{:S(2)}) collective-permute-start(bf16[1,4,48,128]{3,2,1,0:T(8,128)(2,1)S(1)} %get-tuple-element.80), channel_id=1, source_target_pairs={{0,20},{4,24},{8,28},{20,0},{24,4},{28,8},{1,21},{5,25},{9,29},{21... | collective-permute-start | bytes 147464 | tf_op jit(solution)/shard_map/ppermute | solution.py:455
  28.9 5.5 %collective-permute-done.5.refs_2_ = bf16[1,4,48,128]{3,2,1,0:T(8,128)(2,1)S(1)} collective-permute-done((bf16[1,4,48,128]{3,2,1,0:T(8,128)(2,1)S(1)}, bf16[1,4,48,128]{3,2,1,0:T(8,128)(2,1)S(1)}, u32[]{:S(2)}, u32[]{:S(2)}) %collective-permute-start.5) | collective-permute-done | bytes 49184 | tf_op jit(solution)/shard_map/ppermute | solution.py:455
  36.9 3.2 %weight_sums.2 = (f32[992,128]{1,0:T(8,128)S(1)}, bf16[992,128]{1,0:T(8,128)(2,1)S(1)}) custom-call(s32[1,27,16]{2,1,0:T(8,128)S(1)} %copy.15.pin_ref, bf16[48,2048]{1,0:T(8,128)(2,1)S(1)} %get-tuple-element.72.other_ref.own_ref, bf16[48,2048]{1,0:T(8,128)(2,1)S(1)} %get-tuple-element.71.refs_0_.other_ref, ...), custom_call_target="tpu_custom_call" | custom-call | flops 1019215872 | bytes 2385600 | tf_op jit(solution)/shard_map/weight_sums/pallas_call | solution.py:27
  40.1 2.5 %collective-permute-done.10.refs_2_ = bf16[48,2048]{1,0:T(8,128)(2,1)S(1)} collective-permute-done((bf16[48,2048]{1,0:T(8,128)(2,1)S(1)}, bf16[48,2048]{1,0:T(8,128)(2,1)S(1)}, u32[]{:S(2)}, u32[]{:S(2)}) %collective-permute-start.10) | collective-permute-done | bytes 196640 | tf_op jit(solution)/shard_map/ppermute | solution.py:439
  44.1 3.2 %weight_sums.3 = (f32[496,128]{1,0:T(8,128)S(1)}, bf16[496,128]{1,0:T(8,128)(2,1)S(1)}, bf16[496,128]{1,0:T(8,128)(2,1)S(1)}, bf16[496,128]{1,0:T(8,128)(2,1)S(1)}) custom-call(s32[1,27,16]{2,1,0:T(8,128)S(1)} %copy.15.pin_ref, bf16[48,2048]{1,0:T(8,128)(2,1)S(1)} %get-tuple-element.95.own_ref, bf16[48,2048]{1,0:T(8,128)(2,1)S(1)} %settle.2.refs_0_, ...), custom_call_target="tpu_custom_call" | custom-call | flops 1019215872 | bytes 2258624 | tf_op jit(solution)/shard_map/weight_sums/pallas_call | solution.py:27
  50.7 1.8 %collective-permute-start.16 = (bf16[496,128]{1,0:T(8,128)(2,1)S(1)}, bf16[496,128]{1,0:T(8,128)(2,1)S(1)}, u32[]{:S(2)}, u32[]{:S(2)}) collective-permute-start(bf16[496,128]{1,0:T(8,128)(2,1)S(1)} %get-tuple-element.116), channel_id=1, source_target_pairs={{0,12},{1,13},{2,14},{3,15},{4,8},{5,9},{6,10},{7,11},{8,4},{9,5},... | collective-permute-start | bytes 380936 | tf_op jit(solution)/shard_map/ppermute | solution.py:342
  52.5 3.8 %partial_sums.3 = (f32[16,48,128]{2,1,0:T(8,128)S(1)}, bf16[1,4,48,128]{3,2,1,0:T(8,128)(2,1)S(1)}, bf16[1,4,48,128]{3,2,1,0:T(8,128)(2,1)S(1)}, bf16[1,4,48,128...) custom-call(s32[1,27,16]{2,1,0:T(8,128)S(1)} %copy.15.pin_ref, ...), custom_call_target="tpu_custom_call" | custom-call | flops 1019215872 | bytes 1924800 | tf_op jit(solution)/shard_map/partial_sums/pallas_call | solution.py:27
  56.8 2.1 %collective-permute-done.16.refs_4_ = bf16[496,128]{1,0:T(8,128)(2,1)S(1)} collective-permute-done((bf16[496,128]{1,0:T(8,128)(2,1)S(1)}, bf16[496,128]{1,0:T(8,128)(2,1)S(1)}, u32[]{:S(2)}, u32[]{:S(2)}) %collective-permute-start.16) | collective-permute-done | bytes 127008 | tf_op jit(solution)/shard_map/ppermute | solution.py:342
  59.0 2.1 %collective-permute-start.17 = (bf16[2,248,128]{2,1,0:T(8,128)(2,1)S(1)}, bf16[2,248,128]{2,1,0:T(8,128)(2,1)S(1)}, u32[]{:S(2)}, u32[]{:S(2)}) collective-permute-start(bf16[2,248,128]{2,1,0:T(8,128)(2,1)S(1)} %get-tuple-element.120), channel_id=1, source_target_pairs={{0,16},{1,17},{2,18},{3,19},{4,20},{5,21},{6,22},{7,23},{8,24},{9,... | collective-permute-start | bytes 380936 | tf_op jit(solution)/shard_map/ppermute | solution.py:342
  61.1 4.0 %collective-permute-start.18 = (bf16[1,4,48,128]{3,2,1,0:T(8,128)(2,1)S(1)}, bf16[1,4,48,128]{3,2,1,0:T(8,128)(2,1)S(1)}, u32[]{:S(2)}, u32[]{:S(2)}) collective-permute-start(bf16[1,4,48,128]{3,2,1,0:T(8,128)(2,1)S(1)} %get-tuple-element.121), channel_id=1, source_target_pairs={{8,4},{24,20},{4,8},{20,24},{9,5},{25,21},{5,9},{21,25},{10,6},{26... | collective-permute-start | bytes 147464 | tf_op jit(solution)/shard_map/ppermute | solution.py:455
  65.1 2.8 %collective-permute-done.18.refs_0_ = bf16[1,4,48,128]{3,2,1,0:T(8,128)(2,1)S(1)} collective-permute-done((bf16[1,4,48,128]{3,2,1,0:T(8,128)(2,1)S(1)}, bf16[1,4,48,128]{3,2,1,0:T(8,128)(2,1)S(1)}, u32[]{:S(2)}, u32[]{:S(2)}) %collective-permute-start.18) | collective-permute-done | bytes 49184 | tf_op jit(solution)/shard_map/ppermute | solution.py:455
  69.6 2.7 %collective-permute-start.21 = (bf16[1,4,48,128]{3,2,1,0:T(8,128)(2,1)S(1)}, bf16[1,4,48,128]{3,2,1,0:T(8,128)(2,1)S(1)}, u32[]{:S(2)}, u32[]{:S(2)}) collective-permute-start(bf16[1,4,48,128]{3,2,1,0:T(8,128)(2,1)S(1)} %get-tuple-element.129), channel_id=1, source_target_pairs={{0,16},{4,20},{8,24},{12,28},{16,0},{20,4},{24,8},{28,12},{1,17},{... | collective-permute-start | bytes 147464 | tf_op jit(solution)/shard_map/ppermute | solution.py:455
  72.3 4.3 %collective-permute-done.21.refs_3_ = bf16[1,4,48,128]{3,2,1,0:T(8,128)(2,1)S(1)} collective-permute-done((bf16[1,4,48,128]{3,2,1,0:T(8,128)(2,1)S(1)}, bf16[1,4,48,128]{3,2,1,0:T(8,128)(2,1)S(1)}, u32[]{:S(2)}, u32[]{:S(2)}) %collective-permute-start.21) | collective-permute-done | bytes 49184 | tf_op jit(solution)/shard_map/ppermute | solution.py:455
  77.9 2.3 %collective-permute-start.24 = (bf16[2,2,248,128]{3,2,1,0:T(8,128)(2,1)S(1)}, bf16[2,2,248,128]{3,2,1,0:T(8,128)(2,1)S(1)}, u32[]{:S(2)}, u32[]{:S(2)}) collective-permute-start(bf16[2,2,248,128]{3,2,1,0:T(8,128)(2,1)S(1)} %pad_maximum_fusion.refs_0_), channel_id=1, source_target_pairs={{0,8},{1,5},{2,10},{3,7},{4,12},{5,1},{6,14},{7,3},{8,0},{9,13},{1... | collective-permute-start | bytes 761864 | tf_op jit(solution)/shard_map/ppermute | solution.py:342
  80.1 4.0 %collective-permute-start.22 = (bf16[1,4,48,128]{3,2,1,0:T(8,128)(2,1)S(1)}, bf16[1,4,48,128]{3,2,1,0:T(8,128)(2,1)S(1)}, u32[]{:S(2)}, u32[]{:S(2)}) collective-permute-start(bf16[1,4,48,128]{3,2,1,0:T(8,128)(2,1)S(1)} %get-tuple-element.133), channel_id=1, source_target_pairs={{0,20},{4,24},{8,28},{20,0},{24,4},{28,8},{1,21},{5,25},{9,29},{21... | collective-permute-start | bytes 147464 | tf_op jit(solution)/shard_map/ppermute | solution.py:455
  84.2 1.9 %collective-permute-start.23 = (bf16[1,4,48,128]{3,2,1,0:T(8,128)(2,1)S(1)}, bf16[1,4,48,128]{3,2,1,0:T(8,128)(2,1)S(1)}, u32[]{:S(2)}, u32[]{:S(2)}) collective-permute-start(bf16[1,4,48,128]{3,2,1,0:T(8,128)(2,1)S(1)} %get-tuple-element.135), channel_id=1, source_target_pairs={{4,16},{8,20},{12,24},{16,4},{20,8},{24,12},{5,17},{9,21},{13,25},... | collective-permute-start | bytes 147464 | tf_op jit(solution)/shard_map/ppermute | solution.py:455
  86.1 3.9 %collective-permute-done.22.refs_2_ = bf16[1,4,48,128]{3,2,1,0:T(8,128)(2,1)S(1)} collective-permute-done((bf16[1,4,48,128]{3,2,1,0:T(8,128)(2,1)S(1)}, bf16[1,4,48,128]{3,2,1,0:T(8,128)(2,1)S(1)}, u32[]{:S(2)}, u32[]{:S(2)}) %collective-permute-start.22) | collective-permute-done | bytes 49184 | tf_op jit(solution)/shard_map/ppermute | solution.py:455
  90.0 2.0 %collective-permute-done.23.refs_4_ = bf16[1,4,48,128]{3,2,1,0:T(8,128)(2,1)S(1)} collective-permute-done((bf16[1,4,48,128]{3,2,1,0:T(8,128)(2,1)S(1)}, bf16[1,4,48,128]{3,2,1,0:T(8,128)(2,1)S(1)}, u32[]{:S(2)}, u32[]{:S(2)}) %collective-permute-start.23) | collective-permute-done | bytes 49184 | tf_op jit(solution)/shard_map/ppermute | solution.py:455
  93.4 1.7 %unpack_sums.1 = (f32[1296,192]{1,0:T(8,128)}, f32[1296,192]{1,0:T(8,128)}) custom-call(bf16[2,2,248,128]{3,2,1,0:T(8,128)(2,1)S(1)} %pad_maximum_fusion.refs_0_, bf16[2,2,248,128]{3,2,1,0:T(8,128)(2,1)S(1)} %collective-permute-done.24.refs_1_, bf16[2,2,248,128]{3,2,1,0:T(8,128)(2,1)S(1)} %collective-permute-done.25.refs_2_, ...), custom_call_target="tpu_custom_call" | custom-call | bytes 3006464 | tf_op jit(solution)/shard_map/unpack_sums/pallas_call | solution.py:27
  (46 shorter events, 16.7 us)
Async XLA Ops:
  0.6 11.4 %collective-permute-start = (bf16[48,2048]{1,0:T(8,128)(2,1)}, bf16[48,2048]{1,0:T(8,128)(2,1)S(1)}, u32[]{:S(2)}, u32[]{:S(2)}) collective-permute-start(bf16[48,2048]{1,0:T(8,128)(2,1)} %refs_2_.1), channel_id=1, source_target_pairs={{0,1},{1,0},{2,3},{3,2},{4,5},{5,4},{6,7},{7,6},{8,9},{9,8},{10,11... | collective-permute-start | bytes 589832 | tf_op jit(solution)/shard_map/ppermute | solution.py:439
  0.7 11.3 %collective-permute-start.2 = (bf16[48,2048]{1,0:T(8,128)(2,1)}, bf16[48,2048]{1,0:T(8,128)(2,1)S(1)}, u32[]{:S(2)}, u32[]{:S(2)}) collective-permute-start(bf16[48,2048]{1,0:T(8,128)(2,1)} %refs_2_.1), channel_id=1, source_target_pairs={{0,3},{1,2},{2,1},{3,0},{4,7},{5,6},{6,5},{7,4},{8,11},{9,10},{10,... | collective-permute-start | bytes 589832 | tf_op jit(solution)/shard_map/ppermute | solution.py:439
  2.3 10.1 %collective-permute-start.1 = (bf16[48,2048]{1,0:T(8,128)(2,1)}, bf16[48,2048]{1,0:T(8,128)(2,1)S(1)}, u32[]{:S(2)}, u32[]{:S(2)}) collective-permute-start(bf16[48,2048]{1,0:T(8,128)(2,1)} %refs_2_.1), channel_id=1, source_target_pairs={{0,2},{1,3},{2,0},{3,1},{4,6},{5,7},{6,4},{7,5},{8,10},{9,11},{10,... | collective-permute-start | bytes 589832 | tf_op jit(solution)/shard_map/ppermute | solution.py:439
  5.6 20.0 %collective-permute-start.8 = (bf16[2,4,48,128]{3,2,1,0:T(8,128)(2,1)S(1)}, bf16[2,4,48,128]{3,2,1,0:T(8,128)(2,1)S(1)}, u32[]{:S(2)}, u32[]{:S(2)}) collective-permute-start(bf16[2,4,48,128]{3,2,1,0:T(8,128)(2,1)S(1)} %get-tuple-element.83), channel_id=1, source_target_pairs={{20,0},{24,4},{28,8},{0,20},{4,24},{8,28},{21,1},{25,5},{29,9},{1,... | collective-permute-start | bytes 294920 | tf_op jit(solution)/shard_map/ppermute | solution.py:455
  11.1 17.7 %collective-permute-start.9 = (bf16[2,4,48,128]{3,2,1,0:T(8,128)(2,1)S(1)}, bf16[2,4,48,128]{3,2,1,0:T(8,128)(2,1)S(1)}, u32[]{:S(2)}, u32[]{:S(2)}) collective-permute-start(bf16[2,4,48,128]{3,2,1,0:T(8,128)(2,1)S(1)} %get-tuple-element.84), channel_id=1, source_target_pairs={{16,0},{20,4},{24,8},{28,12},{0,16},{4,20},{8,24},{12,28},{17,1},{... | collective-permute-start | bytes 294920 | tf_op jit(solution)/shard_map/ppermute | solution.py:455
  16.2 18.2 %collective-permute-start.3 = (bf16[3,4,48,128]{3,2,1,0:T(8,128)(2,1)S(1)}, bf16[3,4,48,128]{3,2,1,0:T(8,128)(2,1)S(1)}, u32[]{:S(2)}, u32[]{:S(2)}) collective-permute-start(bf16[3,4,48,128]{3,2,1,0:T(8,128)(2,1)S(1)} %get-tuple-element.78), channel_id=1, source_target_pairs={{8,4},{24,20},{4,8},{20,24},{9,5},{25,21},{5,9},{21,25},{10,6},{26... | collective-permute-start | bytes 442376 | tf_op jit(solution)/shard_map/ppermute | solution.py:455
  19.6 14.8 %collective-permute-start.4 = (bf16[3,4,48,128]{3,2,1,0:T(8,128)(2,1)S(1)}, bf16[3,4,48,128]{3,2,1,0:T(8,128)(2,1)S(1)}, u32[]{:S(2)}, u32[]{:S(2)}) collective-permute-start(bf16[3,4,48,128]{3,2,1,0:T(8,128)(2,1)S(1)} %get-tuple-element.79), channel_id=1, source_target_pairs={{4,0},{12,8},{20,16},{28,24},{0,4},{8,12},{16,20},{24,28},{5,1},{1... | collective-permute-start | bytes 442376 | tf_op jit(solution)/shard_map/ppermute | solution.py:455
  19.7 14.7 %collective-permute-start.7 = (bf16[3,4,48,128]{3,2,1,0:T(8,128)(2,1)S(1)}, bf16[3,4,48,128]{3,2,1,0:T(8,128)(2,1)S(1)}, u32[]{:S(2)}, u32[]{:S(2)}) collective-permute-start(bf16[3,4,48,128]{3,2,1,0:T(8,128)(2,1)S(1)} %get-tuple-element.82), channel_id=1, source_target_pairs={{4,16},{8,20},{12,24},{16,4},{20,8},{24,12},{5,17},{9,21},{13,25},... | collective-permute-start | bytes 442376 | tf_op jit(solution)/shard_map/ppermute | solution.py:455
  25.6 8.8 %collective-permute-start.5 = (bf16[1,4,48,128]{3,2,1,0:T(8,128)(2,1)S(1)}, bf16[1,4,48,128]{3,2,1,0:T(8,128)(2,1)S(1)}, u32[]{:S(2)}, u32[]{:S(2)}) collective-permute-start(bf16[1,4,48,128]{3,2,1,0:T(8,128)(2,1)S(1)} %get-tuple-element.80), channel_id=1, source_target_pairs={{0,20},{4,24},{8,28},{20,0},{24,4},{28,8},{1,21},{5,25},{9,29},{21... | collective-permute-start | bytes 147464 | tf_op jit(solution)/shard_map/ppermute | solution.py:455
  28.8 5.6 %collective-permute-start.6 = (bf16[1,4,48,128]{3,2,1,0:T(8,128)(2,1)S(1)}, bf16[1,4,48,128]{3,2,1,0:T(8,128)(2,1)S(1)}, u32[]{:S(2)}, u32[]{:S(2)}) collective-permute-start(bf16[1,4,48,128]{3,2,1,0:T(8,128)(2,1)S(1)} %get-tuple-element.81), channel_id=1, source_target_pairs={{0,16},{4,20},{8,24},{12,28},{16,0},{20,4},{24,8},{28,12},{1,17},{... | collective-permute-start | bytes 147464 | tf_op jit(solution)/shard_map/ppermute | solution.py:455
  35.3 7.3 %collective-permute-start.10 = (bf16[48,2048]{1,0:T(8,128)(2,1)S(1)}, bf16[48,2048]{1,0:T(8,128)(2,1)S(1)}, u32[]{:S(2)}, u32[]{:S(2)}) collective-permute-start(bf16[48,2048]{1,0:T(8,128)(2,1)S(1)} %settle.2.refs_0_), channel_id=1, source_target_pairs={{0,2},{1,3},{2,0},{3,1},{4,6},{5,7},{6,4},{7,5},{8,10},{9,11},{10,... | collective-permute-start | bytes 589832 | tf_op jit(solution)/shard_map/ppermute | solution.py:439
  42.6 6.3 %collective-permute-start.13 = (bf16[992,128]{1,0:T(8,128)(2,1)S(1)}, bf16[992,128]{1,0:T(8,128)(2,1)S(1)}, u32[]{:S(2)}, u32[]{:S(2)}) collective-permute-start(bf16[992,128]{1,0:T(8,128)(2,1)S(1)} %get-tuple-element.92), channel_id=1, source_target_pairs={{0,4},{1,9},{2,6},{3,11},{4,0},{5,13},{6,2},{7,15},{8,12},{9,1},{1... | collective-permute-start | bytes 761864 | tf_op jit(solution)/shard_map/ppermute | solution.py:342
  49.0 7.8 %collective-permute-start.14 = (bf16[2,496,128]{2,1,0:T(8,128)(2,1)S(1)}, bf16[2,496,128]{2,1,0:T(8,128)(2,1)S(1)}, u32[]{:S(2)}, u32[]{:S(2)}) collective-permute-start(bf16[2,496,128]{2,1,0:T(8,128)(2,1)S(1)} %get-tuple-element.107), channel_id=1, source_target_pairs={{0,8},{1,5},{2,10},{3,7},{4,12},{5,1},{6,14},{7,3},{8,0},{9,13},{1... | collective-permute-start | bytes 761864 | tf_op jit(solution)/shard_map/ppermute | solution.py:342
  49.0 7.8 %collective-permute-start.15 = (bf16[496,128]{1,0:T(8,128)(2,1)S(1)}, bf16[496,128]{1,0:T(8,128)(2,1)S(1)}, u32[]{:S(2)}, u32[]{:S(2)}) collective-permute-start(bf16[496,128]{1,0:T(8,128)(2,1)S(1)} %get-tuple-element.115), channel_id=1, source_target_pairs={{0,4},{1,9},{2,6},{3,11},{4,0},{5,13},{6,2},{7,15},{8,12},{9,1},{1... | collective-permute-start | bytes 380936 | tf_op jit(solution)/shard_map/ppermute | solution.py:342
  50.7 8.2 %collective-permute-start.16 = (bf16[496,128]{1,0:T(8,128)(2,1)S(1)}, bf16[496,128]{1,0:T(8,128)(2,1)S(1)}, u32[]{:S(2)}, u32[]{:S(2)}) collective-permute-start(bf16[496,128]{1,0:T(8,128)(2,1)S(1)} %get-tuple-element.116), channel_id=1, source_target_pairs={{0,12},{1,13},{2,14},{3,15},{4,8},{5,9},{6,10},{7,11},{8,4},{9,5},... | collective-permute-start | bytes 380936 | tf_op jit(solution)/shard_map/ppermute | solution.py:342
  59.0 10.2 %collective-permute-start.17 = (bf16[2,248,128]{2,1,0:T(8,128)(2,1)S(1)}, bf16[2,248,128]{2,1,0:T(8,128)(2,1)S(1)}, u32[]{:S(2)}, u32[]{:S(2)}) collective-permute-start(bf16[2,248,128]{2,1,0:T(8,128)(2,1)S(1)} %get-tuple-element.120), channel_id=1, source_target_pairs={{0,16},{1,17},{2,18},{3,19},{4,20},{5,21},{6,22},{7,23},{8,24},{9,... | collective-permute-start | bytes 380936 | tf_op jit(solution)/shard_map/ppermute | solution.py:342
  61.1 6.9 %collective-permute-start.18 = (bf16[1,4,48,128]{3,2,1,0:T(8,128)(2,1)S(1)}, bf16[1,4,48,128]{3,2,1,0:T(8,128)(2,1)S(1)}, u32[]{:S(2)}, u32[]{:S(2)}) collective-permute-start(bf16[1,4,48,128]{3,2,1,0:T(8,128)(2,1)S(1)} %get-tuple-element.121), channel_id=1, source_target_pairs={{8,4},{24,20},{4,8},{20,24},{9,5},{25,21},{5,9},{21,25},{10,6},{26... | collective-permute-start | bytes 147464 | tf_op jit(solution)/shard_map/ppermute | solution.py:455
  69.3 7.3 %collective-permute-start.20 = (bf16[1,2,248,128]{3,2,1,0:T(8,128)(2,1)S(1)}, bf16[1,2,248,128]{3,2,1,0:T(8,128)(2,1)S(1)}, u32[]{:S(2)}, u32[]{:S(2)}) collective-permute-start(bf16[1,2,248,128]{3,2,1,0:T(8,128)(2,1)S(1)} %fusion), channel_id=1, source_target_pairs={{0,16},{1,17},{2,18},{3,19},{4,20},{5,21},{6,22},{7,23},{8,24},{9,... | collective-permute-start | bytes 380936 | tf_op jit(solution)/shard_map/ppermute | solution.py:342
  69.6 7.0 %collective-permute-start.21 = (bf16[1,4,48,128]{3,2,1,0:T(8,128)(2,1)S(1)}, bf16[1,4,48,128]{3,2,1,0:T(8,128)(2,1)S(1)}, u32[]{:S(2)}, u32[]{:S(2)}) collective-permute-start(bf16[1,4,48,128]{3,2,1,0:T(8,128)(2,1)S(1)} %get-tuple-element.129), channel_id=1, source_target_pairs={{0,16},{4,20},{8,24},{12,28},{16,0},{20,4},{24,8},{28,12},{1,17},{... | collective-permute-start | bytes 147464 | tf_op jit(solution)/shard_map/ppermute | solution.py:455
  76.6 16.8 %collective-permute-start.26 = (bf16[2,2,248,128]{3,2,1,0:T(8,128)(2,1)S(1)}, bf16[2,2,248,128]{3,2,1,0:T(8,128)(2,1)S(1)}, u32[]{:S(2)}, u32[]{:S(2)}) collective-permute-start(bf16[2,2,248,128]{3,2,1,0:T(8,128)(2,1)S(1)} %pad_maximum_fusion.refs_0_), channel_id=1, source_target_pairs={{0,12},{1,13},{2,14},{3,15},{4,8},{5,9},{6,10},{7,11},{8,4},{9,5},... | collective-permute-start | bytes 761864 | tf_op jit(solution)/shard_map/ppermute | solution.py:342
  77.2 16.2 %collective-permute-start.25 = (bf16[2,2,248,128]{3,2,1,0:T(8,128)(2,1)S(1)}, bf16[2,2,248,128]{3,2,1,0:T(8,128)(2,1)S(1)}, u32[]{:S(2)}, u32[]{:S(2)}) collective-permute-start(bf16[2,2,248,128]{3,2,1,0:T(8,128)(2,1)S(1)} %pad_maximum_fusion.refs_0_), channel_id=1, source_target_pairs={{0,4},{1,9},{2,6},{3,11},{4,0},{5,13},{6,2},{7,15},{8,12},{9,1},{1... | collective-permute-start | bytes 761864 | tf_op jit(solution)/shard_map/ppermute | solution.py:342
  77.9 15.6 %collective-permute-start.24 = (bf16[2,2,248,128]{3,2,1,0:T(8,128)(2,1)S(1)}, bf16[2,2,248,128]{3,2,1,0:T(8,128)(2,1)S(1)}, u32[]{:S(2)}, u32[]{:S(2)}) collective-permute-start(bf16[2,2,248,128]{3,2,1,0:T(8,128)(2,1)S(1)} %pad_maximum_fusion.refs_0_), channel_id=1, source_target_pairs={{0,8},{1,5},{2,10},{3,7},{4,12},{5,1},{6,14},{7,3},{8,0},{9,13},{1... | collective-permute-start | bytes 761864 | tf_op jit(solution)/shard_map/ppermute | solution.py:342
  80.1 9.9 %collective-permute-start.22 = (bf16[1,4,48,128]{3,2,1,0:T(8,128)(2,1)S(1)}, bf16[1,4,48,128]{3,2,1,0:T(8,128)(2,1)S(1)}, u32[]{:S(2)}, u32[]{:S(2)}) collective-permute-start(bf16[1,4,48,128]{3,2,1,0:T(8,128)(2,1)S(1)} %get-tuple-element.133), channel_id=1, source_target_pairs={{0,20},{4,24},{8,28},{20,0},{24,4},{28,8},{1,21},{5,25},{9,29},{21... | collective-permute-start | bytes 147464 | tf_op jit(solution)/shard_map/ppermute | solution.py:455
  84.2 7.8 %collective-permute-start.23 = (bf16[1,4,48,128]{3,2,1,0:T(8,128)(2,1)S(1)}, bf16[1,4,48,128]{3,2,1,0:T(8,128)(2,1)S(1)}, u32[]{:S(2)}, u32[]{:S(2)}) collective-permute-start(bf16[1,4,48,128]{3,2,1,0:T(8,128)(2,1)S(1)} %get-tuple-element.135), channel_id=1, source_target_pairs={{4,16},{8,20},{12,24},{16,4},{20,8},{24,12},{5,17},{9,21},{13,25},... | collective-permute-start | bytes 147464 | tf_op jit(solution)/shard_map/ppermute | solution.py:455
  (4 other events, 19.0 us)

commit v7 on v6

--- a/solution.py
+++ b/solution.py
@@ -456,7 +456,7 @@
 
     back_lists = [[(t, s) for s, t in p] for p in pair_lists]
 
-    early = range(2, min(4, len(pair_lists)))
+    early = (3, 2)
     riders = [g for g in range(len(pair_lists)) if g not in early]
 
     far, near, last = (swap_part(cotangent, bits) for bits in (2, 1, 3))
@@ -489,7 +489,6 @@
     got_one = trade(send, 1)
     pre_parts, keep_one = tie(pre_parts, keep_one)
     local_one, backs = partial_sums(pair_in, plan, pre_parts, weight_one, slot_count)
-    got_one, backs = tie(got_one, backs)
     shares = [[0, 1], [3], [2] + list(range(4, len(backs)))]
     returned = [None] * len(backs)
 

time: 95.3 us -> 95.3 us (level)
  transfers between devices with their start and end apart: 27 -> 27, of which waited for: 12 -> 11; matrix products, arithmetic and copies ran while one was open for 2% -> 2% of each run, Pallas kernels for 18% -> 18%
where the time goes in v7:
time: 95.3 us; the launch traced here: 94.8 us
  starting transfers between devices  44.3 us (46%)
  waiting for transfers between devices  28.2 us (30%)
  Pallas kernels  19.9 us (21%)
  local copies, waits for them, and re-layouts  1.54 us (2%)
    ppermute x12, starting transfers between devices, give(): return [lax.ppermute(v, 'tile', p) for v, p in zip(values, lists)]  30.9 us
    pallas_call x10, Pallas kernels, call(): pl.pallas_call(kernel, out_shape=list(outs), in_specs=[pl.BlockSpec(memor...  19.9 us
    ppermute x12, waiting for transfers between devices, give(): return [lax.ppermute(v, 'tile', p) for v, p in zip(values, lists)]  19.9 us
    ppermute x9, starting transfers between devices, trade(): return lax.ppermute(value, ('tile', 'chan'), pairs)  9.57 us
    ppermute x9, waiting for transfers between devices, trade(): return lax.ppermute(value, ('tile', 'chan'), pairs)  4.31 us
    ppermute x6, waiting for transfers between devices, swap_part(): return lax.ppermute(value, 'chan', [(i, i ^ bits) for i in range(4)])  4 us
    ppermute x6, starting transfers between devices, swap_part(): return lax.ppermute(value, 'chan', [(i, i ^ bits) for i in range(4)])  3.87 us
  transfers between devices with their start and end apart: 27, of which 11 were waited for; matrix products, arithmetic and copies ran while one was open for 2% of the time, Pallas kernels for 18%

profile of v7, /device:TPU:2, one launch (start us, length us, event | category | flops | bytes accessed | tf_op | source)
XLA Modules:
  0.0 94.8 jit_solution(14640563549455019864)
XLA Ops:
  3.6 2.0 %pack_sends.1 = (bf16[2,4,48,128]{3,2,1,0:T(8,128)(2,1)S(1)}, bf16[2,4,48,128]{3,2,1,0:T(8,128)(2,1)S(1)}, bf16[2,4,48,128]{3,2,1,0:T(8,128)(2,1)S(1)}, bf16[2,4...) custom-call(s32[1,8,4]{2,1,0:T(8,128)S(1)} %copy.16.lists_ref, ...), custom_call_target="tpu_custom_call" | custom-call | bytes 2666624 | tf_op jit(solution)/shard_map/pack_sends/pallas_call | solution.py:27
  5.6 2.7 %collective-permute-start.8 = (bf16[2,4,48,128]{3,2,1,0:T(8,128)(2,1)S(1)}, bf16[2,4,48,128]{3,2,1,0:T(8,128)(2,1)S(1)}, u32[]{:S(2)}, u32[]{:S(2)}) collective-permute-start(bf16[2,4,48,128]{3,2,1,0:T(8,128)(2,1)S(1)} %get-tuple-element.77), channel_id=1, source_target_pairs={{16,0},{20,4},{24,8},{28,12},{0,16},{4,20},{8,24},{12,28},{17,1},{... | collective-permute-start | bytes 294920 | tf_op jit(solution)/shard_map/ppermute | solution.py:455
  8.3 3.2 %collective-permute-start.9 = (bf16[2,4,48,128]{3,2,1,0:T(8,128)(2,1)S(1)}, bf16[2,4,48,128]{3,2,1,0:T(8,128)(2,1)S(1)}, u32[]{:S(2)}, u32[]{:S(2)}) collective-permute-start(bf16[2,4,48,128]{3,2,1,0:T(8,128)(2,1)S(1)} %get-tuple-element.78), channel_id=1, source_target_pairs={{20,0},{24,4},{28,8},{0,20},{4,24},{8,28},{21,1},{25,5},{29,9},{1,... | collective-permute-start | bytes 294920 | tf_op jit(solution)/shard_map/ppermute | solution.py:455
  12.4 3.7 %partial_sums.2 = (f32[16,48,128]{2,1,0:T(8,128)S(1)}, bf16[3,4,48,128]{3,2,1,0:T(8,128)(2,1)S(1)}, bf16[3,4,48,128]{3,2,1,0:T(8,128)(2,1)S(1)}, bf16[1,4,48,128...) custom-call(s32[1,27,16]{2,1,0:T(8,128)S(1)} %copy.15.pin_ref, ...), custom_call_target="tpu_custom_call" | custom-call | flops 1019215872 | bytes 2514624 | tf_op jit(solution)/shard_map/partial_sums/pallas_call | solution.py:27
  16.1 3.4 %collective-permute-start.3 = (bf16[3,4,48,128]{3,2,1,0:T(8,128)(2,1)S(1)}, bf16[3,4,48,128]{3,2,1,0:T(8,128)(2,1)S(1)}, u32[]{:S(2)}, u32[]{:S(2)}) collective-permute-start(bf16[3,4,48,128]{3,2,1,0:T(8,128)(2,1)S(1)} %get-tuple-element.72), channel_id=1, source_target_pairs={{8,4},{24,20},{4,8},{20,24},{9,5},{25,21},{5,9},{21,25},{10,6},{26... | collective-permute-start | bytes 442376 | tf_op jit(solution)/shard_map/ppermute | solution.py:455
  19.7 6.0 %collective-permute-start.7 = (bf16[3,4,48,128]{3,2,1,0:T(8,128)(2,1)S(1)}, bf16[3,4,48,128]{3,2,1,0:T(8,128)(2,1)S(1)}, u32[]{:S(2)}, u32[]{:S(2)}) collective-permute-start(bf16[3,4,48,128]{3,2,1,0:T(8,128)(2,1)S(1)} %get-tuple-element.76), channel_id=1, source_target_pairs={{4,16},{8,20},{12,24},{16,4},{20,8},{24,12},{5,17},{9,21},{13,25},... | collective-permute-start | bytes 442376 | tf_op jit(solution)/shard_map/ppermute | solution.py:455
  25.7 3.0 %collective-permute-start.5 = (bf16[1,4,48,128]{3,2,1,0:T(8,128)(2,1)S(1)}, bf16[1,4,48,128]{3,2,1,0:T(8,128)(2,1)S(1)}, u32[]{:S(2)}, u32[]{:S(2)}) collective-permute-start(bf16[1,4,48,128]{3,2,1,0:T(8,128)(2,1)S(1)} %get-tuple-element.74), channel_id=1, source_target_pairs={{0,20},{4,24},{8,28},{20,0},{24,4},{28,8},{1,21},{5,25},{9,29},{21... | collective-permute-start | bytes 147464 | tf_op jit(solution)/shard_map/ppermute | solution.py:455
  28.8 5.6 %collective-permute-done.5.refs_2_ = bf16[1,4,48,128]{3,2,1,0:T(8,128)(2,1)S(1)} collective-permute-done((bf16[1,4,48,128]{3,2,1,0:T(8,128)(2,1)S(1)}, bf16[1,4,48,128]{3,2,1,0:T(8,128)(2,1)S(1)}, u32[]{:S(2)}, u32[]{:S(2)}) %collective-permute-start.5) | collective-permute-done | bytes 49184 | tf_op jit(solution)/shard_map/ppermute | solution.py:455
  36.9 3.2 %weight_sums.2 = (f32[992,128]{1,0:T(8,128)S(1)}, bf16[992,128]{1,0:T(8,128)(2,1)S(1)}) custom-call(s32[1,27,16]{2,1,0:T(8,128)S(1)} %copy.15.pin_ref, bf16[48,2048]{1,0:T(8,128)(2,1)S(1)} %get-tuple-element.66.other_ref.own_ref, bf16[48,2048]{1,0:T(8,128)(2,1)S(1)} %get-tuple-element.65.refs_0_.other_ref, ...), custom_call_target="tpu_custom_call" | custom-call | flops 1019215872 | bytes 2385600 | tf_op jit(solution)/shard_map/weight_sums/pallas_call | solution.py:27
  40.1 2.5 %collective-permute-done.10.refs_2_ = bf16[48,2048]{1,0:T(8,128)(2,1)S(1)} collective-permute-done((bf16[48,2048]{1,0:T(8,128)(2,1)S(1)}, bf16[48,2048]{1,0:T(8,128)(2,1)S(1)}, u32[]{:S(2)}, u32[]{:S(2)}) %collective-permute-start.10) | collective-permute-done | bytes 196640 | tf_op jit(solution)/shard_map/ppermute | solution.py:439
  44.1 3.2 %weight_sums.3 = (f32[496,128]{1,0:T(8,128)S(1)}, bf16[496,128]{1,0:T(8,128)(2,1)S(1)}, bf16[496,128]{1,0:T(8,128)(2,1)S(1)}, bf16[496,128]{1,0:T(8,128)(2,1)S(1)}) custom-call(s32[1,27,16]{2,1,0:T(8,128)S(1)} %copy.15.pin_ref, bf16[48,2048]{1,0:T(8,128)(2,1)S(1)} %get-tuple-element.89.own_ref, bf16[48,2048]{1,0:T(8,128)(2,1)S(1)} %settle.2.refs_0_, ...), custom_call_target="tpu_custom_call" | custom-call | flops 1019215872 | bytes 2258624 | tf_op jit(solution)/shard_map/weight_sums/pallas_call | solution.py:27
  50.7 1.8 %collective-permute-start.16 = (bf16[496,128]{1,0:T(8,128)(2,1)S(1)}, bf16[496,128]{1,0:T(8,128)(2,1)S(1)}, u32[]{:S(2)}, u32[]{:S(2)}) collective-permute-start(bf16[496,128]{1,0:T(8,128)(2,1)S(1)} %get-tuple-element.104), channel_id=1, source_target_pairs={{0,12},{1,13},{2,14},{3,15},{4,8},{5,9},{6,10},{7,11},{8,4},{9,5},... | collective-permute-start | bytes 380936 | tf_op jit(solution)/shard_map/ppermute | solution.py:342
  52.6 3.7 %partial_sums.3 = (f32[16,48,128]{2,1,0:T(8,128)S(1)}, bf16[1,4,48,128]{3,2,1,0:T(8,128)(2,1)S(1)}, bf16[1,4,48,128]{3,2,1,0:T(8,128)(2,1)S(1)}, bf16[1,4,48,128...) custom-call(s32[1,27,16]{2,1,0:T(8,128)S(1)} %copy.15.pin_ref, ...), custom_call_target="tpu_custom_call" | custom-call | flops 1019215872 | bytes 1924800 | tf_op jit(solution)/shard_map/partial_sums/pallas_call | solution.py:27
  56.3 2.6 %collective-permute-done.16.refs_4_ = bf16[496,128]{1,0:T(8,128)(2,1)S(1)} collective-permute-done((bf16[496,128]{1,0:T(8,128)(2,1)S(1)}, bf16[496,128]{1,0:T(8,128)(2,1)S(1)}, u32[]{:S(2)}, u32[]{:S(2)}) %collective-permute-start.16) | collective-permute-done | bytes 127008 | tf_op jit(solution)/shard_map/ppermute | solution.py:342
  59.0 2.1 %collective-permute-start.17 = (bf16[2,248,128]{2,1,0:T(8,128)(2,1)S(1)}, bf16[2,248,128]{2,1,0:T(8,128)(2,1)S(1)}, u32[]{:S(2)}, u32[]{:S(2)}) collective-permute-start(bf16[2,248,128]{2,1,0:T(8,128)(2,1)S(1)} %get-tuple-element.108), channel_id=1, source_target_pairs={{0,16},{1,17},{2,18},{3,19},{4,20},{5,21},{6,22},{7,23},{8,24},{9,... | collective-permute-start | bytes 380936 | tf_op jit(solution)/shard_map/ppermute | solution.py:342
  61.1 4.0 %collective-permute-start.18 = (bf16[1,4,48,128]{3,2,1,0:T(8,128)(2,1)S(1)}, bf16[1,4,48,128]{3,2,1,0:T(8,128)(2,1)S(1)}, u32[]{:S(2)}, u32[]{:S(2)}) collective-permute-start(bf16[1,4,48,128]{3,2,1,0:T(8,128)(2,1)S(1)} %get-tuple-element.109), channel_id=1, source_target_pairs={{8,4},{24,20},{4,8},{20,24},{9,5},{25,21},{5,9},{21,25},{10,6},{26... | collective-permute-start | bytes 147464 | tf_op jit(solution)/shard_map/ppermute | solution.py:455
  65.2 2.8 %collective-permute-done.18.refs_0_ = bf16[1,4,48,128]{3,2,1,0:T(8,128)(2,1)S(1)} collective-permute-done((bf16[1,4,48,128]{3,2,1,0:T(8,128)(2,1)S(1)}, bf16[1,4,48,128]{3,2,1,0:T(8,128)(2,1)S(1)}, u32[]{:S(2)}, u32[]{:S(2)}) %collective-permute-start.18) | collective-permute-done | bytes 49184 | tf_op jit(solution)/shard_map/ppermute | solution.py:455
  69.6 2.7 %collective-permute-start.21 = (bf16[1,4,48,128]{3,2,1,0:T(8,128)(2,1)S(1)}, bf16[1,4,48,128]{3,2,1,0:T(8,128)(2,1)S(1)}, u32[]{:S(2)}, u32[]{:S(2)}) collective-permute-start(bf16[1,4,48,128]{3,2,1,0:T(8,128)(2,1)S(1)} %get-tuple-element.117), channel_id=1, source_target_pairs={{0,16},{4,20},{8,24},{12,28},{16,0},{20,4},{24,8},{28,12},{1,17},{... | collective-permute-start | bytes 147464 | tf_op jit(solution)/shard_map/ppermute | solution.py:455
  72.3 4.3 %collective-permute-done.21.refs_3_ = bf16[1,4,48,128]{3,2,1,0:T(8,128)(2,1)S(1)} collective-permute-done((bf16[1,4,48,128]{3,2,1,0:T(8,128)(2,1)S(1)}, bf16[1,4,48,128]{3,2,1,0:T(8,128)(2,1)S(1)}, u32[]{:S(2)}, u32[]{:S(2)}) %collective-permute-start.21) | collective-permute-done | bytes 49184 | tf_op jit(solution)/shard_map/ppermute | solution.py:455
  77.9 2.3 %collective-permute-start.24 = (bf16[2,2,248,128]{3,2,1,0:T(8,128)(2,1)S(1)}, bf16[2,2,248,128]{3,2,1,0:T(8,128)(2,1)S(1)}, u32[]{:S(2)}, u32[]{:S(2)}) collective-permute-start(bf16[2,2,248,128]{3,2,1,0:T(8,128)(2,1)S(1)} %pad_maximum_fusion.refs_0_), channel_id=1, source_target_pairs={{0,8},{1,5},{2,10},{3,7},{4,12},{5,1},{6,14},{7,3},{8,0},{9,13},{1... | collective-permute-start | bytes 761864 | tf_op jit(solution)/shard_map/ppermute | solution.py:342
  80.2 3.7 %collective-permute-start.22 = (bf16[1,4,48,128]{3,2,1,0:T(8,128)(2,1)S(1)}, bf16[1,4,48,128]{3,2,1,0:T(8,128)(2,1)S(1)}, u32[]{:S(2)}, u32[]{:S(2)}) collective-permute-start(bf16[1,4,48,128]{3,2,1,0:T(8,128)(2,1)S(1)} %get-tuple-element.121), channel_id=1, source_target_pairs={{0,20},{4,24},{8,28},{20,0},{24,4},{28,8},{1,21},{5,25},{9,29},{21... | collective-permute-start | bytes 147464 | tf_op jit(solution)/shard_map/ppermute | solution.py:455
  83.9 1.9 %collective-permute-start.23 = (bf16[1,4,48,128]{3,2,1,0:T(8,128)(2,1)S(1)}, bf16[1,4,48,128]{3,2,1,0:T(8,128)(2,1)S(1)}, u32[]{:S(2)}, u32[]{:S(2)}) collective-permute-start(bf16[1,4,48,128]{3,2,1,0:T(8,128)(2,1)S(1)} %get-tuple-element.123), channel_id=1, source_target_pairs={{4,16},{8,20},{12,24},{16,4},{20,8},{24,12},{5,17},{9,21},{13,25},... | collective-permute-start | bytes 147464 | tf_op jit(solution)/shard_map/ppermute | solution.py:455
  85.9 3.3 %collective-permute-done.22.refs_2_ = bf16[1,4,48,128]{3,2,1,0:T(8,128)(2,1)S(1)} collective-permute-done((bf16[1,4,48,128]{3,2,1,0:T(8,128)(2,1)S(1)}, bf16[1,4,48,128]{3,2,1,0:T(8,128)(2,1)S(1)}, u32[]{:S(2)}, u32[]{:S(2)}) %collective-permute-start.22) | collective-permute-done | bytes 49184 | tf_op jit(solution)/shard_map/ppermute | solution.py:455
  89.2 2.6 %collective-permute-done.23.refs_4_ = bf16[1,4,48,128]{3,2,1,0:T(8,128)(2,1)S(1)} collective-permute-done((bf16[1,4,48,128]{3,2,1,0:T(8,128)(2,1)S(1)}, bf16[1,4,48,128]{3,2,1,0:T(8,128)(2,1)S(1)}, u32[]{:S(2)}, u32[]{:S(2)}) %collective-permute-start.23) | collective-permute-done | bytes 49184 | tf_op jit(solution)/shard_map/ppermute | solution.py:455
  (46 shorter events, 17.6 us)
Async XLA Ops:
  0.6 11.7 %collective-permute-start = (bf16[48,2048]{1,0:T(8,128)(2,1)}, bf16[48,2048]{1,0:T(8,128)(2,1)S(1)}, u32[]{:S(2)}, u32[]{:S(2)}) collective-permute-start(bf16[48,2048]{1,0:T(8,128)(2,1)} %refs_2_.1), channel_id=1, source_target_pairs={{0,1},{1,0},{2,3},{3,2},{4,5},{5,4},{6,7},{7,6},{8,9},{9,8},{10,11... | collective-permute-start | bytes 589832 | tf_op jit(solution)/shard_map/ppermute | solution.py:439
  0.7 11.6 %collective-permute-start.2 = (bf16[48,2048]{1,0:T(8,128)(2,1)}, bf16[48,2048]{1,0:T(8,128)(2,1)S(1)}, u32[]{:S(2)}, u32[]{:S(2)}) collective-permute-start(bf16[48,2048]{1,0:T(8,128)(2,1)} %refs_2_.1), channel_id=1, source_target_pairs={{0,3},{1,2},{2,1},{3,0},{4,7},{5,6},{6,5},{7,4},{8,11},{9,10},{10,... | collective-permute-start | bytes 589832 | tf_op jit(solution)/shard_map/ppermute | solution.py:439
  2.3 10.1 %collective-permute-start.1 = (bf16[48,2048]{1,0:T(8,128)(2,1)}, bf16[48,2048]{1,0:T(8,128)(2,1)S(1)}, u32[]{:S(2)}, u32[]{:S(2)}) collective-permute-start(bf16[48,2048]{1,0:T(8,128)(2,1)} %refs_2_.1), channel_id=1, source_target_pairs={{0,2},{1,3},{2,0},{3,1},{4,6},{5,7},{6,4},{7,5},{8,10},{9,11},{10,... | collective-permute-start | bytes 589832 | tf_op jit(solution)/shard_map/ppermute | solution.py:439
  5.6 20.0 %collective-permute-start.8 = (bf16[2,4,48,128]{3,2,1,0:T(8,128)(2,1)S(1)}, bf16[2,4,48,128]{3,2,1,0:T(8,128)(2,1)S(1)}, u32[]{:S(2)}, u32[]{:S(2)}) collective-permute-start(bf16[2,4,48,128]{3,2,1,0:T(8,128)(2,1)S(1)} %get-tuple-element.77), channel_id=1, source_target_pairs={{16,0},{20,4},{24,8},{28,12},{0,16},{4,20},{8,24},{12,28},{17,1},{... | collective-permute-start | bytes 294920 | tf_op jit(solution)/shard_map/ppermute | solution.py:455
  8.3 20.4 %collective-permute-start.9 = (bf16[2,4,48,128]{3,2,1,0:T(8,128)(2,1)S(1)}, bf16[2,4,48,128]{3,2,1,0:T(8,128)(2,1)S(1)}, u32[]{:S(2)}, u32[]{:S(2)}) collective-permute-start(bf16[2,4,48,128]{3,2,1,0:T(8,128)(2,1)S(1)} %get-tuple-element.78), channel_id=1, source_target_pairs={{20,0},{24,4},{28,8},{0,20},{4,24},{8,28},{21,1},{25,5},{29,9},{1,... | collective-permute-start | bytes 294920 | tf_op jit(solution)/shard_map/ppermute | solution.py:455
  16.1 18.3 %collective-permute-start.3 = (bf16[3,4,48,128]{3,2,1,0:T(8,128)(2,1)S(1)}, bf16[3,4,48,128]{3,2,1,0:T(8,128)(2,1)S(1)}, u32[]{:S(2)}, u32[]{:S(2)}) collective-permute-start(bf16[3,4,48,128]{3,2,1,0:T(8,128)(2,1)S(1)} %get-tuple-element.72), channel_id=1, source_target_pairs={{8,4},{24,20},{4,8},{20,24},{9,5},{25,21},{5,9},{21,25},{10,6},{26... | collective-permute-start | bytes 442376 | tf_op jit(solution)/shard_map/ppermute | solution.py:455
  19.6 14.8 %collective-permute-start.4 = (bf16[3,4,48,128]{3,2,1,0:T(8,128)(2,1)S(1)}, bf16[3,4,48,128]{3,2,1,0:T(8,128)(2,1)S(1)}, u32[]{:S(2)}, u32[]{:S(2)}) collective-permute-start(bf16[3,4,48,128]{3,2,1,0:T(8,128)(2,1)S(1)} %get-tuple-element.73), channel_id=1, source_target_pairs={{4,0},{12,8},{20,16},{28,24},{0,4},{8,12},{16,20},{24,28},{5,1},{1... | collective-permute-start | bytes 442376 | tf_op jit(solution)/shard_map/ppermute | solution.py:455
  19.7 14.8 %collective-permute-start.7 = (bf16[3,4,48,128]{3,2,1,0:T(8,128)(2,1)S(1)}, bf16[3,4,48,128]{3,2,1,0:T(8,128)(2,1)S(1)}, u32[]{:S(2)}, u32[]{:S(2)}) collective-permute-start(bf16[3,4,48,128]{3,2,1,0:T(8,128)(2,1)S(1)} %get-tuple-element.76), channel_id=1, source_target_pairs={{4,16},{8,20},{12,24},{16,4},{20,8},{24,12},{5,17},{9,21},{13,25},... | collective-permute-start | bytes 442376 | tf_op jit(solution)/shard_map/ppermute | solution.py:455
  25.7 8.8 %collective-permute-start.5 = (bf16[1,4,48,128]{3,2,1,0:T(8,128)(2,1)S(1)}, bf16[1,4,48,128]{3,2,1,0:T(8,128)(2,1)S(1)}, u32[]{:S(2)}, u32[]{:S(2)}) collective-permute-start(bf16[1,4,48,128]{3,2,1,0:T(8,128)(2,1)S(1)} %get-tuple-element.74), channel_id=1, source_target_pairs={{0,20},{4,24},{8,28},{20,0},{24,4},{28,8},{1,21},{5,25},{9,29},{21... | collective-permute-start | bytes 147464 | tf_op jit(solution)/shard_map/ppermute | solution.py:455
  28.7 5.7 %collective-permute-start.6 = (bf16[1,4,48,128]{3,2,1,0:T(8,128)(2,1)S(1)}, bf16[1,4,48,128]{3,2,1,0:T(8,128)(2,1)S(1)}, u32[]{:S(2)}, u32[]{:S(2)}) collective-permute-start(bf16[1,4,48,128]{3,2,1,0:T(8,128)(2,1)S(1)} %get-tuple-element.75), channel_id=1, source_target_pairs={{0,16},{4,20},{8,24},{12,28},{16,0},{20,4},{24,8},{28,12},{1,17},{... | collective-permute-start | bytes 147464 | tf_op jit(solution)/shard_map/ppermute | solution.py:455
  35.3 7.3 %collective-permute-start.10 = (bf16[48,2048]{1,0:T(8,128)(2,1)S(1)}, bf16[48,2048]{1,0:T(8,128)(2,1)S(1)}, u32[]{:S(2)}, u32[]{:S(2)}) collective-permute-start(bf16[48,2048]{1,0:T(8,128)(2,1)S(1)} %settle.2.refs_0_), channel_id=1, source_target_pairs={{0,2},{1,3},{2,0},{3,1},{4,6},{5,7},{6,4},{7,5},{8,10},{9,11},{10,... | collective-permute-start | bytes 589832 | tf_op jit(solution)/shard_map/ppermute | solution.py:439
  42.6 6.3 %collective-permute-start.13 = (bf16[992,128]{1,0:T(8,128)(2,1)S(1)}, bf16[992,128]{1,0:T(8,128)(2,1)S(1)}, u32[]{:S(2)}, u32[]{:S(2)}) collective-permute-start(bf16[992,128]{1,0:T(8,128)(2,1)S(1)} %get-tuple-element.86), channel_id=1, source_target_pairs={{0,4},{1,9},{2,6},{3,11},{4,0},{5,13},{6,2},{7,15},{8,12},{9,1},{1... | collective-permute-start | bytes 761864 | tf_op jit(solution)/shard_map/ppermute | solution.py:342
  49.0 9.9 %collective-permute-start.14 = (bf16[2,496,128]{2,1,0:T(8,128)(2,1)S(1)}, bf16[2,496,128]{2,1,0:T(8,128)(2,1)S(1)}, u32[]{:S(2)}, u32[]{:S(2)}) collective-permute-start(bf16[2,496,128]{2,1,0:T(8,128)(2,1)S(1)} %get-tuple-element.101), channel_id=1, source_target_pairs={{0,8},{1,5},{2,10},{3,7},{4,12},{5,1},{6,14},{7,3},{8,0},{9,13},{1... | collective-permute-start | bytes 761864 | tf_op jit(solution)/shard_map/ppermute | solution.py:342
  49.1 7.1 %collective-permute-start.15 = (bf16[496,128]{1,0:T(8,128)(2,1)S(1)}, bf16[496,128]{1,0:T(8,128)(2,1)S(1)}, u32[]{:S(2)}, u32[]{:S(2)}) collective-permute-start(bf16[496,128]{1,0:T(8,128)(2,1)S(1)} %get-tuple-element.103), channel_id=1, source_target_pairs={{0,4},{1,9},{2,6},{3,11},{4,0},{5,13},{6,2},{7,15},{8,12},{9,1},{1... | collective-permute-start | bytes 380936 | tf_op jit(solution)/shard_map/ppermute | solution.py:342
  50.7 8.2 %collective-permute-start.16 = (bf16[496,128]{1,0:T(8,128)(2,1)S(1)}, bf16[496,128]{1,0:T(8,128)(2,1)S(1)}, u32[]{:S(2)}, u32[]{:S(2)}) collective-permute-start(bf16[496,128]{1,0:T(8,128)(2,1)S(1)} %get-tuple-element.104), channel_id=1, source_target_pairs={{0,12},{1,13},{2,14},{3,15},{4,8},{5,9},{6,10},{7,11},{8,4},{9,5},... | collective-permute-start | bytes 380936 | tf_op jit(solution)/shard_map/ppermute | solution.py:342
  59.0 10.3 %collective-permute-start.17 = (bf16[2,248,128]{2,1,0:T(8,128)(2,1)S(1)}, bf16[2,248,128]{2,1,0:T(8,128)(2,1)S(1)}, u32[]{:S(2)}, u32[]{:S(2)}) collective-permute-start(bf16[2,248,128]{2,1,0:T(8,128)(2,1)S(1)} %get-tuple-element.108), channel_id=1, source_target_pairs={{0,16},{1,17},{2,18},{3,19},{4,20},{5,21},{6,22},{7,23},{8,24},{9,... | collective-permute-start | bytes 380936 | tf_op jit(solution)/shard_map/ppermute | solution.py:342
  61.1 6.9 %collective-permute-start.18 = (bf16[1,4,48,128]{3,2,1,0:T(8,128)(2,1)S(1)}, bf16[1,4,48,128]{3,2,1,0:T(8,128)(2,1)S(1)}, u32[]{:S(2)}, u32[]{:S(2)}) collective-permute-start(bf16[1,4,48,128]{3,2,1,0:T(8,128)(2,1)S(1)} %get-tuple-element.109), channel_id=1, source_target_pairs={{8,4},{24,20},{4,8},{20,24},{9,5},{25,21},{5,9},{21,25},{10,6},{26... | collective-permute-start | bytes 147464 | tf_op jit(solution)/shard_map/ppermute | solution.py:455
  69.3 7.3 %collective-permute-start.20 = (bf16[1,2,248,128]{3,2,1,0:T(8,128)(2,1)S(1)}, bf16[1,2,248,128]{3,2,1,0:T(8,128)(2,1)S(1)}, u32[]{:S(2)}, u32[]{:S(2)}) collective-permute-start(bf16[1,2,248,128]{3,2,1,0:T(8,128)(2,1)S(1)} %fusion), channel_id=1, source_target_pairs={{0,16},{1,17},{2,18},{3,19},{4,20},{5,21},{6,22},{7,23},{8,24},{9,... | collective-permute-start | bytes 380936 | tf_op jit(solution)/shard_map/ppermute | solution.py:342
  69.6 7.0 %collective-permute-start.21 = (bf16[1,4,48,128]{3,2,1,0:T(8,128)(2,1)S(1)}, bf16[1,4,48,128]{3,2,1,0:T(8,128)(2,1)S(1)}, u32[]{:S(2)}, u32[]{:S(2)}) collective-permute-start(bf16[1,4,48,128]{3,2,1,0:T(8,128)(2,1)S(1)} %get-tuple-element.117), channel_id=1, source_target_pairs={{0,16},{4,20},{8,24},{12,28},{16,0},{20,4},{24,8},{28,12},{1,17},{... | collective-permute-start | bytes 147464 | tf_op jit(solution)/shard_map/ppermute | solution.py:455
  76.7 16.5 %collective-permute-start.26 = (bf16[2,2,248,128]{3,2,1,0:T(8,128)(2,1)S(1)}, bf16[2,2,248,128]{3,2,1,0:T(8,128)(2,1)S(1)}, u32[]{:S(2)}, u32[]{:S(2)}) collective-permute-start(bf16[2,2,248,128]{3,2,1,0:T(8,128)(2,1)S(1)} %pad_maximum_fusion.refs_0_), channel_id=1, source_target_pairs={{0,12},{1,13},{2,14},{3,15},{4,8},{5,9},{6,10},{7,11},{8,4},{9,5},... | collective-permute-start | bytes 761864 | tf_op jit(solution)/shard_map/ppermute | solution.py:342
  77.3 15.9 %collective-permute-start.25 = (bf16[2,2,248,128]{3,2,1,0:T(8,128)(2,1)S(1)}, bf16[2,2,248,128]{3,2,1,0:T(8,128)(2,1)S(1)}, u32[]{:S(2)}, u32[]{:S(2)}) collective-permute-start(bf16[2,2,248,128]{3,2,1,0:T(8,128)(2,1)S(1)} %pad_maximum_fusion.refs_0_), channel_id=1, source_target_pairs={{0,4},{1,9},{2,6},{3,11},{4,0},{5,13},{6,2},{7,15},{8,12},{9,1},{1... | collective-permute-start | bytes 761864 | tf_op jit(solution)/shard_map/ppermute | solution.py:342
  77.9 15.2 %collective-permute-start.24 = (bf16[2,2,248,128]{3,2,1,0:T(8,128)(2,1)S(1)}, bf16[2,2,248,128]{3,2,1,0:T(8,128)(2,1)S(1)}, u32[]{:S(2)}, u32[]{:S(2)}) collective-permute-start(bf16[2,2,248,128]{3,2,1,0:T(8,128)(2,1)S(1)} %pad_maximum_fusion.refs_0_), channel_id=1, source_target_pairs={{0,8},{1,5},{2,10},{3,7},{4,12},{5,1},{6,14},{7,3},{8,0},{9,13},{1... | collective-permute-start | bytes 761864 | tf_op jit(solution)/shard_map/ppermute | solution.py:342
  80.2 9.0 %collective-permute-start.22 = (bf16[1,4,48,128]{3,2,1,0:T(8,128)(2,1)S(1)}, bf16[1,4,48,128]{3,2,1,0:T(8,128)(2,1)S(1)}, u32[]{:S(2)}, u32[]{:S(2)}) collective-permute-start(bf16[1,4,48,128]{3,2,1,0:T(8,128)(2,1)S(1)} %get-tuple-element.121), channel_id=1, source_target_pairs={{0,20},{4,24},{8,28},{20,0},{24,4},{28,8},{1,21},{5,25},{9,29},{21... | collective-permute-start | bytes 147464 | tf_op jit(solution)/shard_map/ppermute | solution.py:455
  83.9 7.8 %collective-permute-start.23 = (bf16[1,4,48,128]{3,2,1,0:T(8,128)(2,1)S(1)}, bf16[1,4,48,128]{3,2,1,0:T(8,128)(2,1)S(1)}, u32[]{:S(2)}, u32[]{:S(2)}) collective-permute-start(bf16[1,4,48,128]{3,2,1,0:T(8,128)(2,1)S(1)} %get-tuple-element.123), channel_id=1, source_target_pairs={{4,16},{8,20},{12,24},{16,4},{20,8},{24,12},{5,17},{9,21},{13,25},... | collective-permute-start | bytes 147464 | tf_op jit(solution)/shard_map/ppermute | solution.py:455
  (4 other events, 19.0 us)
